TPU v7x, 32 devices: a whole 2x2x4 slice. The times are simulated.
32 devices in a mesh: section: 2 (over x), expert: 4 (over z), replica: 4 (over y, core).
Axes of the slice: x: 2, y: 2, z: 4, core: 2. Of those that a mesh axis runs over, the one named last changes fastest.
Arguments:
- inputs: bfloat16 [2, 4, 1024, 1024], P(None, 'expert', 'replica'), may hold values from -8 to 8
- cotangent: bfloat16 [2, 4, 1024, 1024], P(None, 'expert', 'replica'), may hold values from -6 to 6
- routes: int32 [2, 2, 4, 1024, 2], P('section', None, 'expert', 'replica'), may hold values from 0 to 3, all different within a row; in each aligned block of 256 rows (0 to 255, 256 to 511, ..., all dimensions but the last counted through in order) at most 144 rows name the same one
- bucket_table: int32 [2047], replicated, may hold values from 0 to 31
- query_weight: bfloat16 [2, 1024, 1024], P('section', 'expert'), may hold values from -0.1875 to 0.1875
- key_weight: bfloat16 [2, 1024, 1024], P('section', 'expert'), may hold values from -0.1875 to 0.1875
- value_weight: bfloat16 [2, 1024, 1024], P('section', 'expert'), may hold values from -0.1875 to 0.1875
- output_weight: bfloat16 [2, 1024, 1024], P('section', 'expert'), may hold values from -2 to 2
- router_weight: bfloat16 [2, 1024, 4], P('section', 'expert'), may hold values from -0.1875 to 0.1875
- attention_gain: bfloat16 [2, 1024], P('section', 'expert'), may hold values from 0.25 to 1.75
- mixture_gain: bfloat16 [2, 1024], P('section', 'expert'), may hold values from 0.25 to 1.75
- position_bias: bfloat16 [2, 16, 32], P('section', 'expert'), may hold values from -4 to 4
- expert_gate: bfloat16 [2, 4, 1024, 2816], P('section', 'expert', 'replica'), may hold values from -0.1875 to 0.1875
- expert_up: bfloat16 [2, 4, 1024, 2816], P('section', 'expert', 'replica'), may hold values from -0.1875 to 0.1875
- expert_down: bfloat16 [2, 4, 2816, 1024], P('section', 'expert', None, 'replica'), may hold values from -0.4375 to 0.4375
Outputs:
- section_output: bfloat16 [2, 2, 4, 1024, 1024], P('section', None, 'expert', 'replica')
- input_gradient: float32 [2, 2, 4, 1024, 1024], P('section', None, 'expert', 'replica')
- gradient_query: float32 [2, 1024, 1024], P('section', 'expert')
- gradient_key: float32 [2, 1024, 1024], P('section', 'expert')
- gradient_value: float32 [2, 1024, 1024], P('section', 'expert')
- gradient_output: float32 [2, 1024, 1024], P('section', 'expert')
- gradient_router: float32 [2, 1024, 4], P('section', 'expert')
- gradient_attention_gain: float32 [2, 1024], P('section', 'expert')
- gradient_mixture_gain: float32 [2, 1024], P('section', 'expert')
- gradient_position: float32 [2, 16, 32], P('section', 'expert')
- gradient_expert_gate: float32 [2, 4, 1024, 2816], P('section', 'expert', 'replica')
- gradient_expert_up: float32 [2, 4, 1024, 2816], P('section', 'expert', 'replica')
- gradient_expert_down: float32 [2, 4, 2816, 1024], P('section', 'expert', None, 'replica')
Inputs may be any that keep to these rules, and one draw needn't show every extreme that they name: `routes`: each token names two different experts. Among the 256 tokens of one block (one device's rows of one micro-batch) no expert is named more than 144 times, a bound that some block reaches.
All inputs are finite; a program needn't handle non-finite values.
Results may differ from a plain program's by a relative error of at most 0.023.
Values may be sent and summed in bfloat16 or wider, within the bound.
No kernel may reach another device: no remote copies, remote signals or barrier semaphores. Data moves between devices by JAX's collectives and lax.ppermute only.
A program may use at most 512 MiB of HBM per device.

v0:
```python
import math

import jax
import jax.numpy as jnp
from jax import lax
from jax.sharding import PartitionSpec as P

HEADS = 16
HEAD_DIM = 64


EPSILON = 1e-06


def from_behind(value, axis, steps):
    count = lax.axis_size(axis)
    first, last = (max(0, -steps), min(count, count - steps))
    return lax.ppermute(value, axis, [(source, source + steps) for source in range(first, last)])


def matmul(left, right):
    return jnp.dot(left, right, preferred_element_type=jnp.float32)


def rms_scale(values, gain):
    return values * lax.rsqrt(jnp.mean(values * values, axis=-1, keepdims=True) + EPSILON) * gain


def softmax_rows(scores):
    row_top = jnp.max(scores, axis=-1, keepdims=True)
    expos = jnp.exp(scores - row_top)
    return expos / jnp.sum(expos, axis=-1, keepdims=True)


def gated_gelu(gate_part, up_part):
    return jax.nn.gelu(gate_part, approximate=True) * up_part


def shards(
    inputs,
    cotangent,
    routes,
    bucket_table,
    query_weight,
    key_weight,
    value_weight,
    output_weight,
    router_weight,
    attention_gain,
    mixture_gain,
    position_bias,
    expert_gate,
    expert_up,
    expert_down,
):
    micro_count = inputs.shape[0]
    tok_rows = inputs.shape[2]
    model_width = inputs.shape[3]
    expert_count = lax.axis_size("expert")
    length = tok_rows * lax.axis_size("replica")
    capacity = max(2, 9 * tok_rows // (4 * expert_count))
    slot_count = expert_count * capacity
    root_size = math.sqrt(HEAD_DIM)
    section_index = lax.axis_index("section")
    replica_index = lax.axis_index("replica")
    expert_range = jnp.arange(expert_count, dtype=jnp.int32)
    slot_range = jnp.arange(slot_count, dtype=jnp.int32)
    dense_args = (
        query_weight,
        key_weight,
        value_weight,
        output_weight,
        router_weight,
        attention_gain,
        mixture_gain,
        position_bias,
    )
    query_places = replica_index * tok_rows + jnp.arange(tok_rows, dtype=jnp.int32)
    offsets = jnp.arange(length, dtype=jnp.int32)[None, :] - query_places[:, None] + length - 1

    def attention_scores(queries, keys_all, bias):
        raw = jnp.einsum(
            "qhd,khd->hqk",
            queries.reshape(tok_rows, HEADS, HEAD_DIM),
            keys_all.reshape(length, HEADS, HEAD_DIM),
            preferred_element_type=jnp.float32,
        )
        return raw / root_size + bias

    def forward(section_in, route, dense, experts, bias):
        (
            weight_query,
            weight_key,
            weight_value,
            weight_output,
            weight_router,
            gain_first,
            gain_second,
            position,
        ) = dense
        normed = rms_scale(section_in, gain_first.astype(jnp.float32)).astype(jnp.bfloat16)
        queries = matmul(normed, weight_query).astype(jnp.bfloat16)
        keys_local = matmul(normed, weight_key).astype(jnp.bfloat16)
        values_local = matmul(normed, weight_value).astype(jnp.bfloat16)
        keys_all, values_all = (
            lax.all_gather(keys_local, "replica", axis=0, tiled=True),
            lax.all_gather(values_local, "replica", axis=0, tiled=True),
        )
        scores = attention_scores(queries, keys_all, bias)
        row_top = jnp.max(scores, axis=-1, keepdims=True)
        log_total = row_top + jnp.log(jnp.sum(jnp.exp(scores - row_top), axis=-1, keepdims=True))
        attention = jnp.exp(scores - log_total)
        attended = jnp.einsum(
            "hqk,khd->qhd",
            attention.astype(jnp.bfloat16),
            values_all.reshape(length, HEADS, HEAD_DIM),
            preferred_element_type=jnp.float32,
        )
        attended = attended.reshape(tok_rows, model_width).astype(jnp.bfloat16)
        middle = section_in + matmul(attended, weight_output)
        mixed_in = rms_scale(middle, gain_second.astype(jnp.float32)).astype(jnp.bfloat16)
        gates_all = softmax_rows(matmul(mixed_in, weight_router))
        onehot = (route[:, :, None] == expert_range[None, None, :]).astype(jnp.int32)
        per_row = jnp.sum(onehot, axis=1)
        before = jnp.cumsum(per_row, axis=0) - per_row
        slot_place = jnp.sum(before[:, None, :] * onehot, axis=2)
        target = route * capacity + slot_place
        slot_table = jnp.sum(
            (target[:, :, None] == slot_range[None, None, :]).astype(jnp.bfloat16), axis=1
        )
        packed = jnp.einsum(
            "ts,td->sd", slot_table, mixed_in, preferred_element_type=jnp.float32
        ).astype(jnp.bfloat16)
        arrived = lax.all_to_all(
            packed.reshape(expert_count, capacity, model_width),
            "expert",
            split_axis=0,
            concat_axis=0,
            tiled=True,
        ).reshape(slot_count, model_width)
        gate_part = matmul(arrived, experts[0])
        up_part = matmul(arrived, experts[1])
        produced = matmul(gated_gelu(gate_part, up_part).astype(jnp.bfloat16), experts[2]).astype(
            jnp.bfloat16
        )
        returned = lax.all_to_all(
            produced.reshape(expert_count, capacity, model_width),
            "expert",
            split_axis=0,
            concat_axis=0,
            tiled=True,
        ).reshape(slot_count, model_width)
        picked = jnp.take_along_axis(gates_all, route, axis=1)
        mixed_out = jnp.sum(picked[:, :, None] * returned[target].astype(jnp.float32), axis=1)
        stored = (
            section_in,
            normed,
            queries,
            keys_all,
            values_all,
            log_total,
            attended,
            middle,
            mixed_in,
            gates_all,
            arrived,
            gate_part,
            up_part,
            returned,
            target,
            slot_table,
        )
        return (middle + mixed_out, stored)

    def backward(grad_out, stored, route, dense, experts, bias):
        (
            weight_query,
            weight_key,
            weight_value,
            weight_output,
            weight_router,
            gain_first,
            gain_second,
            position,
        ) = dense
        (
            section_in,
            normed,
            queries,
            keys_all,
            values_all,
            log_total,
            attended,
            middle,
            mixed_in,
            gates_all,
            arrived,
            gate_part,
            up_part,
            returned,
            target,
            slot_table,
        ) = stored
        picked = jnp.take_along_axis(gates_all, route, axis=1)
        chosen = returned[target].astype(jnp.float32)
        grad_picked = jnp.sum(chosen * grad_out[:, None, :], axis=2)
        spread = (picked[:, :, None] * grad_out[:, None, :]).reshape(-1, model_width)
        grad_slots = (
            jnp.zeros((slot_count, model_width), jnp.float32)
            .at[target.reshape(-1)]
            .add(spread)
            .astype(jnp.bfloat16)
        )
        received = lax.all_to_all(
            grad_slots.reshape(expert_count, capacity, model_width),
            "expert",
            split_axis=0,
            concat_axis=0,
            tiled=True,
        ).reshape(slot_count, model_width)
        hidden = gated_gelu(gate_part, up_part).astype(jnp.bfloat16)
        term_down = jnp.einsum("rf,rd->fd", hidden, received, preferred_element_type=jnp.float32)
        grad_hidden = jnp.einsum(
            "rd,fd->rf", received, experts[2], preferred_element_type=jnp.float32
        )
        unused_value, pull_gelu = jax.vjp(gated_gelu, gate_part, up_part)
        grad_gate, grad_up = pull_gelu(grad_hidden)
        grad_gate = grad_gate.astype(jnp.bfloat16)
        grad_up = grad_up.astype(jnp.bfloat16)
        term_gate = jnp.einsum("rd,rf->df", arrived, grad_gate, preferred_element_type=jnp.float32)
        term_up = jnp.einsum("rd,rf->df", arrived, grad_up, preferred_element_type=jnp.float32)
        grad_arrived = jnp.einsum(
            "rf,df->rd", grad_gate, experts[0], preferred_element_type=jnp.float32
        )
        grad_arrived = (
            grad_arrived
            + jnp.einsum("rf,df->rd", grad_up, experts[1], preferred_element_type=jnp.float32)
        ).astype(jnp.bfloat16)
        back_rows = lax.all_to_all(
            grad_arrived.reshape(expert_count, capacity, model_width),
            "expert",
            split_axis=0,
            concat_axis=0,
            tiled=True,
        ).reshape(slot_count, model_width)
        grad_mixed = jnp.einsum(
            "ts,sd->td", slot_table, back_rows, preferred_element_type=jnp.float32
        )
        onehot = (route[:, :, None] == expert_range[None, None, :]).astype(jnp.float32)
        grad_gates = jnp.sum(onehot * grad_picked[:, :, None], axis=1)
        unused_soft, pull_soft = jax.vjp(softmax_rows, matmul(mixed_in, weight_router))
        grad_logits = pull_soft(grad_gates)[0].astype(jnp.bfloat16)
        term_router = jnp.einsum(
            "td,te->de", mixed_in, grad_logits, preferred_element_type=jnp.float32
        )
        grad_mixed = grad_mixed + jnp.einsum(
            "te,de->td", grad_logits, weight_router, preferred_element_type=jnp.float32
        )
        unused_second, pull_second = jax.vjp(rms_scale, middle, gain_second.astype(jnp.float32))
        grad_middle, term_second = pull_second(grad_mixed)
        grad_middle = grad_middle + grad_out
        grad_branch = grad_middle.astype(jnp.bfloat16)
        term_output = jnp.einsum(
            "td,te->de", attended, grad_branch, preferred_element_type=jnp.float32
        )
        grad_attended = jnp.einsum(
            "te,de->td", grad_branch, weight_output, preferred_element_type=jnp.float32
        ).astype(jnp.bfloat16)
        attention = jnp.exp(attention_scores(queries, keys_all, bias) - log_total)
        grad_heads = grad_attended.reshape(tok_rows, HEADS, HEAD_DIM)
        grad_attention = jnp.einsum(
            "qhd,khd->hqk",
            grad_heads,
            values_all.reshape(length, HEADS, HEAD_DIM),
            preferred_element_type=jnp.float32,
        )
        row_dot = jnp.sum(attention * grad_attention, axis=-1, keepdims=True)
        grad_scores = (attention * (grad_attention - row_dot)).astype(jnp.bfloat16)
        grad_queries = (
            jnp.einsum(
                "hqk,khd->qhd",
                grad_scores,
                keys_all.reshape(length, HEADS, HEAD_DIM),
                preferred_element_type=jnp.float32,
            )
            / root_size
        )
        grad_queries = grad_queries.reshape(tok_rows, model_width).astype(jnp.bfloat16)
        part_keys = (
            jnp.einsum(
                "hqk,qhd->khd",
                grad_scores,
                queries.reshape(tok_rows, HEADS, HEAD_DIM),
                preferred_element_type=jnp.float32,
            )
            / root_size
        )
        part_values = jnp.einsum(
            "hqk,qhd->khd",
            attention.astype(jnp.bfloat16),
            grad_heads,
            preferred_element_type=jnp.float32,
        )
        grad_keys, grad_values = (
            lax.psum_scatter(
                part_keys.reshape(length, model_width).astype(jnp.bfloat16),
                "replica",
                scatter_dimension=0,
                tiled=True,
            ).astype(jnp.float32),
            lax.psum_scatter(
                part_values.reshape(length, model_width).astype(jnp.bfloat16),
                "replica",
                scatter_dimension=0,
                tiled=True,
            ).astype(jnp.float32),
        )
        grad_keys = grad_keys.astype(jnp.bfloat16)
        grad_values = grad_values.astype(jnp.bfloat16)
        term_query = jnp.einsum(
            "td,te->de", normed, grad_queries, preferred_element_type=jnp.float32
        )
        term_key = jnp.einsum("td,te->de", normed, grad_keys, preferred_element_type=jnp.float32)
        term_value = jnp.einsum(
            "td,te->de", normed, grad_values, preferred_element_type=jnp.float32
        )
        grad_normed = jnp.einsum(
            "te,de->td", grad_queries, weight_query, preferred_element_type=jnp.float32
        )
        grad_normed = grad_normed + jnp.einsum(
            "te,de->td", grad_keys, weight_key, preferred_element_type=jnp.float32
        )
        grad_normed = grad_normed + jnp.einsum(
            "te,de->td", grad_values, weight_value, preferred_element_type=jnp.float32
        )
        unused_first, pull_first = jax.vjp(rms_scale, section_in, gain_first.astype(jnp.float32))
        grad_in, term_first = pull_first(grad_normed)
        grad_in = grad_in + grad_middle
        terms = (
            term_query,
            term_key,
            term_value,
            term_output,
            term_router,
            term_first,
            term_second,
            grad_scores.astype(jnp.float32),
            term_gate,
            term_up,
            term_down,
        )
        return (grad_in, terms)

    gathered_dense = (
        lax.all_gather(dense_args[0], "expert", axis=1, tiled=True),
        lax.all_gather(dense_args[1], "expert", axis=1, tiled=True),
        lax.all_gather(dense_args[2], "expert", axis=1, tiled=True),
        lax.all_gather(dense_args[3], "expert", axis=1, tiled=True),
        lax.all_gather(dense_args[4], "expert", axis=1, tiled=True),
        lax.all_gather(dense_args[5], "expert", axis=1, tiled=True),
        lax.all_gather(dense_args[6], "expert", axis=1, tiled=True),
        lax.all_gather(dense_args[7], "expert", axis=1, tiled=True),
    )
    dense_now = tuple((member[0] for member in gathered_dense))
    gathered_experts = (
        lax.all_gather(expert_gate, "replica", axis=2, tiled=True),
        lax.all_gather(expert_up, "replica", axis=2, tiled=True),
        lax.all_gather(expert_down, "replica", axis=3, tiled=True),
    )
    experts_now = tuple((member[0, 0] for member in gathered_experts))
    by_offset = jnp.take(dense_now[7].astype(jnp.float32), bucket_table, axis=1)
    bias_now = jnp.take(by_offset, offsets, axis=1)
    own_inputs = inputs[:, 0]
    own_routes = routes[0, :, 0]
    own_cotangent = cotangent[:, 0]

    def forward_tick(incoming, tick_index):
        micro_index = tick_index - section_index
        chosen_index = jnp.clip(micro_index, 0, micro_count - 1)
        first_rows = lax.dynamic_index_in_dim(
            own_inputs, jnp.clip(tick_index, 0, micro_count - 1), 0, keepdims=False
        ).astype(jnp.float32)
        section_in = jnp.where(section_index == 0, first_rows, incoming.astype(jnp.float32))
        route = lax.dynamic_index_in_dim(own_routes, chosen_index, 0, keepdims=False)
        result, stored = forward(section_in, route, dense_now, experts_now, bias_now)
        outgoing = result.astype(jnp.bfloat16)
        following = from_behind(outgoing, "section", 1)
        return (following, (outgoing, stored))

    ticks = jnp.arange(micro_count + 1, dtype=jnp.int32)
    start_rows = jnp.zeros((tok_rows, model_width), jnp.bfloat16)
    unused_rows, (outgoing_all, stored_all) = lax.scan(forward_tick, start_rows, ticks)

    def backward_tick(carried, tick_index):
        incoming, totals = carried
        micro_index = micro_count - tick_index - section_index
        active = ((micro_index >= 0) & (micro_index < micro_count)).astype(jnp.float32)
        chosen_index = jnp.clip(micro_index, 0, micro_count - 1)
        stored = jax.tree.map(
            lambda stacked: lax.dynamic_index_in_dim(
                stacked, chosen_index + section_index, 0, keepdims=False
            ),
            stored_all,
        )
        last_rows = lax.dynamic_index_in_dim(own_cotangent, chosen_index, 0, keepdims=False).astype(
            jnp.float32
        )
        grad_out = jnp.where(section_index == 1, last_rows, incoming.astype(jnp.float32))
        route = lax.dynamic_index_in_dim(own_routes, chosen_index, 0, keepdims=False)
        grad_in, terms = backward(grad_out, stored, route, dense_now, experts_now, bias_now)
        totals = jax.tree.map(lambda running, addition: running + active * addition, totals, terms)
        previous = from_behind(grad_in.astype(jnp.bfloat16), "section", -1)
        return ((previous, totals), grad_in)

    zero_totals = (
        jnp.zeros((model_width, model_width), jnp.float32),
        jnp.zeros((model_width, model_width), jnp.float32),
        jnp.zeros((model_width, model_width), jnp.float32),
        jnp.zeros((model_width, model_width), jnp.float32),
        jnp.zeros((model_width, expert_count), jnp.float32),
        jnp.zeros((model_width,), jnp.float32),
        jnp.zeros((model_width,), jnp.float32),
        jnp.zeros((HEADS, tok_rows, length), jnp.float32),
        jnp.zeros(experts_now[0].shape, jnp.float32),
        jnp.zeros(experts_now[1].shape, jnp.float32),
        jnp.zeros(experts_now[2].shape, jnp.float32),
    )
    (unused_back, totals), grad_all = lax.scan(
        backward_tick, (jnp.zeros((tok_rows, model_width), jnp.bfloat16), zero_totals), ticks
    )
    (
        sum_query,
        sum_key,
        sum_value,
        sum_output,
        sum_router,
        sum_first,
        sum_second,
        sum_scores,
        sum_gate,
        sum_up,
        sum_down,
    ) = totals
    by_offset = jax.ops.segment_sum(
        sum_scores.reshape(HEADS, -1).T, offsets.reshape(-1), num_segments=2 * length - 1
    )
    sum_position = jax.ops.segment_sum(
        by_offset, bucket_table, num_segments=position_bias.shape[2]
    ).T
    (
        share_query,
        share_key,
        share_value,
        share_output,
        share_router,
        share_first,
        share_second,
        share_position,
    ) = (
        lax.psum_scatter(
            sum_query.astype(jnp.bfloat16), "expert", scatter_dimension=0, tiled=True
        ).astype(jnp.float32),
        lax.psum_scatter(
            sum_key.astype(jnp.bfloat16), "expert", scatter_dimension=0, tiled=True
        ).astype(jnp.float32),
        lax.psum_scatter(
            sum_value.astype(jnp.bfloat16), "expert", scatter_dimension=0, tiled=True
        ).astype(jnp.float32),
        lax.psum_scatter(
            sum_output.astype(jnp.bfloat16), "expert", scatter_dimension=0, tiled=True
        ).astype(jnp.float32),
        lax.psum_scatter(
            sum_router.astype(jnp.bfloat16), "expert", scatter_dimension=0, tiled=True
        ).astype(jnp.float32),
        lax.psum_scatter(
            sum_first.astype(jnp.bfloat16), "expert", scatter_dimension=0, tiled=True
        ).astype(jnp.float32),
        lax.psum_scatter(
            sum_second.astype(jnp.bfloat16), "expert", scatter_dimension=0, tiled=True
        ).astype(jnp.float32),
        lax.psum_scatter(
            sum_position.astype(jnp.bfloat16), "expert", scatter_dimension=0, tiled=True
        ).astype(jnp.float32),
    )
    (
        final_query,
        final_key,
        final_value,
        final_output,
        final_router,
        final_first,
        final_second,
        final_position,
    ) = (
        lax.psum(share_query.astype(jnp.bfloat16), "replica").astype(jnp.float32),
        lax.psum(share_key.astype(jnp.bfloat16), "replica").astype(jnp.float32),
        lax.psum(share_value.astype(jnp.bfloat16), "replica").astype(jnp.float32),
        lax.psum(share_output.astype(jnp.bfloat16), "replica").astype(jnp.float32),
        lax.psum(share_router.astype(jnp.bfloat16), "replica").astype(jnp.float32),
        lax.psum(share_first.astype(jnp.bfloat16), "replica").astype(jnp.float32),
        lax.psum(share_second.astype(jnp.bfloat16), "replica").astype(jnp.float32),
        lax.psum(share_position.astype(jnp.bfloat16), "replica").astype(jnp.float32),
    )
    final_gate, final_up, final_down = (
        lax.psum_scatter(
            sum_gate.astype(jnp.bfloat16), "replica", scatter_dimension=0, tiled=True
        ).astype(jnp.float32),
        lax.psum_scatter(
            sum_up.astype(jnp.bfloat16), "replica", scatter_dimension=0, tiled=True
        ).astype(jnp.float32),
        lax.psum_scatter(
            sum_down.astype(jnp.bfloat16), "replica", scatter_dimension=1, tiled=True
        ).astype(jnp.float32),
    )
    section_output = jnp.take(
        outgoing_all, jnp.arange(micro_count, dtype=jnp.int32) + section_index, axis=0
    )
    section_output = section_output.reshape(1, micro_count, 1, tok_rows, model_width)
    input_gradient = jnp.take(
        grad_all, micro_count - section_index - jnp.arange(micro_count, dtype=jnp.int32), axis=0
    )
    input_gradient = input_gradient.reshape(1, micro_count, 1, tok_rows, model_width)
    return (
        section_output,
        input_gradient,
        final_query[None],
        final_key[None],
        final_value[None],
        final_output[None],
        final_router[None],
        final_first[None],
        final_second[None],
        final_position[None],
        final_gate[None, None],
        final_up[None, None],
        final_down[None, None],
    )


def solution(mesh):
    in_specs = (
        P(None, "expert", "replica", None),
        P(None, "expert", "replica", None),
        P("section", None, "expert", "replica", None),
        P(),
        P("section", "expert", None),
        P("section", "expert", None),
        P("section", "expert", None),
        P("section", "expert", None),
        P("section", "expert", None),
        P("section", "expert"),
        P("section", "expert"),
        P("section", "expert", None),
        P("section", "expert", "replica", None),
        P("section", "expert", "replica", None),
        P("section", "expert", None, "replica"),
    )
    out_specs = (
        P("section", None, "expert", "replica", None),
        P("section", None, "expert", "replica", None),
        P("section", "expert", None),
        P("section", "expert", None),
        P("section", "expert", None),
        P("section", "expert", None),
        P("section", "expert", None),
        P("section", "expert"),
        P("section", "expert"),
        P("section", "expert", None),
        P("section", "expert", "replica", None),
        P("section", "expert", "replica", None),
        P("section", "expert", None, "replica"),
    )
    return jax.shard_map(shards, mesh=mesh, in_specs=in_specs, out_specs=out_specs, check_vma=False)
```

profile of v0, /device:TPU:0, one launch (start us, length us, event | category | flops | bytes accessed | tf_op | source)
XLA Modules:
  0.0 4141.1 jit_solution(12064376894180830838)
XLA Ops:
  32.4 865.9 %gather_fusion.5 = f32[262144,16]{1,0:T(8,128)} fusion(f32[16,2047]{0,1:T(8,128)S(1)} %select_bitcast_fusion.1, s32[262144]{0:T(1024)S(1)} %broadcast_clamp_fusion), kind=kCustom, calls=%fused_computation.5 | custom fusion | bytes 34603008 | tf_op jit(solution)/shard_map/jit(_take)/gather | solution.py:372
  898.3 75.3 %copy.133 = f32[256,1024,16]{1,0,2:T(8,128)} copy(f32[256,1024,16]{2,1,0:T(8,128)} %bitcast.6) | data formatting | bytes 33554432 | tf_op jit(solution)/shard_map/jit(_take)/gather | solution.py:372
  1019.9 559.5 %while.84 = (s32[]{:T(128)}, bf16[256,1024]{1,0:T(8,128)(2,1)S(1)}, bf16[3,256,1024]{2,1,0:T(8,128)(2,1)}, f32[3,256,1024]{2,1,0:T(8,128)}, bf16[3,256,1024]{2,1...) while((s32[]{:T(128)}, bf16[256,1024]{1,0:T(8,128)(2,1)S(1)}, ...), condition=%wide.region_13.15_spmd.clone, body=%wide.region_0.14_spmd.clone.sunk | while | flops 13547025408 | bytes 268893408 | solution.py:392
  1116.1 24.4 all-to-all-done
  1297.2 24.3 all-to-all-done
  1478.0 24.4 all-to-all-done
  1581.6 825.2 %while.85 = (s32[]{:T(128)}, bf16[256,1024]{1,0:T(8,128)(2,1)S(1)}, f32[1024,1024]{1,0:T(8,128)}, f32[1024,1024]{1,0:T(8,128)}, f32[1024,1024]{1,0:T(8,128)}, /*...) while((s32[]{:T(128)}, bf16[256,1024]{1,0:T(8,128)(2,1)S(1)}, ...), condition=%wide.region_32.34_spmd.clone, body=%wide.region_14.33_spmd.clone.sunk | while | flops 27384700928 | bytes 660260352 | solution.py:428
  1618.8 18.0 all-to-all-done.2
  1713.5 19.3 multiply_reduce_fusion.15
  1732.8 17.7 select_add_fusion.20
  1878.7 18.4 all-to-all-done.2
  1973.7 19.3 multiply_reduce_fusion.15
  1993.1 22.8 select_add_fusion.20
  2061.8 19.5 select_add_fusion.29
  2157.2 18.4 all-to-all-done.2
  2252.2 19.3 multiply_reduce_fusion.15
  2271.5 22.8 select_add_fusion.20
  2340.3 19.3 select_add_fusion.29
  2423.7 26.9 reduce-scatter.14.cloned.1.call-done
  2450.6 46.2 %reduce-scatter.16.cloned.1.call-done = bf16[256,1024]{1,0:T(8,128)(2,1)} async-done(((bf16[1024,1024]{1,0:T(8,128)(2,1)}), bf16[256,1024]{1,0:T(8,128)(2,1)}) %reduce-scatter.16.cloned.1.call-update) | async-done | bytes 524304 | tf_op jit(solution)/shard_map/reduce_scatter | solution.py:463
  2496.8 46.1 %reduce-scatter.18.cloned.1.call-done = bf16[256,1024]{1,0:T(8,128)(2,1)} async-done(((bf16[1024,1024]{1,0:T(8,128)(2,1)}), bf16[256,1024]{1,0:T(8,128)(2,1)}) %reduce-scatter.18.cloned.1.call-update) | async-done | bytes 524304 | tf_op jit(solution)/shard_map/reduce_scatter | solution.py:466
  2542.9 46.2 %reduce-scatter.20.cloned.1.call-done = bf16[256,1024]{1,0:T(8,128)(2,1)} async-done(((bf16[1024,1024]{1,0:T(8,128)(2,1)}), bf16[256,1024]{1,0:T(8,128)(2,1)}) %reduce-scatter.20.cloned.1.call-update) | async-done | bytes 524304 | tf_op jit(solution)/shard_map/reduce_scatter | solution.py:469
  2615.6 65.2 %copy.143 = f32[16,256,1024]{0,2,1:T(8,128)} copy(f32[16,256,1024]{2,1,0:T(8,128)} %get-tuple-element.1072) | data formatting | bytes 33554432 | tf_op jit(solution)/shard_map/reshape | solution.py:445
  2680.9 1387.5 %scatter_custom_fusion.1 = f32[2047,16]{1,0:T(8,128)} fusion(s32[262144]{0:T(1024)} %bitcast.594, f32[262144,16]{1,0:T(8,128)} %bitcast.25, f32[]{:T(128)} %constant.390.clone.1), kind=kCustom, calls=%fused_computation.261 | custom fusion | flops 4194304 | bytes 131520 | tf_op jit(solution)/shard_map/scatter-add | solution.py:444
  (859 shorter events, 1244.0 us)
Async XLA Ops:
  7.2 1008.4 %all-gather.10.cloned.1.call-start = ((), (), s32[]{:S(2)}) async-start(), calls=%async_computation.14 | async-start | bytes 2621440 | tf_op jit(solution)/shard_map/all_gather | solution.py:357
  7.9 1007.7 %all-gather.12.cloned.1.call-start = ((), (), s32[]{:S(2)}) async-start(), calls=%async_computation.15 | async-start | bytes 2621440 | tf_op jit(solution)/shard_map/all_gather | solution.py:355
  8.7 1007.0 %all-gather.14.cloned.1.call-start = ((), (), s32[]{:S(2)}) async-start(), calls=%async_computation.16 | async-start | bytes 2621440 | tf_op jit(solution)/shard_map/all_gather | solution.py:356
  9.4 1006.2 %all-gather.16.cloned.1.call-start = ((), (), s32[]{:S(2)}) async-start(), calls=%async_computation.17 | async-start | bytes 2621440 | tf_op jit(solution)/shard_map/all_gather | solution.py:358
  10.0 1005.7 %all-gather.18.cloned.1.call-start = ((), (), s32[]{:S(2)}) async-start(), calls=%async_computation.18 | async-start | bytes 7208960 | tf_op jit(solution)/shard_map/all_gather | solution.py:366
  10.6 1005.1 %all-gather.20.cloned.1.call-start = ((), (), s32[]{:S(2)}) async-start(), calls=%async_computation.19 | async-start | bytes 7208960 | tf_op jit(solution)/shard_map/all_gather | solution.py:367
  11.2 1004.6 %all-gather.22.cloned.1.call-start = ((), (), s32[]{:S(2)}) async-start(), calls=%async_computation.20 | async-start | bytes 7208960 | tf_op jit(solution)/shard_map/all_gather | solution.py:368
  1043.2 47.0 %all-gather.24.cloned.1.call-start = ((), (), s32[]{:S(2)}) async-start(), calls=%async_computation.30 | async-start | bytes 2621440 | tf_op jit(solution)/shard_map/while/body/eval_jaxpr/all_gather | solution.py:107
  1225.3 45.9 %all-gather.24.cloned.1.call-start = ((), (), s32[]{:S(2)}) async-start(), calls=%async_computation.30 | async-start | bytes 2621440 | tf_op jit(solution)/shard_map/while/body/eval_jaxpr/all_gather | solution.py:107
  1406.3 45.9 %all-gather.24.cloned.1.call-start = ((), (), s32[]{:S(2)}) async-start(), calls=%async_computation.30 | async-start | bytes 2621440 | tf_op jit(solution)/shard_map/while/body/eval_jaxpr/all_gather | solution.py:107
  1669.2 149.1 %reduce-scatter.30.cloned.1.call-start = ((), (), s32[]{:S(2)}) async-start(), calls=%async_computation.32 | async-start | bytes 2621440 | tf_op jit(solution)/shard_map/while/body/eval_jaxpr/reduce_scatter | solution.py:305
  1754.5 66.5 %reduce-scatter.32.cloned.1.call-start = ((), (), s32[]{:S(2)}) async-start(), calls=%async_computation.33 | async-start | bytes 2621440 | tf_op jit(solution)/shard_map/while/body/eval_jaxpr/reduce_scatter | solution.py:311
  1929.5 167.2 %reduce-scatter.30.cloned.1.call-start = ((), (), s32[]{:S(2)}) async-start(), calls=%async_computation.32 | async-start | bytes 2621440 | tf_op jit(solution)/shard_map/while/body/eval_jaxpr/reduce_scatter | solution.py:305
  2019.8 79.5 %reduce-scatter.32.cloned.1.call-start = ((), (), s32[]{:S(2)}) async-start(), calls=%async_computation.33 | async-start | bytes 2621440 | tf_op jit(solution)/shard_map/while/body/eval_jaxpr/reduce_scatter | solution.py:311
  2207.9 167.0 %reduce-scatter.30.cloned.1.call-start = ((), (), s32[]{:S(2)}) async-start(), calls=%async_computation.32 | async-start | bytes 2621440 | tf_op jit(solution)/shard_map/while/body/eval_jaxpr/reduce_scatter | solution.py:305
  2298.2 79.2 %reduce-scatter.32.cloned.1.call-start = ((), (), s32[]{:S(2)}) async-start(), calls=%async_computation.33 | async-start | bytes 2621440 | tf_op jit(solution)/shard_map/while/body/eval_jaxpr/reduce_scatter | solution.py:311
  2410.7 86.1 %reduce-scatter.16.cloned.1.call-start = ((), (), s32[]{:S(2)}) async-start(), calls=%async_computation.22 | async-start | bytes 2621440 | tf_op jit(solution)/shard_map/reduce_scatter | solution.py:463
  2414.8 128.1 %reduce-scatter.18.cloned.1.call-start = ((), (), s32[]{:S(2)}) async-start(), calls=%async_computation.23 | async-start | bytes 2621440 | tf_op jit(solution)/shard_map/reduce_scatter | solution.py:466
  2418.7 170.4 %reduce-scatter.20.cloned.1.call-start = ((), (), s32[]{:S(2)}) async-start(), calls=%async_computation.24 | async-start | bytes 2621440 | tf_op jit(solution)/shard_map/reduce_scatter | solution.py:469
  2422.7 1685.4 %reduce-scatter.28.cloned.1.call-start = ((), (), s32[]{:S(2)}) async-start(), calls=%async_computation.28 | async-start | bytes 327680
  2423.6 1693.4 %all-reduce.8.cloned.1.call-start = ((), (), s32[]{:S(2)}) async-start(), calls=%async_computation.29 | async-start | bytes 4194304 | tf_op jit(solution)/shard_map/psum | solution.py:495
  2589.1 1535.5 %reduce-scatter.22.cloned.1.call-start = ((), (), s32[]{:S(2)}) async-start(), calls=%async_computation.25 | async-start | bytes 7208960 | tf_op jit(solution)/shard_map/reduce_scatter | solution.py:505
  2596.5 1531.3 %reduce-scatter.24.cloned.1.call-start = ((), (), s32[]{:S(2)}) async-start(), calls=%async_computation.26 | async-start | bytes 7208960 | tf_op jit(solution)/shard_map/reduce_scatter | solution.py:508
  2603.8 1527.0 %reduce-scatter.26.cloned.1.call-start = ((), (), s32[]{:S(2)}) async-start(), calls=%async_computation.27 | async-start | bytes 7208960 | tf_op jit(solution)/shard_map/reduce_scatter | solution.py:511
  (135 other events, 4609.0 us)
Sparse Core Ops, SparseCore 0:
  9.6 48.6 all-gather.9
  59.9 44.8 all-gather.11
  106.3 44.6 all-gather.13
  152.5 44.6 all-gather.15
  198.6 42.1 all-gather.17
  242.1 43.3 all-gather.19
  287.1 44.1 all-gather.21
  1067.6 22.5 all-gather.23
  1248.6 22.5 all-gather.23
  1429.6 22.5 all-gather.23
  1754.6 30.5 reduce-scatter.29
  1788.1 31.4 reduce-scatter.31
  2019.9 28.6 reduce-scatter.29
  2051.5 31.4 reduce-scatter.31
  2298.4 28.6 reduce-scatter.29
  2330.1 31.3 reduce-scatter.31
  2410.8 39.7 reduce-scatter.13
  2453.6 43.1 reduce-scatter.15
  2499.7 43.1 reduce-scatter.17
  2545.8 43.1 reduce-scatter.19
  2613.5 50.1 all-reduce.7
  2666.1 54.9 reduce-scatter.21
  2723.6 54.8 reduce-scatter.23
  2781.1 54.8 reduce-scatter.25
  (4 shorter events, 82.6 us)
where the time goes:
time: 4150 us; the launch traced here: 4140 us
  other arithmetic  1670 us (40%)
  local copies, waits for them, and re-layouts  1220 us (29%)
  matrix products  605 us (15%)
  waiting for transfers between devices  468 us (11%)
  starting transfers between devices  68.3 us (2%)
  blocking collectives  65.4 us (2%)
    scatter-add x1, other arithmetic, shards(): jax.ops.segment_sum(sum_scores.reshape(HEADS, -1).T, offsets.reshape(-1),...  1390 us
    gather x2, local copies, waits for them, and re-layouts, shards(): bias_now = jnp.take(by_offset, offsets, axis=1)  941 us
    dot_general x27, matrix products, matmul(): return jnp.dot(left, right, preferred_element_type=jnp.float32)  105 us
    dot_general x6, matrix products, attention_scores(): jnp.einsum('qhd,khd->hqk', queries.reshape(tok_rows, HEADS, HEAD_DIM), ke...  90.4 us
  transfers between devices with their start and end apart: 46, of which 28 were waited for; matrix products, arithmetic and copies ran while one was open for 71% of the time, Pallas kernels for 0%

commit v1 on v0

v1 whole, which is shorter than its diff:
```python
import functools
import math

import jax
import jax.numpy as jnp
from jax import lax
from jax.experimental import pallas as pl
from jax.experimental.pallas import tpu as pltpu
from jax.sharding import Mesh
from jax.sharding import PartitionSpec as P

HEADS = 16
HEAD_DIM = 64
EPSILON = 1e-06
ROOT_SIZE = math.sqrt(HEAD_DIM)

SECTION = "section"
EXPERT = "expert"
OUTER = "outer"
INNER = "inner"
REPLICA = (OUTER, INNER)

BF16 = jnp.bfloat16
F32 = jnp.float32
ROWS = 128


def matmul(left, right):
    return jnp.dot(left, right, preferred_element_type=F32)


def dot_nt(left, right):
    return lax.dot_general(left, right, (((1,), (1,)), ((), ())), preferred_element_type=F32)


def dot_tn(left, right):
    return lax.dot_general(left, right, (((0,), (0,)), ((), ())), preferred_element_type=F32)


def rms_scale(values, gain):
    return values * lax.rsqrt(jnp.mean(values * values, axis=-1, keepdims=True) + EPSILON) * gain


def softmax_rows(scores):
    row_top = jnp.max(scores, axis=-1, keepdims=True)
    expos = jnp.exp(scores - row_top)
    return expos / jnp.sum(expos, axis=-1, keepdims=True)


def gated_gelu(gate_part, up_part):
    return jax.nn.gelu(gate_part, approximate=True) * up_part


def shift_to(value, axis, steps):
    count = lax.axis_size(axis)
    return lax.ppermute(value, axis, [(source, (source + steps) % count) for source in range(count)])


def bias_rows(window, half, queries):
    width = queries + ROWS
    start = ROWS * (1 - half)
    part = jnp.broadcast_to(window[:, start : start + width], (ROWS, width))
    return pltpu.roll(part, width - ROWS, axis=1, stride=1, stride_axis=0)[:, :queries]


def attention_forward_kernel(q_ref, k0, k1, k2, k3, v0, v1, v2, v3, w_ref, o_ref, l_ref, s_ref, p_ref):
    queries = q_ref[...]
    count = queries.shape[0]
    lanes = lax.broadcasted_iota(jnp.int32, queries.shape, 1)
    ks, vs = (k0, k1, k2, k3), (v0, v1, v2, v3)
    outs = []
    for head in range(2):
        own = (lanes < HEAD_DIM) if head == 0 else (lanes >= HEAD_DIM)
        q_head = jnp.where(own, queries, jnp.zeros_like(queries)) * jnp.asarray(1.0 / ROOT_SIZE, BF16)
        top = None
        for chunk in range(8):
            block, half = divmod(chunk, 2)
            rows = slice(half * ROWS, (half + 1) * ROWS)
            score = dot_nt(ks[block][rows, :], q_head)
            score = score + bias_rows(w_ref[head, block : block + 1, :], half, count)
            s_ref[chunk * ROWS : (chunk + 1) * ROWS, :] = score
            chunk_top = jnp.max(score, axis=0, keepdims=True)
            top = chunk_top if top is None else jnp.maximum(top, chunk_top)
        total = None
        for chunk in range(8):
            rows = slice(chunk * ROWS, (chunk + 1) * ROWS)
            expo = jnp.exp(s_ref[rows, :] - top)
            p_ref[rows, :] = expo.astype(BF16)
            part = jnp.sum(expo, axis=0, keepdims=True)
            total = part if total is None else total + part
        mixed = None
        for block in range(4):
            part = dot_tn(vs[block][...], p_ref[block * count : (block + 1) * count, :])
            mixed = part if mixed is None else mixed + part
        outs.append(mixed[head * HEAD_DIM : (head + 1) * HEAD_DIM, :] / total)
        l_ref[0, head : head + 1, :] = top + jnp.log(total)
    o_ref[...] = jnp.concatenate(outs, axis=0).T.astype(BF16)


def attention_forward(queries, keys, values, windows):
    rows, width = queries.shape
    pairs = HEADS // 2
    pair = 2 * HEAD_DIM
    chunk_spec = pl.BlockSpec((rows, pair), lambda g: (0, g))
    return pl.pallas_call(
        attention_forward_kernel,
        grid=(pairs,),
        in_specs=[chunk_spec] * 9 + [pl.BlockSpec((2,) + windows.shape[1:], lambda g: (g, 0, 0))],
        out_specs=[chunk_spec, pl.BlockSpec((1, 2, rows), lambda g: (g, 0, 0))],
        out_shape=[
            jax.ShapeDtypeStruct((rows, width), BF16),
            jax.ShapeDtypeStruct((pairs, 2, rows), F32),
        ],
        scratch_shapes=[pltpu.VMEM((4 * rows, rows), F32), pltpu.VMEM((4 * rows, rows), BF16)],
        cost_estimate=pl.CostEstimate(
            flops=16 * rows * rows * width, bytes_accessed=20 * rows * width, transcendentals=4 * rows * rows * HEADS
        ),
        name="attention_forward",
    )(queries, *keys, *values, windows)


def attention_backward_kernel(
    q_ref, g_ref, l_ref, k0, k1, k2, k3, v0, v1, v2, v3, w_ref,
    dq_ref, dk0, dk1, dk2, dk3, dv0, dv1, dv2, dv3, dw_ref, p_ref, d_ref, ds_ref, pb_ref,
):
    queries = q_ref[...]
    grads = g_ref[...]
    count = queries.shape[0]
    lanes = lax.broadcasted_iota(jnp.int32, queries.shape, 1)
    ks, vs = (k0, k1, k2, k3), (v0, v1, v2, v3)
    dks, dvs = (dk0, dk1, dk2, dk3), (dv0, dv1, dv2, dv3)
    key_sums, value_sums, query_parts = [None] * 4, [None] * 4, []
    for head in range(2):
        own = (lanes < HEAD_DIM) if head == 0 else (lanes >= HEAD_DIM)
        q_head = jnp.where(own, queries, jnp.zeros_like(queries)) * jnp.asarray(1.0 / ROOT_SIZE, BF16)
        g_head = jnp.where(own, grads, jnp.zeros_like(grads))
        level = l_ref[0, head : head + 1, :]
        row_dot = None
        for chunk in range(8):
            block, half = divmod(chunk, 2)
            rows = slice(half * ROWS, (half + 1) * ROWS)
            place = slice(chunk * ROWS, (chunk + 1) * ROWS)
            score = dot_nt(ks[block][rows, :], q_head)
            score = score + bias_rows(w_ref[head, block : block + 1, :], half, count)
            attention = jnp.exp(score - level)
            grad_attention = dot_nt(vs[block][rows, :], g_head)
            p_ref[place, :] = attention
            pb_ref[place, :] = attention.astype(BF16)
            d_ref[place, :] = grad_attention
            part = jnp.sum(attention * grad_attention, axis=0, keepdims=True)
            row_dot = part if row_dot is None else row_dot + part
        for chunk in range(8):
            block, half = divmod(chunk, 2)
            place = slice(chunk * ROWS, (chunk + 1) * ROWS)
            grad_score = (p_ref[place, :] * (d_ref[place, :] - row_dot)).astype(BF16)
            ds_ref[place, :] = grad_score
            sheared = jnp.concatenate([grad_score.astype(F32), jnp.zeros((ROWS, ROWS), F32)], axis=1)
            live = ROWS
            while live > 8:
                live = live // 2
                sheared = pltpu.roll(sheared[:live, :], live, axis=1) + sheared[live:, :]
            start = ROWS * (1 - half)
            if half == 0:
                dw_ref[head, block, :, 0:ROWS] = jnp.zeros((8, ROWS), F32)
                dw_ref[head, block, :, start : start + count + ROWS] = sheared
            else:
                dw_ref[head, block, :, start : start + count + ROWS] += sheared
        query_part = None
        for block in range(4):
            place = slice(block * count, (block + 1) * count)
            part = dot_tn(ks[block][...], ds_ref[place, :])
            query_part = part if query_part is None else query_part + part
            key_part = matmul(ds_ref[place, :], q_head)
            value_part = matmul(pb_ref[place, :], g_head)
            if head == 0:
                key_sums[block], value_sums[block] = key_part, value_part
            else:
                dks[block][...] = (key_sums[block] + key_part).astype(dks[block].dtype)
                dvs[block][...] = (value_sums[block] + value_part).astype(dvs[block].dtype)
        query_parts.append(query_part[head * HEAD_DIM : (head + 1) * HEAD_DIM, :])
    dq_ref[...] = (jnp.concatenate(query_parts, axis=0).T * (1.0 / ROOT_SIZE)).astype(BF16)


def attention_backward(queries, grads, levels, keys, values, windows):
    rows, width = queries.shape
    pairs = HEADS // 2
    pair = 2 * HEAD_DIM
    chunk_spec = pl.BlockSpec((rows, pair), lambda g: (0, g))
    span = windows.shape[-1]
    kinds = [BF16] + [F32, BF16, F32, BF16] * 2
    outs = pl.pallas_call(
        attention_backward_kernel,
        grid=(pairs,),
        in_specs=[chunk_spec] * 2
        + [pl.BlockSpec((1, 2, rows), lambda g: (g, 0, 0))]
        + [chunk_spec] * 8
        + [pl.BlockSpec((2,) + windows.shape[1:], lambda g: (g, 0, 0))],
        out_specs=[chunk_spec] * 9 + [pl.BlockSpec((2, 4, 8, span), lambda g: (g, 0, 0, 0))],
        out_shape=[jax.ShapeDtypeStruct((rows, width), kind) for kind in kinds]
        + [jax.ShapeDtypeStruct((HEADS, 4, 8, span), F32)],
        scratch_shapes=[
            pltpu.VMEM((4 * rows, rows), F32),
            pltpu.VMEM((4 * rows, rows), F32),
            pltpu.VMEM((4 * rows, rows), BF16),
            pltpu.VMEM((4 * rows, rows), BF16),
        ],
        cost_estimate=pl.CostEstimate(
            flops=40 * rows * rows * width, bytes_accessed=60 * rows * width, transcendentals=4 * rows * rows * HEADS
        ),
        name="attention_backward",
    )(queries, grads, levels, *keys, *values, windows)
    return outs[0], outs[1:5], outs[5:9], outs[9]


def fold_rows(sheared):
    span = sheared.shape[-1]
    total = 0.0
    for row in range(8):
        total = total + jnp.roll(sheared[..., row, :], 8 - row, axis=-1)
    return total


def section_swap(value):
    return lax.ppermute(value, SECTION, [(0, 1), (1, 0)])


def inner_swap(value):
    return shift_to(value, INNER, 1)


def outer_swap(value):
    return shift_to(value, OUTER, 1)


def rms_pull(values, gain, grad):
    scale = lax.rsqrt(jnp.mean(values * values, axis=-1, keepdims=True) + EPSILON)
    weighted = grad * gain
    lean = jnp.mean(weighted * values, axis=-1, keepdims=True)
    grad_values = scale * weighted - values * (scale * scale * scale * lean)
    grad_gain = jnp.sum(grad * values * scale, axis=0)
    return grad_values, grad_gain


def send_slots(rows, direction):
    count = lax.axis_size(EXPERT)
    parts = [rows[0]] + [shift_to(rows[k], EXPERT, direction * k) for k in range(1, count)]
    return jnp.concatenate(parts, axis=0)


def route_tables(route, capacity):
    tokens = route.shape[0]
    count = lax.axis_size(EXPERT)
    ahead = jnp.remainder(route - lax.axis_index(EXPERT) + count, count)
    onehot = (ahead[:, :, None] == jnp.arange(count, dtype=jnp.int32)).astype(F32)
    per_row = jnp.sum(onehot, axis=1)
    earlier = (jnp.arange(tokens)[:, None] > jnp.arange(tokens)[None, :]).astype(BF16)
    before = matmul(earlier, per_row.astype(BF16))
    slot_place = jnp.sum(before[:, None, :] * onehot, axis=2).astype(jnp.int32)
    target = ahead * capacity + slot_place
    slots = jnp.arange(count * capacity, dtype=jnp.int32)
    spots = (target[:, 0:1] == slots) | (target[:, 1:2] == slots)
    owner = jnp.remainder(slots // capacity + lax.axis_index(EXPERT), count)
    members = (owner[:, None] == jnp.arange(count, dtype=jnp.int32)).astype(F32)
    return spots, members


def forward(section_in, tables, weights, windows):
    spots, members = tables
    slot_table = spots.astype(BF16)
    slot_count = slot_table.shape[1]
    expert_count = lax.axis_size(EXPERT)
    inputs = section_in.astype(F32)
    width = inputs.shape[1]
    normed = rms_scale(inputs, weights["gain_first"]).astype(BF16)
    key_own = matmul(normed, weights["key"]).astype(BF16)
    value_own = matmul(normed, weights["value"]).astype(BF16)
    key_outer, value_outer = outer_swap(key_own), outer_swap(value_own)
    key_inner, value_inner = inner_swap(key_own), inner_swap(value_own)
    queries = matmul(normed, weights["query"]).astype(BF16)
    key_both, value_both = inner_swap(key_outer), inner_swap(value_outer)
    keys = (key_own, key_inner, key_outer, key_both)
    values = (value_own, value_inner, value_outer, value_both)
    attended, levels = attention_forward(queries, keys, values, windows)
    middle = inputs + matmul(attended, weights["output"])
    mixed_in = rms_scale(middle, weights["gain_second"]).astype(BF16)
    packed = dot_tn(slot_table, mixed_in).astype(BF16)
    arrived = send_slots(packed.reshape(expert_count, -1, width), 1)
    gates_all = softmax_rows(matmul(mixed_in, weights["router"]))
    spread = lax.dot_general(
        gates_all, members, (((1,), (1,)), ((), ())), precision=lax.Precision.HIGHEST, preferred_element_type=F32
    )
    combine = jnp.where(spots, spread, 0.0)
    combine_high = combine.astype(BF16)
    combine_low = (combine - combine_high.astype(F32)).astype(BF16)
    gate_part = matmul(arrived, weights["gate"])
    up_part = matmul(arrived, weights["up"])
    hidden = gated_gelu(gate_part, up_part).astype(BF16)
    produced = matmul(hidden, weights["down"]).astype(BF16)
    returned = send_slots(produced.reshape(expert_count, -1, width), -1)
    mixed_out = matmul(combine_high, returned) + matmul(combine_low, returned)
    result = (middle + mixed_out).astype(BF16)
    stored = (
        inputs, normed, queries, keys, values, attended, levels, middle, mixed_in, gates_all,
        arrived, gate_part, up_part, hidden, returned, combine_high, combine_low,
    )
    return result, stored


def backward(grad_rows, stored, tables, weights, windows, bucket_rows):
    spots, members = tables
    slot_table = spots.astype(BF16)
    (
        inputs, normed, queries, keys, values, attended, levels, middle, mixed_in, gates_all,
        arrived, gate_part, up_part, hidden, returned, combine_high, combine_low,
    ) = stored
    expert_count = lax.axis_size(EXPERT)
    width = inputs.shape[1]
    grad_out = grad_rows.astype(F32)
    grad_slots = (dot_tn(combine_high, grad_rows) + dot_tn(combine_low, grad_rows)).astype(BF16)
    received = send_slots(grad_slots.reshape(expert_count, -1, width), 1)
    products = jnp.where(spots, dot_nt(grad_rows, returned), 0.0)
    grad_gates = jnp.dot(products, members, precision=lax.Precision.HIGHEST, preferred_element_type=F32)
    grad_logits = gates_all * (grad_gates - jnp.sum(gates_all * grad_gates, axis=-1, keepdims=True))
    grad_logits = grad_logits.astype(BF16)
    term_router = dot_tn(mixed_in, grad_logits)

    grad_hidden = dot_nt(received, weights["down"])
    unused_value, pull_gelu = jax.vjp(gated_gelu, gate_part, up_part)
    grad_gate, grad_up = pull_gelu(grad_hidden)
    grad_gate = grad_gate.astype(BF16)
    grad_up = grad_up.astype(BF16)
    grad_arrived = (dot_nt(grad_gate, weights["gate"]) + dot_nt(grad_up, weights["up"])).astype(BF16)
    back_rows = send_slots(grad_arrived.reshape(expert_count, -1, width), -1)
    term_down = dot_tn(hidden, received).astype(BF16)
    term_gate = dot_tn(arrived, grad_gate).astype(BF16)
    term_up = dot_tn(arrived, grad_up).astype(BF16)

    grad_mixed = matmul(slot_table, back_rows) + dot_nt(grad_logits, weights["router"])
    grad_middle, term_second = rms_pull(middle, weights["gain_second"], grad_mixed)
    grad_middle = grad_middle + grad_out
    grad_branch = grad_middle.astype(BF16)
    grad_attended = dot_nt(grad_branch, weights["output"]).astype(BF16)
    term_output = dot_tn(attended, grad_branch).astype(BF16)
    grad_queries, key_parts, value_parts, sheared = attention_backward(
        queries, grad_attended, levels, keys, values, windows
    )

    def gather_parts(parts):
        own, inner, outer, both = parts
        passed = (outer + inner_swap(both).astype(F32)).astype(BF16)
        return own + inner_swap(inner).astype(F32) + outer_swap(passed).astype(F32)

    grad_keys = gather_parts(key_parts).astype(BF16)
    grad_values = gather_parts(value_parts).astype(BF16)
    grad_windows = fold_rows(sheared).reshape(HEADS, -1)
    term_position = lax.dot_general(
        grad_windows, bucket_rows.astype(F32), (((1,), (1,)), ((), ())),
        precision=lax.Precision.HIGHEST, preferred_element_type=F32,
    )
    term_query = dot_tn(normed, grad_queries).astype(BF16)
    term_key = dot_tn(normed, grad_keys).astype(BF16)
    term_value = dot_tn(normed, grad_values).astype(BF16)
    grad_normed = (
        dot_nt(grad_queries, weights["query"])
        + dot_nt(grad_keys, weights["key"])
        + dot_nt(grad_values, weights["value"])
    )
    grad_in, term_first = rms_pull(inputs, weights["gain_first"], grad_normed)
    grad_in = grad_in + grad_middle
    dense_terms = (term_query, term_key, term_value, term_output)
    small_terms = (term_router, term_first, term_second, term_position)
    expert_terms = (term_gate, term_up, term_down)
    return grad_in, dense_terms, small_terms, expert_terms


def pack_small(router, first, second, position, count):
    parts = [router.reshape(count, -1), first.reshape(count, -1), second.reshape(count, -1), position.reshape(count, -1)]
    flat = jnp.concatenate(parts, axis=1)
    return jnp.pad(flat, ((0, 0), (0, -flat.shape[1] % 1024)))


def unpack_small(flat, rows, experts, heads, buckets):
    sizes = [rows * experts, rows, rows, heads * buckets]
    starts = [sum(sizes[:k]) for k in range(5)]
    pieces = [flat[:, starts[k] : starts[k + 1]] for k in range(4)]
    return pieces[0].reshape(-1, experts), pieces[1].reshape(-1), pieces[2].reshape(-1), pieces[3].reshape(-1, buckets)


def shards(
    inputs,
    cotangent,
    routes,
    bucket_table,
    query_weight,
    key_weight,
    value_weight,
    output_weight,
    router_weight,
    attention_gain,
    mixture_gain,
    position_bias,
    expert_gate,
    expert_up,
    expert_down,
):
    micro_count = inputs.shape[0]
    tok_rows = inputs.shape[2]
    model_width = inputs.shape[3]
    expert_count = lax.axis_size(EXPERT)
    replica_count = lax.axis_size(OUTER) * lax.axis_size(INNER)
    assert micro_count == lax.axis_size(SECTION) == 2 and replica_count == 4
    capacity = max(2, 9 * tok_rows // (4 * expert_count))
    length = tok_rows * replica_count
    buckets = position_bias.shape[2]
    section_index = lax.axis_index(SECTION)
    replica_index = 2 * lax.axis_index(OUTER) + lax.axis_index(INNER)
    first_section = section_index == 0

    own_rows = lax.dynamic_index_in_dim(inputs[:, 0], section_index, 0, keepdims=False)
    own_cotangent = lax.dynamic_index_in_dim(cotangent[:, 0], section_index, 0, keepdims=False)
    layer_routes = routes[0, :, 0]
    route_kept = lax.dynamic_index_in_dim(layer_routes, section_index, 0, keepdims=False)
    route_given = lax.dynamic_index_in_dim(layer_routes, 1 - section_index, 0, keepdims=False)
    route_taken = section_swap(route_given)
    layer_route = (
        jnp.where(first_section, route_kept, route_taken),
        jnp.where(first_section, route_taken, route_kept),
    )

    dense_rows = query_weight.shape[1]
    dense_stack = jnp.stack([query_weight[0], key_weight[0], value_weight[0], output_weight[0]])
    dense_piece = lax.dynamic_index_in_dim(dense_stack, replica_index, 0, keepdims=False)
    dense_all = lax.all_gather(dense_piece, (SECTION, OUTER, INNER, EXPERT), axis=0, tiled=False)
    dense_all = dense_all.reshape(2, 4, model_width, model_width)
    heads_own = position_bias.shape[1]
    small_piece = pack_small(router_weight[0], attention_gain[0], mixture_gain[0], position_bias[0], 1)
    small_all = lax.all_gather(small_piece[0].reshape(-1, 128), (SECTION, EXPERT), axis=0, tiled=False)
    small_all = small_all.reshape(2, expert_count, -1)
    gate_all = lax.all_gather(expert_gate[0, 0], (SECTION,) + REPLICA, axis=0, tiled=False)
    up_all = lax.all_gather(expert_up[0, 0], (SECTION,) + REPLICA, axis=0, tiled=False)
    down_all = lax.all_gather(expert_down[0, 0], (SECTION,) + REPLICA, axis=0, tiled=False)
    hidden_width = expert_gate.shape[3]
    gate_all = gate_all.reshape(2, model_width, hidden_width)
    up_all = up_all.reshape(2, model_width, hidden_width)
    down_all = down_all.reshape(2, replica_count, hidden_width, -1)

    reversed_table = jnp.concatenate([jnp.full((1,), -1, jnp.int32), bucket_table[::-1]])
    bucket_onehot = (jnp.arange(buckets, dtype=jnp.int32)[:, None] == reversed_table[None, :]).astype(BF16)
    bucket_rows = jnp.concatenate(
        [
            lax.dynamic_slice(
                bucket_onehot,
                (0, (3 + replica_index - jnp.bitwise_xor(replica_index, ahead)) * tok_rows),
                (buckets, 2 * tok_rows),
            )
            for ahead in range(4)
        ],
        axis=1,
    )

    layers = []
    for layer in range(2):
        router, first, second, position = unpack_small(small_all[layer], dense_rows, expert_count, heads_own, buckets)
        weights = dict(
            query=dense_all[layer, 0],
            key=dense_all[layer, 1],
            value=dense_all[layer, 2],
            output=dense_all[layer, 3],
            router=router,
            gain_first=first.astype(F32),
            gain_second=second.astype(F32),
            gate=gate_all[layer],
            up=up_all[layer],
            down=down_all[layer].transpose(1, 0, 2).reshape(hidden_width, model_width),
        )
        windows = matmul(position, bucket_rows).reshape(HEADS, 4, 2 * tok_rows)
        layers.append((weights, windows, route_tables(layer_route[layer], capacity)))

    rows, outputs, kept = own_rows, [], []
    for weights, windows, tables in layers:
        rows, stored = forward(rows, tables, weights, windows)
        outputs.append(rows)
        kept.append(stored)

    grads, results = own_cotangent, [None, None]
    input_grads = [None, None]
    for layer in (1, 0):
        weights, windows, tables = layers[layer]
        grad_in, dense_terms, small_terms, expert_terms = backward(
            grads, kept[layer], tables, weights, windows, bucket_rows
        )
        grads = grad_in.astype(BF16)
        input_grads[layer] = (grad_in, grads)
        gate_share = lax.psum_scatter(expert_terms[0], REPLICA, scatter_dimension=0, tiled=True)
        up_share = lax.psum_scatter(expert_terms[1], REPLICA, scatter_dimension=0, tiled=True)
        down_share = lax.psum_scatter(expert_terms[2], REPLICA, scatter_dimension=1, tiled=True)
        dense = jnp.stack(dense_terms).reshape(4 * expert_count, dense_rows, model_width)
        dense_share = lax.psum_scatter(dense, REPLICA + (EXPERT,), scatter_dimension=0, tiled=False)
        small = pack_small(*small_terms, expert_count)
        results[layer] = ((gate_share, up_share, down_share, dense_share), small)

    def settle(layer_pair):
        zero, one = layer_pair
        from_zero = lax.ppermute(zero, SECTION, [(1, 0)])
        from_one = lax.ppermute(one, SECTION, [(0, 1)])
        own = jnp.where(first_section, zero, one).astype(F32)
        other = jnp.where(first_section, from_zero, from_one).astype(F32)
        return own + other

    final_gate, final_up, final_down, final_dense = (
        settle((results[0][0][k], results[1][0][k])) for k in range(4)
    )
    final_dense = lax.all_gather(final_dense.astype(BF16), REPLICA, axis=0, tiled=False).astype(F32)
    small_sum = lax.psum(
        jnp.stack([results[0][1], results[1][1]]).astype(BF16), (SECTION, EXPERT) + REPLICA
    ).astype(F32)
    small_own = lax.dynamic_slice(
        small_sum, (section_index, lax.axis_index(EXPERT), 0), (1, 1, small_sum.shape[2])
    )[0]
    final_router, final_first, final_second, final_position = unpack_small(
        small_own, dense_rows, expert_count, heads_own, buckets
    )

    def both_micros(kept_one, taken_one):
        return jnp.where(
            first_section, jnp.stack([kept_one, taken_one]), jnp.stack([taken_one, kept_one])
        )[None, :, None]

    output_taken = section_swap(jnp.where(first_section, outputs[1], outputs[0]))
    section_output = both_micros(jnp.where(first_section, outputs[0], outputs[1]), output_taken)
    grad_from_one = lax.ppermute(input_grads[1][1], SECTION, [(0, 1)])
    grad_from_zero = lax.ppermute(input_grads[0][1], SECTION, [(1, 0)])
    grad_taken = jnp.where(first_section, grad_from_zero, grad_from_one).astype(F32)
    grad_kept = jnp.where(first_section, input_grads[0][0], input_grads[1][0])
    input_gradient = both_micros(grad_kept, grad_taken)
    return (
        section_output,
        input_gradient,
        final_dense[0:1],
        final_dense[1:2],
        final_dense[2:3],
        final_dense[3:4],
        final_router[None],
        final_first[None],
        final_second[None],
        final_position[None],
        final_gate[None, None],
        final_up[None, None],
        final_down[None, None],
    )


def solution(mesh):
    sections, experts, replicas = (mesh.shape[name] for name in ("section", "expert", "replica"))
    fine = Mesh(
        mesh.devices.reshape(sections, experts, replicas // 2, 2), (SECTION, EXPERT, OUTER, INNER)
    )
    rep = REPLICA
    in_specs = (
        P(None, "expert", rep, None),
        P(None, "expert", rep, None),
        P("section", None, "expert", rep, None),
        P(),
        P("section", "expert", None),
        P("section", "expert", None),
        P("section", "expert", None),
        P("section", "expert", None),
        P("section", "expert", None),
        P("section", "expert"),
        P("section", "expert"),
        P("section", "expert", None),
        P("section", "expert", rep, None),
        P("section", "expert", rep, None),
        P("section", "expert", None, rep),
    )
    out_specs = (
        P("section", None, "expert", rep, None),
        P("section", None, "expert", rep, None),
        P("section", "expert", None),
        P("section", "expert", None),
        P("section", "expert", None),
        P("section", "expert", None),
        P("section", "expert", None),
        P("section", "expert"),
        P("section", "expert"),
        P("section", "expert", None),
        P("section", "expert", rep, None),
        P("section", "expert", rep, None),
        P("section", "expert", None, rep),
    )
    return jax.shard_map(shards, mesh=fine, in_specs=in_specs, out_specs=out_specs, check_vma=False)
```

time: 4150 us -> 1290 us (0.31)
  other arithmetic: 1670 us -> 40.6 us
  local copies, waits for them, and re-layouts: 1220 us -> 78.1 us
  matrix products: 605 us -> 205 us
  waiting for transfers between devices: 468 us -> 644 us
  Pallas kernels: 0 us -> 103 us
    scatter-add x5 -> x0, other arithmetic: 1420 us -> none  [the longest x1 1390 us: shards(): jax.ops.segment_sum(sum_scores.reshape(HEADS, -1).T, offsets.reshape(-1),...]
    gather x41 -> x0, local copies, waits for them, and re-layouts: 998 us -> none  [the longest x2 941 us: shards(): bias_now = jnp.take(by_offset, offsets, axis=1)]
    dot_general x102 -> x72, matrix products: 605 us -> 205 us  [the longest x18 75.1 us: dot_nt(): lax.dot_general(left, right, (((1,), (1,)), ((), ())), preferred_element_...]
    all_to_all x12 -> x0, waiting for transfers between devices: 204 us -> none  [the longest x3 73.2 us: forward(): lax.all_to_all(packed.reshape(expert_count, capacity, model_width), 'expe...]
    all_gather x13 -> x5, waiting for transfers between devices: 44.9 us -> 247 us  [the longest x1 80.5 us: shards(): lax.all_gather(dense_piece, (SECTION, OUTER, INNER, EXPERT), axis=0, tile...]
    ppermute x6 -> x60, waiting for transfers between devices: 48.7 us -> 211 us  [the longest x48 175 us: shift_to(): lax.ppermute(value, axis, [(source, (source + steps) % count) for source...]
    pallas_call x0 -> x4, Pallas kernels: none -> 103 us  [the longest x2 72.1 us: attention_backward(): pl.pallas_call(attention_backward_kernel, grid=(pairs,), in_specs=[chunk_...]
    ppermute x6 -> x60, starting transfers between devices: 14.6 us -> 102 us  [the longest x48 70.6 us: shift_to(): lax.ppermute(value, axis, [(source, (source + steps) % count) for source...]
  transfers between devices with their start and end apart: 46 -> 73, of which waited for: 28 -> 29; matrix products, arithmetic and copies ran while one was open for 71% -> 21% of each run, Pallas kernels for 0% -> 7%
where the time goes in v1:
time: 1290 us; the launch traced here: 1280 us
  waiting for transfers between devices  644 us (50%)
  matrix products  205 us (16%)
  starting transfers between devices  103 us (8%)
  Pallas kernels  103 us (8%)
  blocking collectives  94.6 us (7%)
  local copies, waits for them, and re-layouts  78.1 us (6%)
  other arithmetic  40.6 us (3%)
  between operations  16.7 us (1%)
    ppermute x48, waiting for transfers between devices, shift_to(): lax.ppermute(value, axis, [(source, (source + steps) % count) for source...  175 us
    reduce_scatter x2, waiting for transfers between devices, shards(): lax.psum_scatter(expert_terms[2], REPLICA, scatter_dimension=1, tiled=True)  105 us
    all_gather x1, waiting for transfers between devices, shards(): lax.all_gather(dense_piece, (SECTION, OUTER, INNER, EXPERT), axis=0, tile...  80.5 us
    reduce_scatter x2, waiting for transfers between devices, shards(): lax.psum_scatter(expert_terms[1], REPLICA, scatter_dimension=0, tiled=True)  78.4 us
    dot_general x18, matrix products, dot_nt(): lax.dot_general(left, right, (((1,), (1,)), ((), ())), preferred_element_...  75.1 us
    all_gather x1, waiting for transfers between devices, shards(): lax.all_gather(expert_gate[0, 0], (SECTION,) + REPLICA, axis=0, tiled=False)  74.5 us
    pallas_call x2, Pallas kernels, attention_backward(): pl.pallas_call(attention_backward_kernel, grid=(pairs,), in_specs=[chunk_...  72.1 us
    ppermute x48, starting transfers between devices, shift_to(): lax.ppermute(value, axis, [(source, (source + steps) % count) for source...  70.6 us
  transfers between devices with their start and end apart: 73, of which 29 were waited for; matrix products, arithmetic and copies ran while one was open for 21% of the time, Pallas kernels for 7%

profile of v1, /device:TPU:0, one launch (start us, length us, event | category | flops | bytes accessed | tf_op | source)
XLA Modules:
  0.0 1284.8 jit_solution(11737922777513566260)
XLA Ops:
  15.3 30.6 %all_gather.22 = bf16[8,16,128]{2,1,0:T(8,128)(2,1)S(1)} all-gather(bf16[1,16,128]{2,1,0:T(8,128)(2,1)S(1)} %bitcast.416), channel_id=1, replica_groups=mesh['section'=2,'expert'=4,'outer'=2,'inner'=2] {'section','expert'}, dimensions={0}, use_global_device_ids=true | all-gather | bytes 36864 | tf_op jit(solution)/shard_map/all_gather | solution.py:437
  49.0 80.5 %all-gather.10.cloned.1.call-done = bf16[32,256,1024]{2,1,0:T(8,128)(2,1)} async-done(((bf16[1,256,1024]{2,1,0:T(8,128)(2,1)}), bf16[32,256,1024]{2,1,0:T(8,128)(2,1)}) %all-gather.10.cloned.1.call-update) | async-done | bytes 16777232 | tf_op jit(solution)/shard_map/all_gather | solution.py:433
  137.1 74.5 %all-gather.12.cloned.1.call-done = bf16[8,1,256,2816]{3,2,1,0:T(8,128)(2,1)} async-done(((bf16[1,1,256,2816]{3,2,1,0:T(8,128)(2,1)}), bf16[8,1,256,2816]{3,2,1,0:T(8,128)(2,1)}) %all-gather.12.cloned.1.call-update) | async-done | bytes 11534352 | tf_op jit(solution)/shard_map/all_gather | solution.py:439
  222.0 59.2 %all-gather.14.cloned.1.call-done = bf16[8,1,256,2816]{3,2,1,0:T(8,128)(2,1)} async-done(((bf16[1,1,256,2816]{3,2,1,0:T(8,128)(2,1)}), bf16[8,1,256,2816]{3,2,1,0:T(8,128)(2,1)}) %all-gather.14.cloned.1.call-update) | async-done | bytes 11534352 | tf_op jit(solution)/shard_map/all_gather | solution.py:440
  294.1 15.2 %attention_forward.2 = (bf16[256,1024]{1,0:T(8,128)(2,1)}, f32[8,2,256]{2,1,0:T(2,128)}) custom-call(bf16[256,1024]{1,0:T(8,128)(2,1)} %fusion.51.q_ref, bf16[256,1024]{1,0:T(8,128)(2,1)} %copy-done.94, bf16[256,1024]{1,0:T(8,128)(2,1)} %collective-permute-done.k1, bf16[256,1024]{1,0:T(8,128)(2,1)} %copy-done.95, ...), custom_call_target="tpu_custom_call" | custom-call | flops 1073741824 | bytes 5242880 | tf_op jit(solution)/shard_map/attention_forward/pallas_call | solution.py:105
  317.8 32.8 %all-gather.16.cloned.1.call-done = bf16[8,1,2816,256]{3,2,1,0:T(8,128)(2,1)} async-done(((bf16[1,1,2816,256]{3,2,1,0:T(8,128)(2,1)}), bf16[8,1,2816,256]{3,2,1,0:T(8,128)(2,1)}) %all-gather.16.cloned.1.call-update) | async-done | bytes 11534352 | tf_op jit(solution)/shard_map/all_gather | solution.py:441
  398.4 12.0 collective-permute-done.11
  451.0 15.2 %attention_forward.3 = (bf16[256,1024]{1,0:T(8,128)(2,1)}, f32[8,2,256]{2,1,0:T(2,128)}) custom-call(bf16[256,1024]{1,0:T(8,128)(2,1)} %fusion.47.q_ref, bf16[256,1024]{1,0:T(8,128)(2,1)} %copy-done.98, bf16[256,1024]{1,0:T(8,128)(2,1)} %collective-permute-done.13.k1, bf16[256,1024]{1,0:T(8,128)(2,1)} %copy-done.99, ...), custom_call_target="tpu_custom_call" | custom-call | flops 1073741824 | bytes 5242880 | tf_op jit(solution)/shard_map/attention_forward/pallas_call | solution.py:105
  485.1 14.8 %collective-permute-start.26 = (bf16[144,1024]{1,0:T(8,128)(2,1)S(1)}, bf16[144,1024]{1,0:T(8,128)(2,1)S(1)}, u32[]{:S(2)}, u32[]{:S(2)}) collective-permute-start(bf16[144,1024]{1,0:T(8,128)(2,1)S(1)} %get-tuple-element.140), channel_id=1, source_target_pairs={{0,4},{4,8},{8,12},{12,0},{1,5},{5,9},{9,13},{13,1},{2,6},{6,10},{... | collective-permute-start | bytes 884744 | tf_op jit(solution)/shard_map/ppermute | solution.py:56
  499.9 18.2 %collective-permute-done.20 = bf16[144,1024]{1,0:T(8,128)(2,1)S(1)} collective-permute-done((bf16[144,1024]{1,0:T(8,128)(2,1)S(1)}, bf16[144,1024]{1,0:T(8,128)(2,1)S(1)}, u32[]{:S(2)}, u32[]{:S(2)}) %collective-permute-start.20) | collective-permute-done | bytes 294944 | tf_op jit(solution)/shard_map/ppermute | solution.py:56
  530.2 12.1 multiply_convert_fusion.1
  601.8 36.1 %attention_backward.2 = (bf16[256,1024]{1,0:T(8,128)(2,1)}, f32[256,1024]{1,0:T(8,128)}, bf16[256,1024]{1,0:T(8,128)(2,1)}, f32[256,1024]{1,0:T(8,128)}, bf16[25...) custom-call(bf16[256,1024]{1,0:T(8,128)(2,1)} %fusion.47.q_ref, ...), custom_call_target="tpu_custom_call" | custom-call | flops 2684354560 | bytes 15728640 | tf_op jit(solution)/shard_map/attention_backward/pallas_call | solution.py:191
  643.8 12.5 collective-permute-done.34
  692.3 18.7 %collective-permute-done.39 = bf16[144,1024]{1,0:T(8,128)(2,1)S(1)} collective-permute-done((bf16[144,1024]{1,0:T(8,128)(2,1)S(1)}, bf16[144,1024]{1,0:T(8,128)(2,1)S(1)}, u32[]{:S(2)}, u32[]{:S(2)}) %collective-permute-start.39) | collective-permute-done | bytes 294944 | tf_op jit(solution)/shard_map/ppermute | solution.py:56
  711.0 11.0 multiply_convert_fusion
  780.6 36.1 %attention_backward.3 = (bf16[256,1024]{1,0:T(8,128)(2,1)}, f32[256,1024]{1,0:T(8,128)}, bf16[256,1024]{1,0:T(8,128)(2,1)}, f32[256,1024]{1,0:T(8,128)}, bf16[25...) custom-call(bf16[256,1024]{1,0:T(8,128)(2,1)} %fusion.51.q_ref, ...), custom_call_target="tpu_custom_call" | custom-call | flops 2684354560 | bytes 15728640 | tf_op jit(solution)/shard_map/attention_backward/pallas_call | solution.py:191
  824.5 20.5 %collective-permute-done.46 = bf16[256,1024]{1,0:T(8,128)(2,1)S(1)} collective-permute-done((bf16[256,1024]{1,0:T(8,128)(2,1)S(1)}, bf16[256,1024]{1,0:T(8,128)(2,1)S(1)}, u32[]{:S(2)}, u32[]{:S(2)}) %collective-permute-start.46) | collective-permute-done | bytes 524320 | tf_op jit(solution)/shard_map/ppermute | solution.py:56
  846.1 14.6 %collective-permute-done.49 = bf16[256,1024]{1,0:T(8,128)(2,1)S(1)} collective-permute-done((bf16[256,1024]{1,0:T(8,128)(2,1)S(1)}, bf16[256,1024]{1,0:T(8,128)(2,1)S(1)}, u32[]{:S(2)}, u32[]{:S(2)}) %collective-permute-start.49) | collective-permute-done | bytes 524320 | tf_op jit(solution)/shard_map/ppermute | solution.py:56
  965.3 64.0 %psum.7 = bf16[2,4,2048]{2,1,0:T(4,128)(2,1)S(1)} all-reduce(bf16[2,4,2048]{2,1,0:T(4,128)(2,1)S(1)} %pad_maximum_fusion.13), channel_id=1, replica_groups=mesh['section'=2,'expert'=4,'outer'=2,'inner'=2] {'section','expert','ou..., use_global_device_ids=true, to_apply=%region_24.25 | all-reduce | flops 16384 | bytes 65536 | tf_op jit(solution)/shard_map/psum | solution.py:514
  1038.2 25.6 %reduce-scatter.19.cloned.1.call-done = bf16[256,2816]{1,0:T(8,128)(2,1)} async-done(((bf16[1024,2816]{1,0:T(8,128)(2,1)}), bf16[256,2816]{1,0:T(8,128)(2,1)}) %reduce-scatter.19.cloned.1.call-update) | async-done | bytes 1441808 | tf_op jit(solution)/shard_map/reduce_scatter | solution.py:495
  1068.4 52.9 %reduce-scatter.17.cloned.1.call-done = bf16[256,2816]{1,0:T(8,128)(2,1)} async-done(((bf16[1024,2816]{1,0:T(8,128)(2,1)}), bf16[256,2816]{1,0:T(8,128)(2,1)}) %reduce-scatter.17.cloned.1.call-update) | async-done | bytes 1441808 | tf_op jit(solution)/shard_map/reduce_scatter | solution.py:495
  1126.6 52.2 %reduce-scatter.23.cloned.1.call-done = bf16[2816,256]{1,0:T(8,128)(2,1)} async-done(((bf16[2816,1024]{1,0:T(8,128)(2,1)}), bf16[2816,256]{1,0:T(8,128)(2,1)}) %reduce-scatter.23.cloned.1.call-update) | async-done | bytes 1441808 | tf_op jit(solution)/shard_map/reduce_scatter | solution.py:496
  1183.2 53.0 %reduce-scatter.21.cloned.1.call-done = bf16[2816,256]{1,0:T(8,128)(2,1)} async-done(((bf16[2816,1024]{1,0:T(8,128)(2,1)}), bf16[2816,256]{1,0:T(8,128)(2,1)}) %reduce-scatter.21.cloned.1.call-update) | async-done | bytes 1441808 | tf_op jit(solution)/shard_map/reduce_scatter | solution.py:496
  1246.0 25.6 %collective-permute-done.58 = bf16[2816,256]{1,0:T(8,128)(2,1)S(1)} collective-permute-done((bf16[2816,256]{1,0:T(8,128)(2,1)}, bf16[2816,256]{1,0:T(8,128)(2,1)S(1)}, u32[]{:S(2)}, u32[]{:S(2)}) %collective-permute-start.58) | collective-permute-done | bytes 1441824 | tf_op jit(solution)/shard_map/ppermute | solution.py:504
  (633 shorter events, 480.6 us)
Async XLA Ops:
  7.2 122.3 %all-gather.10.cloned.1.call-start = ((), (), s32[]{:S(2)}) async-start(), calls=%async_computation.8 | async-start | bytes 17301504 | tf_op jit(solution)/shard_map/all_gather | solution.py:433
  9.5 202.0 %all-gather.12.cloned.1.call-start = ((), (), s32[]{:S(2)}) async-start(), calls=%async_computation.17 | async-start | bytes 12976128 | tf_op jit(solution)/shard_map/all_gather | solution.py:439
  10.3 270.9 %all-gather.14.cloned.1.call-start = ((), (), s32[]{:S(2)}) async-start(), calls=%async_computation.18 | async-start | bytes 12976128 | tf_op jit(solution)/shard_map/all_gather | solution.py:440
  11.0 339.6 %all-gather.16.cloned.1.call-start = ((), (), s32[]{:S(2)}) async-start(), calls=%async_computation.19 | async-start | bytes 12976128 | tf_op jit(solution)/shard_map/all_gather | solution.py:441
  11.6 950.0 %reduce-scatter.15.cloned.1.call-start = ((), (), s32[]{:S(2)}) async-start(), calls=%async_computation.12 | async-start | bytes 7208960 | tf_op jit(solution)/shard_map/reduce_scatter | solution.py:494
  131.8 89.7 %collective-permute-start.1 = (bf16[256,1024]{1,0:T(8,128)(2,1)S(1)}, bf16[256,1024]{1,0:T(8,128)(2,1)S(1)}, u32[]{:S(2)}, u32[]{:S(2)}) collective-permute-start(bf16[256,1024]{1,0:T(8,128)(2,1)S(1)} %fusion.50.k0), channel_id=1, source_target_pairs={{0,2},{2,0},{1,3},{3,1},{4,6},{6,4},{5,7},{7,5},{8,10},{10,8},{9,1... | collective-permute-start | bytes 1572872 | tf_op jit(solution)/shard_map/ppermute | solution.py:56
  136.5 85.2 %collective-permute-start.4 = (bf16[256,1024]{1,0:T(8,128)(2,1)}, bf16[256,1024]{1,0:T(8,128)(2,1)}, u32[]{:S(2)}, u32[]{:S(2)}) collective-permute-start(bf16[256,1024]{1,0:T(8,128)(2,1)} %fusion.49.v0), channel_id=1, source_target_pairs={{0,2},{2,0},{1,3},{3,1},{4,6},{6,4},{5,7},{7,5},{8,10},{10,8},{9,1... | collective-permute-start | bytes 1572872 | tf_op jit(solution)/shard_map/ppermute | solution.py:56
  221.0 73.1 %collective-permute-start = (bf16[256,1024]{1,0:T(8,128)(2,1)S(1)}, bf16[256,1024]{1,0:T(8,128)(2,1)}, u32[]{:S(2)}, u32[]{:S(2)}) collective-permute-start(bf16[256,1024]{1,0:T(8,128)(2,1)S(1)} %fusion.50.k0), channel_id=1, source_target_pairs={{0,1},{1,0},{2,3},{3,2},{4,5},{5,4},{6,7},{7,6},{8,9},{9,8},{10,11... | collective-permute-start | bytes 1572872 | tf_op jit(solution)/shard_map/ppermute | solution.py:56
  221.2 72.9 %collective-permute-start.3 = (bf16[256,1024]{1,0:T(8,128)(2,1)}, bf16[256,1024]{1,0:T(8,128)(2,1)}, u32[]{:S(2)}, u32[]{:S(2)}) collective-permute-start(bf16[256,1024]{1,0:T(8,128)(2,1)} %fusion.49.v0), channel_id=1, source_target_pairs={{0,1},{1,0},{2,3},{3,2},{4,5},{5,4},{6,7},{7,6},{8,9},{9,8},{10,11... | collective-permute-start | bytes 1572872 | tf_op jit(solution)/shard_map/ppermute | solution.py:56
  560.1 403.9 %reduce-scatter.13.cloned.1.call-start = ((), (), s32[]{:S(2)}) async-start(), calls=%async_computation.11 | async-start | bytes 7208960 | tf_op jit(solution)/shard_map/reduce_scatter | solution.py:494
  731.7 297.6 %reduce-scatter.11.cloned.1.call-start = ((), (), s32[]{:S(2)}) async-start(), calls=%async_computation.10 | async-start | bytes 8912896 | tf_op jit(solution)/shard_map/reduce_scatter | solution.py:498
  741.4 292.1 %reduce-scatter.9.cloned.1.call-start = ((), (), s32[]{:S(2)}) async-start(), calls=%async_computation.9 | async-start | bytes 8912896 | tf_op jit(solution)/shard_map/reduce_scatter | solution.py:498
  866.6 197.2 %reduce-scatter.19.cloned.1.call-start = ((), (), s32[]{:S(2)}) async-start(), calls=%async_computation.14 | async-start | bytes 7208960 | tf_op jit(solution)/shard_map/reduce_scatter | solution.py:495
  877.1 244.2 %reduce-scatter.17.cloned.1.call-start = ((), (), s32[]{:S(2)}) async-start(), calls=%async_computation.13 | async-start | bytes 7208960 | tf_op jit(solution)/shard_map/reduce_scatter | solution.py:495
  886.6 292.1 %reduce-scatter.23.cloned.1.call-start = ((), (), s32[]{:S(2)}) async-start(), calls=%async_computation.16 | async-start | bytes 7208960 | tf_op jit(solution)/shard_map/reduce_scatter | solution.py:496
  896.9 339.2 %reduce-scatter.21.cloned.1.call-start = ((), (), s32[]{:S(2)}) async-start(), calls=%async_computation.15 | async-start | bytes 7208960 | tf_op jit(solution)/shard_map/reduce_scatter | solution.py:496
  907.2 366.7 %all-gather.18.cloned.1.call-start = ((), (), s32[]{:S(2)}) async-start(), calls=%async_computation.20 | async-start | bytes 2621440 | tf_op jit(solution)/shard_map/all_gather | solution.py:513
  935.8 99.1 %collective-permute-start.51 = (bf16[256,1024]{1,0:T(8,128)(2,1)}, bf16[256,1024]{1,0:T(8,128)(2,1)}, u32[]{:S(2)}, u32[]{:S(2)}) collective-permute-start(bf16[256,1024]{1,0:T(8,128)(2,1)} %copy-done.4), channel_id=1, source_target_pairs={{0,16},{1,17},{2,18},{3,19},{4,20},{5,21},{6,22},{7,23},{8,24},{9,... | collective-permute-start | bytes 1572872 | tf_op jit(solution)/shard_map/ppermute | solution.py:531
  961.6 221.6 %collective-permute-start.55 = (bf16[256,2816]{1,0:T(8,128)(2,1)}, bf16[256,2816]{1,0:T(8,128)(2,1)}, u32[]{:S(2)}, u32[]{:S(2)}) collective-permute-start(bf16[256,2816]{1,0:T(8,128)(2,1)} %reduce-scatter.15.cloned.1.call-done), channel_id=1, source_target_pairs={{0,16},{1,17},{2,18},{3,19},{4,20},{5,21},{6,22},{7,23},{8,24},{9,... | collective-permute-start | bytes 4325384 | tf_op jit(solution)/shard_map/ppermute | solution.py:505
  964.0 273.8 %collective-permute-start.54 = (bf16[256,2816]{1,0:T(8,128)(2,1)}, bf16[256,2816]{1,0:T(8,128)(2,1)}, u32[]{:S(2)}, u32[]{:S(2)}) collective-permute-start(bf16[256,2816]{1,0:T(8,128)(2,1)} %reduce-scatter.13.cloned.1.call-done), channel_id=1, source_target_pairs={{16,0},{17,1},{18,2},{19,3},{20,4},{21,5},{22,6},{23,7},{24,8},{25... | collective-permute-start | bytes 4325384 | tf_op jit(solution)/shard_map/ppermute | solution.py:504
  1033.5 87.8 %collective-permute-start.52 = (bf16[256,1024]{1,0:T(8,128)(2,1)}, bf16[256,1024]{1,0:T(8,128)(2,1)S(1)}, u32[]{:S(2)}, u32[]{:S(2)}) collective-permute-start(bf16[256,1024]{1,0:T(8,128)(2,1)} %bitcast.388), channel_id=1, source_target_pairs={{16,0},{17,1},{18,2},{19,3},{20,4},{21,5},{22,6},{23,7},{24,8},{25... | collective-permute-start | bytes 1572872 | tf_op jit(solution)/shard_map/ppermute | solution.py:504
  1034.9 90.1 %collective-permute-start.50 = (bf16[256,1024]{1,0:T(8,128)(2,1)S(1)}, bf16[256,1024]{1,0:T(8,128)(2,1)S(1)}, u32[]{:S(2)}, u32[]{:S(2)}) collective-permute-start(bf16[256,1024]{1,0:T(8,128)(2,1)S(1)} %get-tuple-element.124), channel_id=1, source_target_pairs={{16,0},{17,1},{18,2},{19,3},{20,4},{21,5},{22,6},{23,7},{24,8},{25... | collective-permute-start | bytes 1572872 | tf_op jit(solution)/shard_map/ppermute | solution.py:532
  1063.8 178.0 %collective-permute-start.57 = (bf16[256,2816]{1,0:T(8,128)(2,1)}, bf16[256,2816]{1,0:T(8,128)(2,1)}, u32[]{:S(2)}, u32[]{:S(2)}) collective-permute-start(bf16[256,2816]{1,0:T(8,128)(2,1)} %reduce-scatter.19.cloned.1.call-done), channel_id=1, source_target_pairs={{0,16},{1,17},{2,18},{3,19},{4,20},{5,21},{6,22},{7,23},{8,24},{9,... | collective-permute-start | bytes 4325384 | tf_op jit(solution)/shard_map/ppermute | solution.py:505
  1121.3 120.5 %collective-permute-start.56 = (bf16[256,2816]{1,0:T(8,128)(2,1)}, bf16[256,2816]{1,0:T(8,128)(2,1)}, u32[]{:S(2)}, u32[]{:S(2)}) collective-permute-start(bf16[256,2816]{1,0:T(8,128)(2,1)} %reduce-scatter.17.cloned.1.call-done), channel_id=1, source_target_pairs={{16,0},{17,1},{18,2},{19,3},{20,4},{21,5},{22,6},{23,7},{24,8},{25... | collective-permute-start | bytes 4325384 | tf_op jit(solution)/shard_map/ppermute | solution.py:504
  (187 other events, 5346.5 us)
Sparse Core Ops, SparseCore 0:
  11.6 117.8 all-gather.9
  131.3 80.1 all-gather.11
  213.4 67.6 all-gather.13
  282.9 67.6 all-gather.15
  560.2 53.4 reduce-scatter.14
  731.8 52.5 reduce-scatter.12
  788.5 109.0 reduce-scatter.10
  901.7 104.8 reduce-scatter.8
  1009.1 54.6 reduce-scatter.18
  1066.4 54.8 reduce-scatter.16
  1123.8 54.8 reduce-scatter.22
  1181.3 54.8 reduce-scatter.20
  1238.3 22.5 all-gather.17

commit v2 on v1

v2 whole, which is shorter than its diff:
```python
import functools
import math

import jax
import jax.numpy as jnp
from jax import lax
from jax.experimental import pallas as pl
from jax.experimental.pallas import tpu as pltpu
from jax.sharding import Mesh
from jax.sharding import PartitionSpec as P

HEADS = 16
HEAD_DIM = 64
EPSILON = 1e-06
ROOT_SIZE = math.sqrt(HEAD_DIM)

SECTION = "section"
EXPERT = "expert"
OUTER = "outer"
INNER = "inner"
REPLICA = (OUTER, INNER)

BF16 = jnp.bfloat16
F32 = jnp.float32
ROWS = 128


def matmul(left, right):
    return jnp.dot(left, right, preferred_element_type=F32)


def dot_nt(left, right):
    return lax.dot_general(left, right, (((1,), (1,)), ((), ())), preferred_element_type=F32)


def dot_tn(left, right):
    return lax.dot_general(left, right, (((0,), (0,)), ((), ())), preferred_element_type=F32)


def rms_scale(values, gain):
    return values * lax.rsqrt(jnp.mean(values * values, axis=-1, keepdims=True) + EPSILON) * gain


def softmax_rows(scores):
    row_top = jnp.max(scores, axis=-1, keepdims=True)
    expos = jnp.exp(scores - row_top)
    return expos / jnp.sum(expos, axis=-1, keepdims=True)


def gated_gelu(gate_part, up_part):
    return jax.nn.gelu(gate_part, approximate=True) * up_part


def shift_to(value, axis, steps):
    count = lax.axis_size(axis)
    return lax.ppermute(value, axis, [(source, (source + steps) % count) for source in range(count)])


def bias_rows(window, half, queries):
    width = queries + ROWS
    start = ROWS * (1 - half)
    part = jnp.broadcast_to(window[:, start : start + width], (ROWS, width))
    return pltpu.roll(part, width - ROWS, axis=1, stride=1, stride_axis=0)[:, :queries]


def attention_forward_kernel(q_ref, k0, k1, k2, k3, v0, v1, v2, v3, w_ref, o_ref, x_ref, l_ref, s_ref, p_ref):
    queries = q_ref[...]
    count = queries.shape[0]
    lanes = lax.broadcasted_iota(jnp.int32, queries.shape, 1)
    ks, vs = (k0, k1, k2, k3), (v0, v1, v2, v3)
    outs = []
    for head in range(2):
        own = (lanes < HEAD_DIM) if head == 0 else (lanes >= HEAD_DIM)
        q_head = jnp.where(own, queries, jnp.zeros_like(queries)) * jnp.asarray(1.0 / ROOT_SIZE, BF16)
        top = None
        for chunk in range(8):
            block, half = divmod(chunk, 2)
            rows = slice(half * ROWS, (half + 1) * ROWS)
            score = dot_nt(ks[block][rows, :], q_head)
            score = score + bias_rows(w_ref[head, block : block + 1, :], half, count)
            s_ref[chunk * ROWS : (chunk + 1) * ROWS, :] = score
            chunk_top = jnp.max(score, axis=0, keepdims=True)
            top = chunk_top if top is None else jnp.maximum(top, chunk_top)
        total = None
        for chunk in range(8):
            rows = slice(chunk * ROWS, (chunk + 1) * ROWS)
            expo = jnp.exp(s_ref[rows, :] - top)
            p_ref[rows, :] = expo.astype(BF16)
            part = jnp.sum(expo, axis=0, keepdims=True)
            total = part if total is None else total + part
        mixed = None
        for block in range(4):
            part = dot_tn(vs[block][...], p_ref[block * count : (block + 1) * count, :])
            mixed = part if mixed is None else mixed + part
        outs.append(mixed[head * HEAD_DIM : (head + 1) * HEAD_DIM, :] / total)
        l_ref[0, head : head + 1, :] = top + jnp.log(total)
    mixed_rows = jnp.concatenate(outs, axis=0).T
    o_ref[...] = mixed_rows.astype(BF16)
    x_ref[...] = mixed_rows


def attention_forward(queries, pairs_kv, windows):
    rows, width = queries.shape
    pairs = HEADS // 2
    pair = 2 * HEAD_DIM
    chunk_spec = pl.BlockSpec((rows, pair), lambda g: (0, g))
    value_spec = pl.BlockSpec((rows, pair), lambda g: (0, g + HEADS // 2))
    return pl.pallas_call(
        attention_forward_kernel,
        grid=(pairs,),
        in_specs=[chunk_spec] * 5
        + [value_spec] * 4
        + [pl.BlockSpec((2,) + windows.shape[1:], lambda g: (g, 0, 0))],
        out_specs=[chunk_spec, chunk_spec, pl.BlockSpec((1, 2, rows), lambda g: (g, 0, 0))],
        out_shape=[
            jax.ShapeDtypeStruct((rows, width), BF16),
            jax.ShapeDtypeStruct((rows, width), F32),
            jax.ShapeDtypeStruct((pairs, 2, rows), F32),
        ],
        scratch_shapes=[pltpu.VMEM((4 * rows, rows), F32), pltpu.VMEM((4 * rows, rows), BF16)],
        cost_estimate=pl.CostEstimate(
            flops=16 * rows * rows * width, bytes_accessed=20 * rows * width, transcendentals=4 * rows * rows * HEADS
        ),
        name="attention_forward",
    )(queries, *pairs_kv, *pairs_kv, windows)


def attention_backward_kernel(
    q_ref, g_ref, o_ref, l_ref, k0, k1, v0, v1, w_ref, *rest, given
):
    given_ref, rest = (rest[0], rest[1:]) if given else (None, rest)
    dq_ref, dkv0, dkv1, dw_ref, ds_ref, pb_ref, w8_ref = rest
    queries = q_ref[...]
    grads = g_ref[...]
    count = queries.shape[0]
    lanes = lax.broadcasted_iota(jnp.int32, queries.shape, 1)
    ks, vs, dkvs = (k0, k1), (v0, v1), (dkv0, dkv1)
    products = (grads.astype(F32) * o_ref[...]).T
    key_sums, value_sums, query_parts = [None] * 2, [None] * 2, []
    for head in range(2):
        own = (lanes < HEAD_DIM) if head == 0 else (lanes >= HEAD_DIM)
        place_head = slice(head * HEAD_DIM, (head + 1) * HEAD_DIM)
        q_head = jnp.where(own, queries, jnp.zeros_like(queries)) * jnp.asarray(1.0 / ROOT_SIZE, BF16)
        g_head = jnp.where(own, grads, jnp.zeros_like(grads))
        level = l_ref[0, head : head + 1, :]
        row_dot = jnp.sum(products[place_head, :], axis=0, keepdims=True)
        for chunk in range(4):
            block, half = divmod(chunk, 2)
            rows = slice(half * ROWS, (half + 1) * ROWS)
            place = slice(chunk * ROWS, (chunk + 1) * ROWS)
            score = dot_nt(ks[block][rows, :], q_head)
            score = score + bias_rows(w_ref[head, block : block + 1, :], half, count)
            attention = jnp.exp(score - level)
            pb_ref[place, :] = attention.astype(BF16)
            grad_attention = dot_nt(vs[block][rows, :], g_head)
            grad_score = (attention * (grad_attention - row_dot)).astype(BF16)
            ds_ref[place, :] = grad_score
            sheared = jnp.concatenate([grad_score.astype(F32), jnp.zeros((ROWS, ROWS), F32)], axis=1)
            live = ROWS
            while live > 8:
                live = live // 2
                sheared = pltpu.roll(sheared[:live, :], live, axis=1) + sheared[live:, :]
            start = ROWS * (1 - half)
            if half == 0:
                w8_ref[block, :, 0:ROWS] = jnp.zeros((8, ROWS), F32)
                w8_ref[block, :, start : start + count + ROWS] = sheared
            else:
                w8_ref[block, :, start : start + count + ROWS] += sheared
        query_part = None
        for block in range(2):
            place = slice(block * count, (block + 1) * count)
            part = dot_tn(ks[block][...], ds_ref[place, :])
            query_part = part if query_part is None else query_part + part
            key_part = matmul(ds_ref[place, :], q_head)
            value_part = matmul(pb_ref[place, :], g_head)
            if head == 0:
                key_sums[block], value_sums[block] = key_part, value_part
            else:
                dkvs[block][0] = (key_sums[block] + key_part).astype(dkvs[block].dtype)
                dkvs[block][1] = (value_sums[block] + value_part).astype(dkvs[block].dtype)
        query_parts.append(query_part[place_head, :])
        for block in range(2):
            folded = pltpu.roll(w8_ref[block], 1, axis=1)
            rows8 = lax.broadcasted_iota(jnp.int32, folded.shape, 0)
            for bit in (1, 2, 4):
                folded = jnp.where(jnp.bitwise_and(rows8, bit) == 0, pltpu.roll(folded, bit, axis=1), folded)
            dw_ref[head, block : block + 1, :] = jnp.sum(folded, axis=0, keepdims=True)
    grad_queries = jnp.concatenate(query_parts, axis=0).T * (1.0 / ROOT_SIZE)
    if given:
        grad_queries = grad_queries + given_ref[...]
    dq_ref[...] = grad_queries.astype(dq_ref.dtype)


def attention_backward(queries, grads, attended, levels, pairs_kv, windows, given=None):
    rows, width = queries.shape
    pairs = HEADS // 2
    pair = 2 * HEAD_DIM
    chunk_spec = pl.BlockSpec((rows, pair), lambda g: (0, g))
    value_spec = pl.BlockSpec((rows, pair), lambda g: (0, g + HEADS // 2))
    window_spec = pl.BlockSpec((2,) + windows.shape[1:], lambda g: (g, 0, 0))
    span = windows.shape[-1]
    extra = [] if given is None else [given]
    return pl.pallas_call(
        functools.partial(attention_backward_kernel, given=given is not None),
        grid=(pairs,),
        in_specs=[chunk_spec] * 3
        + [pl.BlockSpec((1, 2, rows), lambda g: (g, 0, 0))]
        + [chunk_spec] * 2
        + [value_spec] * 2
        + [window_spec]
        + [chunk_spec] * len(extra),
        out_specs=[chunk_spec]
        + [pl.BlockSpec((2, rows, pair), lambda g: (0, 0, g))] * 2
        + [pl.BlockSpec((2, 2, span), lambda g: (g, 0, 0))],
        out_shape=[
            jax.ShapeDtypeStruct((rows, width), F32 if given is None else BF16),
            jax.ShapeDtypeStruct((2, rows, width), F32),
            jax.ShapeDtypeStruct((2, rows, width), BF16),
            jax.ShapeDtypeStruct((HEADS, 2, span), F32),
        ],
        scratch_shapes=[
            pltpu.VMEM((2 * rows, rows), BF16),
            pltpu.VMEM((2 * rows, rows), BF16),
            pltpu.VMEM((2, 8, span), F32),
        ],
        cost_estimate=pl.CostEstimate(
            flops=20 * rows * rows * width, bytes_accessed=36 * rows * width, transcendentals=2 * rows * rows * HEADS
        ),
        name="attention_backward",
    )(queries, grads, attended, levels, *pairs_kv, *pairs_kv, windows, *extra)


def section_swap(value):
    return lax.ppermute(value, SECTION, [(0, 1), (1, 0)])


def inner_swap(value):
    return shift_to(value, INNER, 1)


def outer_swap(value):
    return shift_to(value, OUTER, 1)


def rms_pull(values, gain, grad):
    scale = lax.rsqrt(jnp.mean(values * values, axis=-1, keepdims=True) + EPSILON)
    weighted = grad * gain
    lean = jnp.mean(weighted * values, axis=-1, keepdims=True)
    grad_values = scale * weighted - values * (scale * scale * scale * lean)
    grad_gain = jnp.sum(grad * values * scale, axis=0)
    return grad_values, grad_gain


def send_slots(rows, direction):
    count = lax.axis_size(EXPERT)
    parts = [rows[0]] + [shift_to(rows[k], EXPERT, direction * k) for k in range(1, count)]
    return jnp.concatenate(parts, axis=0)


def route_tables(route, capacity):
    tokens = route.shape[0]
    count = lax.axis_size(EXPERT)
    ahead = jnp.remainder(route - lax.axis_index(EXPERT) + count, count)
    onehot = (ahead[:, :, None] == jnp.arange(count, dtype=jnp.int32)).astype(F32)
    per_row = jnp.sum(onehot, axis=1)
    earlier = (jnp.arange(tokens)[:, None] > jnp.arange(tokens)[None, :]).astype(BF16)
    before = matmul(earlier, per_row.astype(BF16))
    slot_place = jnp.sum(before[:, None, :] * onehot, axis=2).astype(jnp.int32)
    target = ahead * capacity + slot_place
    slots = jnp.arange(count * capacity, dtype=jnp.int32)
    spots = (target[:, 0:1] == slots) | (target[:, 1:2] == slots)
    owner = jnp.remainder(slots // capacity + lax.axis_index(EXPERT), count)
    members = (owner[:, None] == jnp.arange(count, dtype=jnp.int32)).astype(F32)
    return spots, members


def forward(section_in, tables, weights, windows, started):
    spots, members = tables
    slot_table = spots.astype(BF16)
    slot_count = slot_table.shape[1]
    expert_count = lax.axis_size(EXPERT)
    inputs = section_in.astype(F32)
    width = inputs.shape[1]
    if started is None:
        normed = rms_scale(inputs, weights["gain_first"]).astype(BF16)
        pair_own = matmul(normed, weights["pair"]).astype(BF16)
        pair_outer = outer_swap(pair_own)
    else:
        normed, pair_own, pair_outer = started
    pair_inner = inner_swap(pair_own)
    queries = matmul(normed, weights["query"]).astype(BF16)
    pair_both = inner_swap(pair_outer)
    pairs_kv = (pair_own, pair_inner, pair_outer, pair_both)
    attended, attended_full, levels = attention_forward(queries, pairs_kv, windows)
    middle = inputs + matmul(attended, weights["output"])
    mixed_in = rms_scale(middle, weights["gain_second"]).astype(BF16)
    packed = dot_tn(slot_table, mixed_in).astype(BF16)
    arrived = send_slots(packed.reshape(expert_count, -1, width), 1)
    gates_all = softmax_rows(matmul(mixed_in, weights["router"]))
    spread = lax.dot_general(
        gates_all, members, (((1,), (1,)), ((), ())), precision=lax.Precision.HIGHEST, preferred_element_type=F32
    )
    combine = jnp.where(spots, spread, 0.0)
    combine_high = combine.astype(BF16)
    combine_low = (combine - combine_high.astype(F32)).astype(BF16)
    gate_part = matmul(arrived, weights["gate"])
    up_part = matmul(arrived, weights["up"])
    hidden = gated_gelu(gate_part, up_part).astype(BF16)
    produced = dot_nt(hidden, weights["down"]).astype(BF16)
    returned = send_slots(produced.reshape(expert_count, -1, width), -1)
    mixed_out = matmul(combine_high, returned) + matmul(combine_low, returned)
    result = (middle + mixed_out).astype(BF16)
    stored = (
        inputs, normed, queries, pairs_kv, attended, attended_full, levels, middle, mixed_in, gates_all,
        arrived, gate_part, up_part, hidden, returned, combine_high, combine_low,
    )
    return result, stored


def backward(grad_rows, stored, tables, weights, windows, bucket_rows, offload, waited):
    spots, members = tables
    slot_table = spots.astype(BF16)
    (
        inputs, normed, queries, pairs_kv, attended, attended_full, levels, middle, mixed_in, gates_all,
        arrived, gate_part, up_part, hidden, returned, combine_high, combine_low,
    ) = stored
    expert_count = lax.axis_size(EXPERT)
    width = inputs.shape[1]
    grad_out = grad_rows.astype(F32)
    grad_slots = (dot_tn(combine_high, grad_rows) + dot_tn(combine_low, grad_rows)).astype(BF16)
    if offload:
        grad_slots, arrived = lax.optimization_barrier((grad_slots, arrived))
    received = send_slots(grad_slots.reshape(expert_count, -1, width), 1)
    received, waited[0] = lax.optimization_barrier((received, waited[0]))
    products = jnp.where(spots, dot_nt(grad_rows, returned), 0.0)
    grad_gates = jnp.dot(products, members, precision=lax.Precision.HIGHEST, preferred_element_type=F32)
    grad_logits = gates_all * (grad_gates - jnp.sum(gates_all * grad_gates, axis=-1, keepdims=True))
    grad_logits = grad_logits.astype(BF16)
    term_router = dot_tn(mixed_in, grad_logits)

    def for_inner(left, right):
        return dot_tn(inner_columns(left, 1), right).astype(BF16)

    def from_inner(term):
        return inner_swap(term).reshape(2, -1, term.shape[1])

    def for_outer(left, right, taken):
        return plus(dot_tn(replica_columns(left, 1), right), take(taken, 1 - lax.axis_index(OUTER), 0))

    down_given, received = lax.optimization_barrier((for_inner(received, hidden), received))
    down_inner = from_inner(down_given)
    grad_hidden = matmul(received, weights["down"])
    unused_value, pull_gelu = jax.vjp(gated_gelu, gate_part, up_part)
    grad_gate, grad_up = pull_gelu(grad_hidden)
    grad_gate, grad_up, down_inner = lax.optimization_barrier(
        (grad_gate.astype(BF16), grad_up.astype(BF16), down_inner)
    )
    grad_gate, grad_up, down_given = lax.optimization_barrier(
        (grad_gate, grad_up, for_outer(received, hidden, down_inner))
    )
    down_outer = outer_swap(down_given)
    gate_given, up_given, grad_gate, grad_up = lax.optimization_barrier(
        (for_inner(arrived, grad_gate), for_inner(arrived, grad_up), grad_gate, grad_up)
    )
    gate_inner, up_inner = from_inner(gate_given), from_inner(up_given)
    grad_arrived = (dot_nt(grad_gate, weights["gate"]) + dot_nt(grad_up, weights["up"])).astype(BF16)
    grad_arrived, gate_inner, up_inner = lax.optimization_barrier((grad_arrived, gate_inner, up_inner))
    back_rows = send_slots(grad_arrived.reshape(expert_count, -1, width), -1)
    gate_given = for_outer(arrived, grad_gate, gate_inner)
    up_given = for_outer(arrived, grad_up, up_inner)
    back_rows, gate_given, up_given, down_outer, waited[1] = lax.optimization_barrier(
        (back_rows, gate_given, up_given, down_outer, waited[1])
    )
    gate_outer = outer_swap(gate_given)

    grad_mixed = matmul(slot_table, back_rows) + dot_nt(grad_logits, weights["router"])
    grad_middle, term_second = rms_pull(middle, weights["gain_second"], grad_mixed)
    grad_middle = grad_middle + grad_out
    grad_branch = grad_middle.astype(BF16)
    grad_attended = dot_nt(grad_branch, weights["output"]).astype(BF16)
    term_output = dot_tn(attended, grad_branch).astype(BF16)
    grad_attended, gate_outer, waited[2] = lax.optimization_barrier((grad_attended, gate_outer, waited[2]))
    up_outer = outer_swap(up_given)
    grad_part, outer, both, windows_far = attention_backward(
        queries, grad_attended, attended_full, levels, pairs_kv[2:], windows[:, 2:]
    )
    far_taken = inner_swap(both)
    grad_part, far_taken, up_outer, waited[3] = lax.optimization_barrier((grad_part, far_taken, up_outer, waited[3]))
    passed = plus(outer, far_taken)
    passed, grad_part = lax.optimization_barrier((passed, grad_part))
    outer_sum = outer_swap(passed)
    grad_queries, own, inner, windows_near = attention_backward(
        queries, grad_attended, attended_full, levels, pairs_kv[:2], windows[:, :2], grad_part
    )
    grad_queries, own, inner, outer_sum, waited[4] = lax.optimization_barrier(
        (grad_queries, own, inner, outer_sum, waited[4])
    )
    grad_windows = jnp.concatenate([windows_near, windows_far], axis=1)
    near_sum = own + inner_swap(inner).astype(F32)
    grad_windows = grad_windows.reshape(HEADS, -1)
    term_position = lax.dot_general(
        grad_windows, bucket_rows.astype(F32), (((1,), (1,)), ((), ())),
        precision=lax.Precision.HIGHEST, preferred_element_type=F32,
    )
    grad_normed = dot_nt(grad_queries, weights["query"])
    small_early = (term_router, term_second, term_position)
    if offload:
        term_query = dot_tn(normed, grad_queries).astype(BF16)
        term_output = dot_tn(attended, grad_branch).astype(BF16)
        near_sum, grad_normed, term_query, term_output, small_early = lax.optimization_barrier(
            (near_sum, grad_normed, term_query, term_output, small_early)
        )
    else:
        even = lax.axis_index(INNER) == 0
        lefts, rights = (attended, normed), (grad_branch, grad_queries)
        first_fold = fold_dense(
            (jnp.where(even, *lefts), jnp.where(even, *rights)),
            (jnp.where(even, *lefts[::-1]), jnp.where(even, *rights[::-1])),
        )
        near_sum, grad_normed, first_fold[0], small_early, waited[5] = lax.optimization_barrier(
            (near_sum, grad_normed, first_fold[0], small_early, waited[5])
        )
    grad_pair = (near_sum + outer_sum.astype(F32)).astype(BF16)
    if offload:
        grad_normed = grad_normed + dot_nt(grad_pair[0], weights["key"]) + dot_nt(grad_pair[1], weights["value"])
    else:
        index = lax.axis_index(INNER)
        second_fold = fold_dense((normed, take(grad_pair, index, 0)), (normed, take(grad_pair, 1 - index, 0)))
        second_fold[0], grad_pair = lax.optimization_barrier((second_fold[0], grad_pair))
        grad_normed = grad_normed + dot_nt(grad_pair[0], weights["key"]) + dot_nt(grad_pair[1], weights["value"])
    grad_in, term_first = rms_pull(inputs, weights["gain_first"], grad_normed)
    grad_in = grad_in + grad_middle
    small_terms = (small_early[0], term_first, small_early[1], small_early[2])
    pending = (
        (arrived, grad_gate, gate_inner, gate_outer),
        (arrived, grad_up, up_inner, up_outer),
        (received, hidden, down_inner, down_outer),
    )
    if offload:
        dense_terms = (
            term_output,
            term_query,
            dot_tn(normed, grad_pair[0]).astype(BF16),
            dot_tn(normed, grad_pair[1]).astype(BF16),
        )
    else:
        dense_terms = (first_fold, second_fold)
    return grad_in, dense_terms, small_terms, pending, waited


def finish_expert(pending):
    left, right, taken, last = pending
    return plus(dot_tn(replica_columns(left, 0), right) + take(taken, lax.axis_index(OUTER), 0).astype(F32), last)


def take(blocks, index, axis):
    return lax.dynamic_index_in_dim(blocks, index, axis, keepdims=False)


def plus(left, right):
    return (left.astype(F32) + right.astype(F32)).astype(BF16)


def pick_columns(values, index, size, count):
    parts = [
        lax.dynamic_slice_in_dim(values, start + index * size, size, 1)
        for start in range(0, values.shape[1], size * count)
    ]
    return jnp.concatenate(parts, axis=1)


def inner_columns(values, other):
    return pick_columns(values, jnp.bitwise_xor(lax.axis_index(INNER), other), values.shape[1] // 4, 2)


def replica_columns(values, other):
    width = values.shape[1] // 4
    place = 2 * jnp.bitwise_xor(lax.axis_index(OUTER), other) + lax.axis_index(INNER)
    return lax.dynamic_slice_in_dim(values, place * width, width, 1)


def fold_experts(blocks):
    count, index = lax.axis_size(EXPERT), lax.axis_index(EXPERT)
    total = take(blocks, index, 0).astype(F32)
    for ahead in range(1, count):
        given = take(blocks, jnp.remainder(index + ahead, count), 0)
        total = total + shift_to(given, EXPERT, ahead).astype(F32)
    return total


def fold_dense(own_pair, given_pair):
    given = dot_tn(*given_pair).astype(BF16)
    return [inner_swap(given), own_pair]


def finish_dense(fold):
    taken, (left, right) = fold
    outer_index, even = lax.axis_index(OUTER), lax.axis_index(INNER) == 0
    count = lax.axis_size(EXPERT)
    size = left.shape[1] // (2 * count)
    rows = taken.reshape(count, 2, -1, taken.shape[1])

    def part(index):
        term = dot_tn(pick_columns(left, index, size, 2), right)
        return term.reshape(count, -1, taken.shape[1]) + take(rows, index, 1).astype(F32)

    outer_taken = outer_swap(part(1 - outer_index).astype(BF16))
    total = fold_experts(plus(part(outer_index), outer_taken)).astype(BF16)
    total = plus(total, lax.ppermute(total, SECTION, [(1, 0)]))
    partner = outer_swap(total)
    lower = outer_index == 0
    own = jnp.concatenate([jnp.where(lower, total, partner), jnp.where(lower, partner, total)], axis=0)
    other = inner_swap(own)
    return jnp.where(even, own, other), jnp.where(even, other, own)


def fold_small(flat, source):
    flat = flat + inner_swap(flat)
    flat = flat + outer_swap(flat)
    flat = fold_experts(flat)
    return flat + lax.ppermute(flat, SECTION, [(source, 1 - source)])


def pack_small(router, first, second, position, count):
    parts = [router.reshape(count, -1), first.reshape(count, -1), second.reshape(count, -1), position.reshape(count, -1)]
    flat = jnp.concatenate(parts, axis=1)
    return jnp.pad(flat, ((0, 0), (0, -flat.shape[1] % 1024)))


def unpack_small(flat, rows, experts, heads, buckets):
    sizes = [rows * experts, rows, rows, heads * buckets]
    starts = [sum(sizes[:k]) for k in range(5)]
    pieces = [flat[:, starts[k] : starts[k + 1]] for k in range(4)]
    return pieces[0].reshape(-1, experts), pieces[1].reshape(-1), pieces[2].reshape(-1), pieces[3].reshape(-1, buckets)


def shards(
    inputs,
    cotangent,
    routes,
    bucket_table,
    query_weight,
    key_weight,
    value_weight,
    output_weight,
    router_weight,
    attention_gain,
    mixture_gain,
    position_bias,
    expert_gate,
    expert_up,
    expert_down,
):
    micro_count = inputs.shape[0]
    tok_rows = inputs.shape[2]
    model_width = inputs.shape[3]
    expert_count = lax.axis_size(EXPERT)
    replica_count = lax.axis_size(OUTER) * lax.axis_size(INNER)
    assert micro_count == lax.axis_size(SECTION) == 2 and replica_count == 4
    capacity = max(2, 9 * tok_rows // (4 * expert_count))
    length = tok_rows * replica_count
    buckets = position_bias.shape[2]
    section_index = lax.axis_index(SECTION)
    replica_index = 2 * lax.axis_index(OUTER) + lax.axis_index(INNER)
    first_section = section_index == 0

    own_rows = lax.dynamic_index_in_dim(inputs[:, 0], section_index, 0, keepdims=False)
    own_cotangent = lax.dynamic_index_in_dim(cotangent[:, 0], section_index, 0, keepdims=False)
    layer_routes = routes[0, :, 0]
    route_kept = lax.dynamic_index_in_dim(layer_routes, section_index, 0, keepdims=False)
    route_given = lax.dynamic_index_in_dim(layer_routes, 1 - section_index, 0, keepdims=False)
    route_taken = section_swap(route_given)
    layer_route = (
        jnp.where(first_section, route_kept, route_taken),
        jnp.where(first_section, route_taken, route_kept),
    )

    dense_rows = query_weight.shape[1]
    inner_index = lax.axis_index(INNER)
    expert_index = lax.axis_index(EXPERT)
    half_rows = dense_rows // 2

    def half_piece(*own_parts):
        return jnp.concatenate(
            [lax.dynamic_slice_in_dim(part, inner_index * half_rows, half_rows, 0) for part in own_parts], axis=1
        )

    def from_first(own):
        return jnp.where(first_section, own, lax.ppermute(own, SECTION, [(0, 1)]))

    def half_of(part, index):
        return lax.dynamic_slice_in_dim(part, index * (part.shape[0] // 2), part.shape[0] // 2, 0)

    def ring_gather(piece):
        whole = jnp.zeros((model_width, piece.shape[1]), BF16)
        for step in range(expert_count):
            start = jnp.remainder(expert_index - step + expert_count, expert_count) * dense_rows
            whole = lax.dynamic_update_slice(whole, piece, (start + inner_index * half_rows, 0))
            whole = lax.dynamic_update_slice(whole, inner_swap(piece), (start + (1 - inner_index) * half_rows, 0))
            if step + 1 < expert_count:
                piece = shift_to(piece, EXPERT, 1)
        return whole

    def half_of(part, index):
        return lax.dynamic_slice_in_dim(part, index * (part.shape[0] // 2), part.shape[0] // 2, 0)

    small_own = pack_small(router_weight[0], attention_gain[0], mixture_gain[0], position_bias[0], 1)[0]
    small_taken = section_swap(small_own)
    pair_piece = from_first(half_piece(key_weight[0], value_weight[0]))
    small_piece = jnp.where(
        first_section, jnp.stack([small_own, small_taken]), jnp.stack([small_taken, small_own])
    ).reshape(2, 1, -1)
    small_all = jnp.zeros((2, expert_count, small_piece.shape[2]), BF16)
    for step in range(expert_count):
        source = jnp.remainder(expert_index - step + expert_count, expert_count)
        small_all = lax.dynamic_update_slice(small_all, small_piece, (0, source, 0))
        if step + 1 < expert_count:
            small_piece = shift_to(small_piece, EXPERT, 1)

    second_own, pair_piece = lax.optimization_barrier(
        (half_piece(query_weight[0], output_weight[0]), pair_piece)
    )
    second_half = from_first(second_own)
    wide_own = (expert_gate[0, 0], expert_up[0, 0], expert_down[0, 0].T)
    wide_kept = jnp.concatenate([half_of(part, section_index) for part in wide_own], axis=1)
    wide_sent = jnp.concatenate([half_of(part, 1 - section_index) for part in wide_own], axis=1)
    wide_sent, second_half = lax.optimization_barrier((wide_sent, second_half))
    wide_taken = section_swap(wide_sent)
    first_pair = ring_gather(pair_piece)
    first_pair, small_all = lax.optimization_barrier((first_pair, small_all))
    small_parts = [
        unpack_small(small_all[layer], dense_rows, expert_count, position_bias.shape[1], position_bias.shape[2])
        for layer in range(2)
    ]
    normed = rms_scale(own_rows.astype(F32), small_parts[0][1].astype(F32)).astype(BF16)
    first_own = matmul(normed, first_pair).astype(BF16)
    second_half, first_own, wide_taken = lax.optimization_barrier((second_half, first_own, wide_taken))
    first_outer = outer_swap(first_own)
    second_whole = ring_gather(second_half)
    second_whole, first_outer = lax.optimization_barrier((second_whole, first_outer))
    first_query, first_output = second_whole[:, :model_width], second_whole[:, model_width:]

    eighth = dense_rows // 8

    def by_layer(kept_part, taken_part):
        return jnp.where(first_section, kept_part, taken_part), jnp.where(first_section, taken_part, kept_part)

    dense_axes = (EXPERT, SECTION) + REPLICA

    def eighths(*parts):
        kept_part = jnp.concatenate(
            [lax.dynamic_slice_in_dim(part, (4 * section_index + replica_index) * eighth, eighth, 0) for part in parts],
            axis=1,
        )
        sent_part = jnp.concatenate(
            [lax.dynamic_slice_in_dim(part, (4 * (1 - section_index) + replica_index) * eighth, eighth, 0) for part in parts],
            axis=1,
        )
        return kept_part, sent_part

    hidden_width = expert_gate.shape[3]
    rest_kept, rest_sent = eighths(key_weight[0], value_weight[0], query_weight[0], output_weight[0])
    rest_sent, first_own = lax.optimization_barrier((rest_sent, first_own))
    second_piece = by_layer(rest_kept, section_swap(rest_sent))[1]
    second_piece, first_query, first_own = lax.optimization_barrier((second_piece, first_query, first_own))
    heads_own = position_bias.shape[1]
    wide_pieces = by_layer(wide_kept, wide_taken)
    wide_all = []
    wide_all.append(lax.all_gather(wide_pieces[0], REPLICA + (SECTION,), axis=0, tiled=True))
    second_all = lax.all_gather(second_piece, dense_axes, axis=0, tiled=True)
    wide_all.append(lax.all_gather(wide_pieces[1], REPLICA + (SECTION,), axis=0, tiled=True))
    dense_all = (
        (first_pair, first_query, first_output),
        tuple(second_all[:, a * model_width : z * model_width] for a, z in ((0, 2), (2, 3), (3, 4))),
    )

    reversed_table = jnp.concatenate([jnp.full((1,), -1, jnp.int32), bucket_table[::-1]])
    bucket_onehot = (jnp.arange(buckets, dtype=jnp.int32)[:, None] == reversed_table[None, :]).astype(BF16)
    bucket_rows = jnp.concatenate(
        [
            lax.dynamic_slice(
                bucket_onehot,
                (0, (3 + replica_index - jnp.bitwise_xor(replica_index, ahead)) * tok_rows),
                (buckets, 2 * tok_rows),
            )
            for ahead in range(4)
        ],
        axis=1,
    )

    layers = []
    for layer in range(2):
        router, first, second, position = small_parts[layer]
        weights = dict(
            pair=dense_all[layer][0],
            key=dense_all[layer][0][:, :model_width],
            value=dense_all[layer][0][:, model_width:],
            query=dense_all[layer][1],
            output=dense_all[layer][2],
            router=router,
            gain_first=first.astype(F32),
            gain_second=second.astype(F32),
            gate=wide_all[layer][:, :hidden_width],
            up=wide_all[layer][:, hidden_width : 2 * hidden_width],
            down=wide_all[layer][:, 2 * hidden_width :],
        )
        windows = matmul(position, bucket_rows).reshape(HEADS, 4, 2 * tok_rows)
        layers.append((weights, windows, route_tables(layer_route[layer], capacity)))

    rows, outputs, kept = own_rows, [], []
    for weights, windows, tables in layers:
        rows, stored = forward(rows, tables, weights, windows, (normed, first_own, first_outer) if not kept else None)
        outputs.append(rows)
        kept.append(stored)

    weights, windows, tables = layers[1]
    grad_in_one, dense_terms, small_one, pending, waited = backward(
        own_cotangent, kept[1], tables, weights, windows, bucket_rows, True, [()] * 6
    )
    grads = grad_in_one.astype(BF16)
    small_one = pack_small(*small_one, expert_count).astype(BF16).reshape(1, expert_count, -1, model_width)
    small_one = jnp.pad(small_one, ((0, 3), (0, 0), (0, -small_one.shape[2] % 16), (0, 0)))
    dense = jnp.stack(dense_terms).reshape(4, expert_count, dense_rows, model_width)
    dense = jnp.concatenate([dense, small_one], axis=2).reshape(4 * expert_count, -1, model_width)
    grads, dense = lax.optimization_barrier((grads, dense))
    dense_share = lax.psum_scatter(dense, REPLICA + (EXPERT,), scatter_dimension=0, tiled=False)
    shares_one = [finish_expert(part) for part in pending]
    hops_one = [lax.ppermute(share, SECTION, [(0, 1)]) for share in shares_one]
    grad_from_one = lax.ppermute(grads, SECTION, [(0, 1)])

    weights, windows, tables = layers[0]
    waited = [tuple(shares_one), hops_one[2], grad_from_one, hops_one[0], (), hops_one[1]]
    grad_in_zero, folds_zero, small_zero, pending, waited = backward(
        grads, kept[0], tables, weights, windows, bucket_rows, False, waited
    )
    shares_one, hop_two, grad_from_one, hop_zero, unused, hop_one = waited
    hops_one = (hop_zero, hop_one, hop_two)
    shares_zero = [finish_expert(part) for part in pending]
    hops_zero = [lax.ppermute(share, SECTION, [(1, 0)]) for share in shares_zero]

    final_gate, final_up, final_down = (
        jnp.where(first_section, zero, one).astype(F32) + jnp.where(first_section, zero_hop, one_hop).astype(F32)
        for zero, zero_hop, one, one_hop in zip(shares_zero, hops_zero, shares_one, hops_one)
    )
    dense_share, grad_in_zero = lax.optimization_barrier((dense_share, grad_in_zero))
    dense_share = plus(dense_share, lax.ppermute(dense_share, SECTION, [(0, 1)]))
    dense_one = lax.all_gather(dense_share, REPLICA, axis=0, tiled=False)
    dense_zero = finish_dense(folds_zero[0]) + finish_dense(folds_zero[1])
    final_output, final_query, final_key, final_value = (
        jnp.where(first_section, dense_zero[k], dense_one[k, :dense_rows]).astype(F32) for k in range(4)
    )
    small_zero = fold_small(pack_small(*small_zero, expert_count), 1)
    small_one = dense_one[0, dense_rows:].reshape(-1)[: small_zero.shape[0]].astype(F32)
    final_router, final_first, final_second, final_position = unpack_small(
        jnp.where(first_section, small_zero, small_one).reshape(1, -1), dense_rows, expert_count, heads_own, buckets
    )

    def both_micros(kept_one, taken_one):
        return jnp.where(
            first_section, jnp.stack([kept_one, taken_one]), jnp.stack([taken_one, kept_one])
        )[None, :, None]

    output_taken = section_swap(jnp.where(first_section, outputs[1], outputs[0]))
    section_output = both_micros(jnp.where(first_section, outputs[0], outputs[1]), output_taken)
    grad_from_zero = lax.ppermute(grad_in_zero.astype(BF16), SECTION, [(1, 0)])
    grad_taken = jnp.where(first_section, grad_from_zero, grad_from_one).astype(F32)
    grad_kept = jnp.where(first_section, grad_in_zero, grad_in_one)
    input_gradient = both_micros(grad_kept, grad_taken)
    return (
        section_output,
        input_gradient,
        final_query[None],
        final_key[None],
        final_value[None],
        final_output[None],
        final_router[None],
        final_first[None],
        final_second[None],
        final_position[None],
        final_gate[None, None],
        final_up[None, None],
        final_down.T[None, None],
    )


def solution(mesh):
    sections, experts, replicas = (mesh.shape[name] for name in ("section", "expert", "replica"))
    fine = Mesh(
        mesh.devices.reshape(sections, experts, replicas // 2, 2), (SECTION, EXPERT, OUTER, INNER)
    )
    rep = REPLICA
    in_specs = (
        P(None, "expert", rep, None),
        P(None, "expert", rep, None),
        P("section", None, "expert", rep, None),
        P(),
        P("section", "expert", None),
        P("section", "expert", None),
        P("section", "expert", None),
        P("section", "expert", None),
        P("section", "expert", None),
        P("section", "expert"),
        P("section", "expert"),
        P("section", "expert", None),
        P("section", "expert", rep, None),
        P("section", "expert", rep, None),
        P("section", "expert", None, rep),
    )
    out_specs = (
        P("section", None, "expert", rep, None),
        P("section", None, "expert", rep, None),
        P("section", "expert", None),
        P("section", "expert", None),
        P("section", "expert", None),
        P("section", "expert", None),
        P("section", "expert", None),
        P("section", "expert"),
        P("section", "expert"),
        P("section", "expert", None),
        P("section", "expert", rep, None),
        P("section", "expert", rep, None),
        P("section", "expert", None, rep),
    )
    return jax.shard_map(shards, mesh=fine, in_specs=in_specs, out_specs=out_specs, check_vma=False)
```

time: 1290 us -> 1130 us (0.88)
  waiting for transfers between devices: 644 us -> 474 us
  blocking collectives: 94.6 us -> 0 us
  starting transfers between devices: 103 us -> 177 us
  matrix products: 205 us -> 234 us
  other arithmetic: 40.6 us -> 62.2 us
    all_gather x5 -> x4, waiting for transfers between devices: 247 us -> 27.1 us  [the longest x1 26.7 us: shards(): second_all = lax.all_gather(second_piece, dense_axes, axis=0, tiled=True)]
    ppermute x48 -> x84, waiting for transfers between devices: 175 us -> 375 us  [shift_to(): lax.ppermute(value, axis, [(source, (source + steps) % count) for source...]
    reduce_scatter x6 -> x0, waiting for transfers between devices: 184 us -> none  [the longest x2 105 us: shards(): lax.psum_scatter(expert_terms[2], REPLICA, scatter_dimension=1, tiled=True)]
    psum x1 -> x0, blocking collectives: 64 us -> none  [shards(): lax.psum(jnp.stack([results[0][1], results[1][1]]).astype(BF16), (SECTION...]
    ppermute x48 -> x84, starting transfers between devices: 70.6 us -> 131 us  [shift_to(): lax.ppermute(value, axis, [(source, (source + steps) % count) for source...]
    all_gather x1 -> x0, blocking collectives: 30.6 us -> none  [shards(): lax.all_gather(small_piece[0].reshape(-1, 128), (SECTION, EXPERT), axis=0...]
    slice x22 -> x3, local copies, waits for them, and re-layouts: 34.4 us -> 4.88 us  [the longest x1 3.47 us: shards(): second_whole[:, :model_width]]
    dot_general x22 -> x36, matrix products: 62.5 us -> 89.9 us  [dot_tn(): lax.dot_general(left, right, (((0,), (0,)), ((), ())), preferred_element_...]
  transfers between devices with their start and end apart: 73 -> 108, of which waited for: 29 -> 43; matrix products, arithmetic and copies ran while one was open for 21% -> 25% of each run, Pallas kernels for 7% -> 8%
where the time goes in v2:
time: 1130 us; the launch traced here: 1120 us
  waiting for transfers between devices  474 us (42%)
  matrix products  234 us (21%)
  starting transfers between devices  177 us (16%)
  Pallas kernels  94.3 us (8%)
  local copies, waits for them, and re-layouts  66.3 us (6%)
  other arithmetic  62.2 us (6%)
  between operations  17.7 us (2%)
    ppermute x84, waiting for transfers between devices, shift_to(): lax.ppermute(value, axis, [(source, (source + steps) % count) for source...  375 us
    ppermute x84, starting transfers between devices, shift_to(): lax.ppermute(value, axis, [(source, (source + steps) % count) for source...  131 us
    dot_general x36, matrix products, dot_tn(): lax.dot_general(left, right, (((0,), (0,)), ((), ())), preferred_element_...  89.9 us
    dot_general x24, matrix products, matmul(): return jnp.dot(left, right, preferred_element_type=F32)  86.5 us
    pallas_call x4, Pallas kernels, attention_backward(): pl.pallas_call(functools.partial(attention_backward_kernel, given=given i...  63.6 us
    dot_general x18, matrix products, dot_nt(): lax.dot_general(left, right, (((1,), (1,)), ((), ())), preferred_element_...  54.3 us
    ppermute x5, waiting for transfers between devices, section_swap(): return lax.ppermute(value, SECTION, [(0, 1), (1, 0)])  32.8 us
    pallas_call x2, Pallas kernels, attention_forward(): pl.pallas_call(attention_forward_kernel, grid=(pairs,), in_specs=[chunk_s...  30.8 us
  transfers between devices with their start and end apart: 108, of which 43 were waited for; matrix products, arithmetic and copies ran while one was open for 25% of the time, Pallas kernels for 8%

profile of v2, /device:TPU:0, one launch (start us, length us, event | category | flops | bytes accessed | tf_op | source)
XLA Modules:
  0.0 1124.9 jit_solution(17014000367660891567)
XLA Ops:
  67.8 14.0 %collective-permute-done.6 = bf16[128,2048]{1,0:T(8,128)(2,1)S(1)} collective-permute-done((bf16[128,2048]{1,0:T(8,128)(2,1)S(1)}, bf16[128,2048]{1,0:T(8,128)(2,1)S(1)}, u32[]{:S(2)}, u32[]{:S(2)}) %collective-permute-start.6) | collective-permute-done | bytes 524320 | tf_op jit(solution)/shard_map/ppermute | solution.py:56
  85.9 18.0 %collective-permute-done.13 = bf16[128,8448]{1,0:T(8,128)(2,1)S(1)} collective-permute-done((bf16[128,8448]{1,0:T(8,128)(2,1)S(1)}, bf16[128,8448]{1,0:T(8,128)(2,1)S(1)}, u32[]{:S(2)}, u32[]{:S(2)}) %collective-permute-start.13) | collective-permute-done | bytes 2162720 | tf_op jit(solution)/shard_map/ppermute | solution.py:234
  124.9 15.5 %collective-permute-done.18 = bf16[128,2048]{1,0:T(8,128)(2,1)} collective-permute-done((bf16[128,2048]{1,0:T(8,128)(2,1)S(1)}, bf16[128,2048]{1,0:T(8,128)(2,1)}, u32[]{:S(2)}, u32[]{:S(2)}) %collective-permute-start.18) | collective-permute-done | bytes 524320 | tf_op jit(solution)/shard_map/ppermute | solution.py:56
  175.9 15.4 %attention_forward.2 = (bf16[256,1024]{1,0:T(8,128)(2,1)}, f32[256,1024]{1,0:T(8,128)}, f32[8,2,256]{2,1,0:T(2,128)}) custom-call(bf16[256,1024]{1,0:T(8,128)(2,1)} %convolution_convert_fusion.15.q_ref, bf16[256,2048]{1,0:T(8,128)(2,1)} %copy-done.12, bf16[256,2048]{1,0:T(8,128)(2,1)} %copy-done.14, bf16[256,2048]{1,0:T(8,128)(2,1)} %copy-done.13, ...), custom_call_target="tpu_custom_call" | custom-call | flops 1073741824 | bytes 5242880 | tf_op jit(solution)/shard_map/attention_forward/pallas_call | solution.py:108
  256.9 26.6 %collective-permute-done.30 = bf16[144,1024]{1,0:T(8,128)(2,1)S(1)} collective-permute-done((bf16[144,1024]{1,0:T(8,128)(2,1)S(1)}, bf16[144,1024]{1,0:T(8,128)(2,1)S(1)}, u32[]{:S(2)}, u32[]{:S(2)}) %collective-permute-start.30) | collective-permute-done | bytes 294944 | tf_op jit(solution)/shard_map/ppermute | solution.py:56
  286.4 26.7 %all-gather.8.cloned.1.call-done = bf16[1024,4096]{1,0:T(8,128)(2,1)} async-done(((bf16[32,4096]{1,0:T(8,128)(2,1)}), bf16[1024,4096]{1,0:T(8,128)(2,1)}) %all-gather.8.cloned.1.call-update) | async-done | bytes 8388624 | tf_op jit(solution)/shard_map/all_gather | solution.py:670
  319.3 41.7 %collective-permute-done.33.k2.v2.k0.v0 = bf16[256,2048]{1,0:T(8,128)(2,1)} collective-permute-done((bf16[256,2048]{1,0:T(8,128)(2,1)}, bf16[256,2048]{1,0:T(8,128)(2,1)}, u32[]{:S(2)}, u32[]{:S(2)}) %collective-permute-start.33) | collective-permute-done | bytes 1048608 | tf_op jit(solution)/shard_map/ppermute | solution.py:56
  366.7 15.4 %attention_forward.3 = (bf16[256,1024]{1,0:T(8,128)(2,1)}, f32[256,1024]{1,0:T(8,128)}, f32[8,2,256]{2,1,0:T(2,128)}) custom-call(bf16[256,1024]{1,0:T(8,128)(2,1)} %fusion.114.q_ref, bf16[256,2048]{1,0:T(8,128)(2,1)} %fusion.52.k0.v0, bf16[256,2048]{1,0:T(8,128)(2,1)} %collective-permute-done.32.k1.v1, ...), custom_call_target="tpu_custom_call" | custom-call | flops 1073741824 | bytes 5242880 | tf_op jit(solution)/shard_map/attention_forward/pallas_call | solution.py:108
  397.4 12.2 %collective-permute-done.36 = bf16[144,1024]{1,0:T(8,128)(2,1)S(1)} collective-permute-done((bf16[144,1024]{1,0:T(8,128)(2,1)S(1)}, bf16[144,1024]{1,0:T(8,128)(2,1)S(1)}, u32[]{:S(2)}, u32[]{:S(2)}) %collective-permute-start.36) | collective-permute-done | bytes 294944 | tf_op jit(solution)/shard_map/ppermute | solution.py:56
  447.3 13.4 %multiply_convert_fusion.1 = (bf16[576,2816]{1,0:T(8,128)(2,1)S(1)}, bf16[576,2816]{1,0:T(8,128)(2,1)S(1)}) fusion(f32[576,2816]{1,0:T(8,128)} %copy-done.192, f32[576,2816]{1,0:T(8,128)} %get-tuple-element.451, bf16[576,1024]{1,0:T(8,128)(2,1)} %copy-done.53, bf16[1024,8448]{1,0:T(8,128)(2,1)} %all-gather.10.cloned.1.call-done), kind=kOutput, calls=%fused_computation.22 | convolution fusion | flops 3360817152 | bytes 26411008 | tf_op jit(solution)/shard_map/dot_general | solution.py:29
  493.6 18.0 %collective-permute-done.39 = bf16[144,1024]{1,0:T(8,128)(2,1)S(1)} collective-permute-done((bf16[144,1024]{1,0:T(8,128)(2,1)S(1)}, bf16[144,1024]{1,0:T(8,128)(2,1)S(1)}, u32[]{:S(2)}, u32[]{:S(2)}) %collective-permute-start.39) | collective-permute-done | bytes 294944 | tf_op jit(solution)/shard_map/ppermute | solution.py:56
  536.2 19.4 %collective-permute-done.49 = bf16[144,1024]{1,0:T(8,128)(2,1)S(1)} collective-permute-done((bf16[144,1024]{1,0:T(8,128)(2,1)S(1)}, bf16[144,1024]{1,0:T(8,128)(2,1)S(1)}, u32[]{:S(2)}, u32[]{:S(2)}) %collective-permute-start.49) | collective-permute-done | bytes 294944 | tf_op jit(solution)/shard_map/ppermute | solution.py:56
  564.6 25.8 %collective-permute-done.52 = bf16[256,2816]{1,0:T(8,128)(2,1)} collective-permute-done((bf16[256,2816]{1,0:T(8,128)(2,1)S(1)}, bf16[256,2816]{1,0:T(8,128)(2,1)}, u32[]{:S(2)}, u32[]{:S(2)}) %collective-permute-start.52) | collective-permute-done | bytes 1441824 | tf_op jit(solution)/shard_map/ppermute | solution.py:56
  590.4 15.6 %attention_backward.4 = (f32[256,1024]{1,0:T(8,128)}, f32[2,256,1024]{2,1,0:T(8,128)}, bf16[2,256,1024]{2,1,0:T(8,128)(2,1)}, f32[16,2,512]{2,1,0:T(2,128)}) custom-call(bf16[256,1024]{1,0:T(8,128)(2,1)} %fusion.114.q_ref, bf16[256,1024]{1,0:T(8,128)(2,1)} %fusion.117.g_ref, f32[256,1024]{1,0:T(8,128)} %get-tuple-element.178.o_ref, ...), custom_call_target="tpu_custom_call" | custom-call | flops 1342177280 | bytes 9437184 | tf_op jit(solution)/shard_map/attention_backward/pallas_call | solution.py:203
  606.1 12.9 %collective-permute-done.54 = bf16[256,2816]{1,0:T(8,128)(2,1)} collective-permute-done((bf16[256,2816]{1,0:T(8,128)(2,1)}, bf16[256,2816]{1,0:T(8,128)(2,1)}, u32[]{:S(2)}, u32[]{:S(2)}) %collective-permute-start.54) | collective-permute-done | bytes 1441824 | tf_op jit(solution)/shard_map/ppermute | solution.py:56
  629.4 16.0 %attention_backward.5 = (bf16[256,1024]{1,0:T(8,128)(2,1)}, f32[2,256,1024]{2,1,0:T(8,128)}, bf16[2,256,1024]{2,1,0:T(8,128)(2,1)}, f32[16,2,512]{2,1,0:T(2,128)}) custom-call(bf16[256,1024]{1,0:T(8,128)(2,1)} %fusion.114.q_ref, bf16[256,1024]{1,0:T(8,128)(2,1)} %fusion.117.g_ref, f32[256,1024]{1,0:T(8,128)} %get-tuple-element.178.o_ref, ...), custom_call_target="tpu_custom_call" | custom-call | flops 1342177280 | bytes 9437184 | tf_op jit(solution)/shard_map/attention_backward/pallas_call | solution.py:203
  691.9 12.1 %collective-permute-done.58 = bf16[144,1024]{1,0:T(8,128)(2,1)S(1)} collective-permute-done((bf16[144,1024]{1,0:T(8,128)(2,1)S(1)}, bf16[144,1024]{1,0:T(8,128)(2,1)S(1)}, u32[]{:S(2)}, u32[]{:S(2)}) %collective-permute-start.58) | collective-permute-done | bytes 294944 | tf_op jit(solution)/shard_map/ppermute | solution.py:56
  779.5 36.3 %collective-permute-done.64 = bf16[144,1024]{1,0:T(8,128)(2,1)S(1)} collective-permute-done((bf16[144,1024]{1,0:T(8,128)(2,1)S(1)}, bf16[144,1024]{1,0:T(8,128)(2,1)S(1)}, u32[]{:S(2)}, u32[]{:S(2)}) %collective-permute-start.64) | collective-permute-done | bytes 294944 | tf_op jit(solution)/shard_map/ppermute | solution.py:56
  831.2 32.9 %collective-permute-done.68 = bf16[256,2816]{1,0:T(8,128)(2,1)S(1)} collective-permute-done((bf16[256,2816]{1,0:T(8,128)(2,1)S(1)}, bf16[256,2816]{1,0:T(8,128)(2,1)S(1)}, u32[]{:S(2)}, u32[]{:S(2)}) %collective-permute-start.68) | collective-permute-done | bytes 1441824 | tf_op jit(solution)/shard_map/ppermute | solution.py:56
  865.2 16.0 %attention_backward.6 = (f32[256,1024]{1,0:T(8,128)}, f32[2,256,1024]{2,1,0:T(8,128)}, bf16[2,256,1024]{2,1,0:T(8,128)(2,1)}, f32[16,2,512]{2,1,0:T(2,128)}) custom-call(bf16[256,1024]{1,0:T(8,128)(2,1)} %convolution_convert_fusion.15.q_ref, bf16[256,1024]{1,0:T(8,128)(2,1)} %fusion.111.g_ref, f32[256,1024]{1,0:T(8,128)} %get-tuple-element.228.o_ref, ...), custom_call_target="tpu_custom_call" | custom-call | flops 1342177280 | bytes 9437184 | tf_op jit(solution)/shard_map/attention_backward/pallas_call | solution.py:203
  915.0 15.9 %attention_backward.7 = (bf16[256,1024]{1,0:T(8,128)(2,1)}, f32[2,256,1024]{2,1,0:T(8,128)}, bf16[2,256,1024]{2,1,0:T(8,128)(2,1)}, f32[16,2,512]{2,1,0:T(2,128)}) custom-call(bf16[256,1024]{1,0:T(8,128)(2,1)} %convolution_convert_fusion.15.q_ref, bf16[256,1024]{1,0:T(8,128)(2,1)} %fusion.111.g_ref, f32[256,1024]{1,0:T(8,128)} %get-tuple-element.228.o_ref, ...), custom_call_target="tpu_custom_call" | custom-call | flops 1342177280 | bytes 9437184 | tf_op jit(solution)/shard_map/attention_backward/pallas_call | solution.py:203
  956.2 18.5 %collective-permute-done.100 = bf16[256,2816]{1,0:T(8,128)(2,1)S(1)} collective-permute-done((bf16[256,2816]{1,0:T(8,128)(2,1)S(1)}, bf16[256,2816]{1,0:T(8,128)(2,1)S(1)}, u32[]{:S(2)}, u32[]{:S(2)}) %collective-permute-start.100) | collective-permute-done | bytes 1441824 | tf_op jit(solution)/shard_map/ppermute | solution.py:739
  1038.5 17.7 %collective-permute-done.87 = bf16[4,128,1024]{2,1,0:T(8,128)(2,1)S(1)} collective-permute-done((bf16[4,128,1024]{2,1,0:T(8,128)(2,1)}, bf16[4,128,1024]{2,1,0:T(8,128)(2,1)S(1)}, u32[]{:S(2)}, u32[]{:S(2)}) %collective-permute-start.87) | collective-permute-done | bytes 1048608 | tf_op jit(solution)/shard_map/ppermute | solution.py:56
  1058.2 12.5 %collective-permute-start.88 = (bf16[128,1024]{1,0:T(8,128)(2,1)S(1)}, bf16[128,1024]{1,0:T(8,128)(2,1)S(1)}, u32[]{:S(2)}, u32[]{:S(2)}) collective-permute-start(bf16[128,1024]{1,0:T(8,128)(2,1)S(1)} %get-tuple-element.374), channel_id=1, source_target_pairs={{0,4},{4,8},{8,12},{12,0},{1,5},{5,9},{9,13},{13,1},{2,6},{6,10},{... | collective-permute-start | bytes 786440 | tf_op jit(solution)/shard_map/ppermute | solution.py:56
  (860 shorter events, 638.8 us)
Async XLA Ops:
  7.2 211.5 %all-gather.6.cloned.1.call-start = ((), (), s32[]{:S(2)}) async-start(), calls=%async_computation.1 | async-start | bytes 19464192 | tf_op jit(solution)/shard_map/all_gather | solution.py:669
  53.3 50.6 %collective-permute-start.13 = (bf16[128,8448]{1,0:T(8,128)(2,1)S(1)}, bf16[128,8448]{1,0:T(8,128)(2,1)S(1)}, u32[]{:S(2)}, u32[]{:S(2)}) collective-permute-start(bf16[128,8448]{1,0:T(8,128)(2,1)S(1)} %copy-done.73), channel_id=1, source_target_pairs={{0,16},{16,0},{1,17},{17,1},{2,18},{18,2},{3,19},{19,3},{4,20},{20... | collective-permute-start | bytes 6488072 | tf_op jit(solution)/shard_map/ppermute | solution.py:234
  106.4 206.8 %all-gather.8.cloned.1.call-start = ((), (), s32[]{:S(2)}) async-start(), calls=%async_computation.2 | async-start | bytes 8650752 | tf_op jit(solution)/shard_map/all_gather | solution.py:670
  110.3 50.2 %collective-permute-start.22 = (bf16[256,2048]{1,0:T(8,128)(2,1)S(1)}, bf16[256,2048]{1,0:T(8,128)(2,1)S(1)}, u32[]{:S(2)}, u32[]{:S(2)}) collective-permute-start(bf16[256,2048]{1,0:T(8,128)(2,1)S(1)} %convolution_convert_fusion.6.k0.v0), channel_id=1, source_target_pairs={{0,2},{2,0},{1,3},{3,1},{4,6},{6,4},{5,7},{7,5},{8,10},{10,8},{9,1... | collective-permute-start | bytes 3145736 | tf_op jit(solution)/shard_map/ppermute | solution.py:56
  164.0 257.7 %all-gather.10.cloned.1.call-start = ((), (), s32[]{:S(2)}) async-start(), calls=%async_computation.3 | async-start | bytes 19464192 | tf_op jit(solution)/shard_map/all_gather | solution.py:671
  164.7 851.9 %reduce-scatter.2.cloned.1.call-start = ((), (), s32[]{:S(2)}) async-start(), calls=%async_computation.4 | async-start | bytes 9469952 | tf_op jit(solution)/shard_map/reduce_scatter | solution.py:726
  319.3 47.4 %collective-permute-start.32 = (bf16[256,2048]{1,0:T(8,128)(2,1)}, bf16[256,2048]{1,0:T(8,128)(2,1)}, u32[]{:S(2)}, u32[]{:S(2)}) collective-permute-start(bf16[256,2048]{1,0:T(8,128)(2,1)} %fusion.52.k0.v0), channel_id=1, source_target_pairs={{0,1},{1,0},{2,3},{3,2},{4,5},{5,4},{6,7},{7,6},{8,9},{9,8},{10,11... | collective-permute-start | bytes 3145736 | tf_op jit(solution)/shard_map/ppermute | solution.py:56
  471.3 55.4 %collective-permute-start.46 = (bf16[512,2816]{1,0:T(8,128)(2,1)}, bf16[512,2816]{1,0:T(8,128)(2,1)S(1)}, u32[]{:S(2)}, u32[]{:S(2)}) collective-permute-start(bf16[512,2816]{1,0:T(8,128)(2,1)} %convolution_convert_fusion.4), channel_id=1, source_target_pairs={{0,1},{1,0},{2,3},{3,2},{4,5},{5,4},{6,7},{7,6},{8,9},{9,8},{10,11... | collective-permute-start | bytes 8650760 | tf_op jit(solution)/shard_map/ppermute | solution.py:56
  471.6 55.1 %collective-permute-start.47 = (bf16[512,2816]{1,0:T(8,128)(2,1)S(1)}, bf16[512,2816]{1,0:T(8,128)(2,1)S(1)}, u32[]{:S(2)}, u32[]{:S(2)}) collective-permute-start(bf16[512,2816]{1,0:T(8,128)(2,1)S(1)} %convolution_convert_fusion.3), channel_id=1, source_target_pairs={{0,1},{1,0},{2,3},{3,2},{4,5},{5,4},{6,7},{7,6},{8,9},{9,8},{10,11... | collective-permute-start | bytes 8650760 | tf_op jit(solution)/shard_map/ppermute | solution.py:56
  512.4 43.3 %collective-permute-start.51 = (bf16[256,2816]{1,0:T(8,128)(2,1)S(1)}, bf16[256,2816]{1,0:T(8,128)(2,1)S(1)}, u32[]{:S(2)}, u32[]{:S(2)}) collective-permute-start(bf16[256,2816]{1,0:T(8,128)(2,1)S(1)} %fusion.44), channel_id=1, source_target_pairs={{0,2},{2,0},{1,3},{3,1},{4,6},{6,4},{5,7},{7,5},{8,10},{10,8},{9,1... | collective-permute-start | bytes 4325384 | tf_op jit(solution)/shard_map/ppermute | solution.py:56
  556.9 62.1 %collective-permute-start.54 = (bf16[256,2816]{1,0:T(8,128)(2,1)}, bf16[256,2816]{1,0:T(8,128)(2,1)}, u32[]{:S(2)}, u32[]{:S(2)}) collective-permute-start(bf16[256,2816]{1,0:T(8,128)(2,1)} %fusion.46), channel_id=1, source_target_pairs={{0,2},{2,0},{1,3},{3,1},{4,6},{6,4},{5,7},{7,5},{8,10},{10,8},{9,1... | collective-permute-start | bytes 4325384 | tf_op jit(solution)/shard_map/ppermute | solution.py:56
  741.5 75.7 %collective-permute-start.67 = (bf16[256,2816]{1,0:T(8,128)(2,1)}, bf16[256,2816]{1,0:T(8,128)(2,1)}, u32[]{:S(2)}, u32[]{:S(2)}) collective-permute-start(bf16[256,2816]{1,0:T(8,128)(2,1)} %add_convert_fusion.1), channel_id=1, source_target_pairs={{0,16},{1,17},{2,18},{3,19},{4,20},{5,21},{6,22},{7,23},{8,24},{9,... | collective-permute-start | bytes 4325384 | tf_op jit(solution)/shard_map/ppermute | solution.py:728
  744.3 366.7 %all-gather.12.cloned.1.call-start = ((), (), s32[]{:S(2)}) async-start(), calls=%async_computation.5 | async-start | bytes 2785280 | tf_op jit(solution)/shard_map/all_gather | solution.py:747
  747.4 69.8 %collective-permute-start.66 = (bf16[256,2816]{1,0:T(8,128)(2,1)S(1)}, bf16[256,2816]{1,0:T(8,128)(2,1)S(1)}, u32[]{:S(2)}, u32[]{:S(2)}) collective-permute-start(bf16[256,2816]{1,0:T(8,128)(2,1)S(1)} %copy-done.85), channel_id=1, source_target_pairs={{0,2},{2,0},{1,3},{3,1},{4,6},{6,4},{5,7},{7,5},{8,10},{10,8},{9,1... | collective-permute-start | bytes 4325384 | tf_op jit(solution)/shard_map/ppermute | solution.py:56
  769.6 46.1 %collective-permute-start.64 = (bf16[144,1024]{1,0:T(8,128)(2,1)S(1)}, bf16[144,1024]{1,0:T(8,128)(2,1)S(1)}, u32[]{:S(2)}, u32[]{:S(2)}) collective-permute-start(bf16[144,1024]{1,0:T(8,128)(2,1)S(1)} %get-tuple-element.336), channel_id=1, source_target_pairs={{0,8},{4,12},{8,0},{12,4},{1,9},{5,13},{9,1},{13,5},{2,10},{6,14},... | collective-permute-start | bytes 884744 | tf_op jit(solution)/shard_map/ppermute | solution.py:56
  769.6 47.4 %collective-permute-start.65 = (bf16[144,1024]{1,0:T(8,128)(2,1)S(1)}, bf16[144,1024]{1,0:T(8,128)(2,1)S(1)}, u32[]{:S(2)}, u32[]{:S(2)}) collective-permute-start(bf16[144,1024]{1,0:T(8,128)(2,1)S(1)} %get-tuple-element.335), channel_id=1, source_target_pairs={{0,4},{4,8},{8,12},{12,0},{1,5},{5,9},{9,13},{13,1},{2,6},{6,10},{... | collective-permute-start | bytes 884744 | tf_op jit(solution)/shard_map/ppermute | solution.py:56
  777.1 127.7 %collective-permute-start.72 = (bf16[256,2816]{1,0:T(8,128)(2,1)}, bf16[256,2816]{1,0:T(8,128)(2,1)}, u32[]{:S(2)}, u32[]{:S(2)}) collective-permute-start(bf16[256,2816]{1,0:T(8,128)(2,1)} %add_convert_fusion.3), channel_id=1, source_target_pairs={{0,16},{1,17},{2,18},{3,19},{4,20},{5,21},{6,22},{7,23},{8,24},{9,... | collective-permute-start | bytes 4325384 | tf_op jit(solution)/shard_map/ppermute | solution.py:728
  817.2 46.8 %collective-permute-start.68 = (bf16[256,2816]{1,0:T(8,128)(2,1)S(1)}, bf16[256,2816]{1,0:T(8,128)(2,1)S(1)}, u32[]{:S(2)}, u32[]{:S(2)}) collective-permute-start(bf16[256,2816]{1,0:T(8,128)(2,1)S(1)} %fusion.48), channel_id=1, source_target_pairs={{0,2},{2,0},{1,3},{3,1},{4,6},{6,4},{5,7},{7,5},{8,10},{10,8},{9,1... | collective-permute-start | bytes 4325384 | tf_op jit(solution)/shard_map/ppermute | solution.py:56
  822.5 87.8 %collective-permute-start.102 = (bf16[256,2816]{1,0:T(8,128)(2,1)}, bf16[256,2816]{1,0:T(8,128)(2,1)}, u32[]{:S(2)}, u32[]{:S(2)}) collective-permute-start(bf16[256,2816]{1,0:T(8,128)(2,1)} %add_convert_fusion), channel_id=1, source_target_pairs={{16,0},{17,1},{18,2},{19,3},{20,4},{21,5},{22,6},{23,7},{24,8},{25... | collective-permute-start | bytes 4325384 | tf_op jit(solution)/shard_map/ppermute | solution.py:739
  824.0 80.9 %collective-permute-start.71 = (bf16[256,2816]{1,0:T(8,128)(2,1)}, bf16[256,2816]{1,0:T(8,128)(2,1)}, u32[]{:S(2)}, u32[]{:S(2)}) collective-permute-start(bf16[256,2816]{1,0:T(8,128)(2,1)} %fusion.49), channel_id=1, source_target_pairs={{0,2},{2,0},{1,3},{3,1},{4,6},{6,4},{5,7},{7,5},{8,10},{10,8},{9,1... | collective-permute-start | bytes 4325384 | tf_op jit(solution)/shard_map/ppermute | solution.py:56
  901.4 48.5 %collective-permute-start.76 = (bf16[256,2816]{1,0:T(8,128)(2,1)}, bf16[256,2816]{1,0:T(8,128)(2,1)}, u32[]{:S(2)}, u32[]{:S(2)}) collective-permute-start(bf16[256,2816]{1,0:T(8,128)(2,1)} %add_convert_fusion.2), channel_id=1, source_target_pairs={{0,16},{1,17},{2,18},{3,19},{4,20},{5,21},{6,22},{7,23},{8,24},{9,... | collective-permute-start | bytes 4325384 | tf_op jit(solution)/shard_map/ppermute | solution.py:728
  943.5 61.6 %collective-permute-start.101 = (bf16[256,2816]{1,0:T(8,128)(2,1)S(1)}, bf16[256,2816]{1,0:T(8,128)(2,1)S(1)}, u32[]{:S(2)}, u32[]{:S(2)}) collective-permute-start(bf16[256,2816]{1,0:T(8,128)(2,1)S(1)} %fusion.50), channel_id=1, source_target_pairs={{16,0},{17,1},{18,2},{19,3},{20,4},{21,5},{22,6},{23,7},{24,8},{25... | collective-permute-start | bytes 4325384 | tf_op jit(solution)/shard_map/ppermute | solution.py:739
  953.8 57.0 %collective-permute-start.77 = (bf16[1024,1024]{1,0:T(8,128)(2,1)}, bf16[1024,1024]{1,0:T(8,128)(2,1)}, u32[]{:S(2)}, u32[]{:S(2)}) collective-permute-start(bf16[1024,1024]{1,0:T(8,128)(2,1)} %convolution_convert_fusion.7), channel_id=1, source_target_pairs={{0,1},{1,0},{2,3},{3,2},{4,5},{5,4},{6,7},{7,6},{8,9},{9,8},{10,11... | collective-permute-start | bytes 6291464 | tf_op jit(solution)/shard_map/ppermute | solution.py:56
  1036.8 43.9 %collective-permute-start.95 = (f32[4,2048]{1,0:T(4,128)S(1)}, f32[4,2048]{1,0:T(4,128)S(1)}, u32[]{:S(2)}, u32[]{:S(2)}) collective-permute-start(f32[4,2048]{1,0:T(4,128)S(1)} %fusion.301), channel_id=1, source_target_pairs={{0,2},{2,0},{1,3},{3,1},{4,6},{6,4},{5,7},{7,5},{8,10},{10,8},{9,1... | collective-permute-start | bytes 98312 | tf_op jit(solution)/shard_map/ppermute | solution.py:56
  (279 other events, 4232.4 us)
Sparse Core Ops, SparseCore 0:
  106.5 110.2 all-gather.5
  220.2 92.8 all-gather.7
  315.6 106.0 all-gather.9
  744.3 143.1 reduce-scatter.1
  1035.8 31.8 all-gather.11

commit v3 on v2

--- a/solution.py
+++ b/solution.py
@@ -317,7 +317,7 @@
     return result, stored
 
 
-def backward(grad_rows, stored, tables, weights, windows, bucket_rows, offload, waited):
+def backward(grad_rows, stored, tables, weights, windows, bucket_rows, source, waited):
     spots, members = tables
     slot_table = spots.astype(BF16)
     (
@@ -328,33 +328,33 @@
     width = inputs.shape[1]
     grad_out = grad_rows.astype(F32)
     grad_slots = (dot_tn(combine_high, grad_rows) + dot_tn(combine_low, grad_rows)).astype(BF16)
-    if offload:
+    if source == 0:
         grad_slots, arrived = lax.optimization_barrier((grad_slots, arrived))
     received = send_slots(grad_slots.reshape(expert_count, -1, width), 1)
     received, waited[0] = lax.optimization_barrier((received, waited[0]))
+    def for_inner(left, right):
+        return dot_tn(inner_columns(left, 1), right).astype(BF16)
+
+    def from_inner(term):
+        return inner_swap(term).reshape(2, -1, term.shape[1])
+
+    def for_outer(left, right, taken):
+        return plus(dot_tn(replica_columns(left, 1), right), take(taken, 1 - lax.axis_index(OUTER), 0))
+
+    down_given, received = lax.optimization_barrier((for_inner(received, hidden), received))
+    down_inner = from_inner(down_given)
+    grad_hidden = matmul(received, weights["down"])
+    unused_value, pull_gelu = jax.vjp(gated_gelu, gate_part, up_part)
+    grad_gate, grad_up = pull_gelu(grad_hidden)
+    grad_gate, grad_up, down_inner, returned = lax.optimization_barrier(
+        (grad_gate.astype(BF16), grad_up.astype(BF16), down_inner, returned)
+    )
     products = jnp.where(spots, dot_nt(grad_rows, returned), 0.0)
     grad_gates = jnp.dot(products, members, precision=lax.Precision.HIGHEST, preferred_element_type=F32)
     grad_logits = gates_all * (grad_gates - jnp.sum(gates_all * grad_gates, axis=-1, keepdims=True))
     grad_logits = grad_logits.astype(BF16)
     term_router = dot_tn(mixed_in, grad_logits)
 
-    def for_inner(left, right):
-        return dot_tn(inner_columns(left, 1), right).astype(BF16)
-
-    def from_inner(term):
-        return inner_swap(term).reshape(2, -1, term.shape[1])
-
-    def for_outer(left, right, taken):
-        return plus(dot_tn(replica_columns(left, 1), right), take(taken, 1 - lax.axis_index(OUTER), 0))
-
-    down_given, received = lax.optimization_barrier((for_inner(received, hidden), received))
-    down_inner = from_inner(down_given)
-    grad_hidden = matmul(received, weights["down"])
-    unused_value, pull_gelu = jax.vjp(gated_gelu, gate_part, up_part)
-    grad_gate, grad_up = pull_gelu(grad_hidden)
-    grad_gate, grad_up, down_inner = lax.optimization_barrier(
-        (grad_gate.astype(BF16), grad_up.astype(BF16), down_inner)
-    )
     grad_gate, grad_up, down_given = lax.optimization_barrier(
         (grad_gate, grad_up, for_outer(received, hidden, down_inner))
     )
@@ -368,10 +368,13 @@
     back_rows = send_slots(grad_arrived.reshape(expert_count, -1, width), -1)
     gate_given = for_outer(arrived, grad_gate, gate_inner)
     up_given = for_outer(arrived, grad_up, up_inner)
-    back_rows, gate_given, up_given, down_outer, waited[1] = lax.optimization_barrier(
-        (back_rows, gate_given, up_given, down_outer, waited[1])
+    back_rows, gate_given, up_given, down_outer, waited[1], waited[5] = lax.optimization_barrier(
+        (back_rows, gate_given, up_given, down_outer, waited[1], waited[5])
     )
     gate_outer = outer_swap(gate_given)
+    if source == 1:
+        waited[5] = reduce_dense(waited[5])
+    share_down = finish_expert(received, hidden, down_inner, down_outer)
 
     grad_mixed = matmul(slot_table, back_rows) + dot_nt(grad_logits, weights["router"])
     grad_middle, term_second = rms_pull(middle, weights["gain_second"], grad_mixed)
@@ -379,22 +382,31 @@
     grad_branch = grad_middle.astype(BF16)
     grad_attended = dot_nt(grad_branch, weights["output"]).astype(BF16)
     term_output = dot_tn(attended, grad_branch).astype(BF16)
-    grad_attended, gate_outer, waited[2] = lax.optimization_barrier((grad_attended, gate_outer, waited[2]))
-    up_outer = outer_swap(up_given)
+    grad_attended, share_down, waited[2] = lax.optimization_barrier((grad_attended, share_down, waited[2]))
+    hop_down = lax.ppermute(share_down, SECTION, [(source, 1 - source)])
     grad_part, outer, both, windows_far = attention_backward(
         queries, grad_attended, attended_full, levels, pairs_kv[2:], windows[:, 2:]
     )
     far_taken = inner_swap(both)
-    grad_part, far_taken, up_outer, waited[3] = lax.optimization_barrier((grad_part, far_taken, up_outer, waited[3]))
+    grad_part, far_taken, gate_outer, waited[3] = lax.optimization_barrier(
+        (grad_part, far_taken, gate_outer, waited[3])
+    )
     passed = plus(outer, far_taken)
     passed, grad_part = lax.optimization_barrier((passed, grad_part))
     outer_sum = outer_swap(passed)
     grad_queries, own, inner, windows_near = attention_backward(
         queries, grad_attended, attended_full, levels, pairs_kv[:2], windows[:, :2], grad_part
     )
-    grad_queries, own, inner, outer_sum, waited[4] = lax.optimization_barrier(
-        (grad_queries, own, inner, outer_sum, waited[4])
-    )
+    share_gate = finish_expert(arrived, grad_gate, gate_inner, gate_outer)
+    even = lax.axis_index(INNER) == 0
+    lefts, rights = (attended, normed), (grad_branch, grad_queries)
+    given = dot_tn(jnp.where(even, *lefts[::-1]), jnp.where(even, *rights[::-1])).astype(BF16)
+    grad_queries, own, inner, outer_sum, share_gate, given, waited[4] = lax.optimization_barrier(
+        (grad_queries, own, inner, outer_sum, share_gate, given, waited[4])
+    )
+    first_taken = inner_swap(given)
+    up_given, own = lax.optimization_barrier((up_given, own))
+    up_outer = outer_swap(up_given)
     grad_windows = jnp.concatenate([windows_near, windows_far], axis=1)
     near_sum = own + inner_swap(inner).astype(F32)
     grad_windows = grad_windows.reshape(HEADS, -1)
@@ -404,52 +416,57 @@
     )
     grad_normed = dot_nt(grad_queries, weights["query"])
     small_early = (term_router, term_second, term_position)
-    if offload:
-        term_query = dot_tn(normed, grad_queries).astype(BF16)
-        term_output = dot_tn(attended, grad_branch).astype(BF16)
-        near_sum, grad_normed, term_query, term_output, small_early = lax.optimization_barrier(
-            (near_sum, grad_normed, term_query, term_output, small_early)
-        )
-    else:
-        even = lax.axis_index(INNER) == 0
-        lefts, rights = (attended, normed), (grad_branch, grad_queries)
-        first_fold = fold_dense(
-            (jnp.where(even, *lefts), jnp.where(even, *rights)),
-            (jnp.where(even, *lefts[::-1]), jnp.where(even, *rights[::-1])),
-        )
-        near_sum, grad_normed, first_fold[0], small_early, waited[5] = lax.optimization_barrier(
-            (near_sum, grad_normed, first_fold[0], small_early, waited[5])
-        )
     grad_pair = (near_sum + outer_sum.astype(F32)).astype(BF16)
-    if offload:
-        grad_normed = grad_normed + dot_nt(grad_pair[0], weights["key"]) + dot_nt(grad_pair[1], weights["value"])
-    else:
-        index = lax.axis_index(INNER)
-        second_fold = fold_dense((normed, take(grad_pair, index, 0)), (normed, take(grad_pair, 1 - index, 0)))
-        second_fold[0], grad_pair = lax.optimization_barrier((second_fold[0], grad_pair))
-        grad_normed = grad_normed + dot_nt(grad_pair[0], weights["key"]) + dot_nt(grad_pair[1], weights["value"])
+    index = lax.axis_index(INNER)
+    given = dot_tn(normed, take(grad_pair, 1 - index, 0)).astype(BF16)
+    grad_pair, grad_normed, first_taken, given, small_early, waited[5] = lax.optimization_barrier(
+        (grad_pair, grad_normed, first_taken, given, small_early, waited[5])
+    )
+    second_taken = inner_swap(given)
+    count = lax.axis_size(EXPERT)
+    first_sum = plus(dot_tn(jnp.where(even, *lefts), jnp.where(even, *rights)), first_taken)
+    first_sum = first_sum.reshape(2 * count, -1, width)
+    grad_normed = grad_normed + dot_nt(grad_pair[0], weights["key"]) + dot_nt(grad_pair[1], weights["value"])
     grad_in, term_first = rms_pull(inputs, weights["gain_first"], grad_normed)
     grad_in = grad_in + grad_middle
-    small_terms = (small_early[0], term_first, small_early[1], small_early[2])
-    pending = (
-        (arrived, grad_gate, gate_inner, gate_outer),
-        (arrived, grad_up, up_inner, up_outer),
-        (received, hidden, down_inner, down_outer),
-    )
-    if offload:
-        dense_terms = (
-            term_output,
-            term_query,
-            dot_tn(normed, grad_pair[0]).astype(BF16),
-            dot_tn(normed, grad_pair[1]).astype(BF16),
-        )
+    grad_rows = grad_in.astype(BF16)
+    small = pack_small(small_early[0], term_first, small_early[1], small_early[2], count).astype(BF16)
+    small = small.reshape(2 * count, -1, width)
+    small = jnp.pad(small, ((0, 0), (0, 16 - small.shape[1]), (0, 0)))
+    second_sum = plus(dot_tn(normed, take(grad_pair, index, 0)), second_taken)
+    second_sum = jnp.concatenate([second_sum.reshape(2 * count, -1, width), small], axis=1)
+    if source == 0:
+        dense = jnp.concatenate([first_sum, second_sum], axis=1)
+        grad_rows, dense = lax.optimization_barrier((grad_rows, dense))
     else:
-        dense_terms = (first_fold, second_fold)
-    return grad_in, dense_terms, small_terms, pending, waited
-
-
-def finish_expert(pending):
-    left, right, taken, last = pending
+        dense = (reduce_dense(first_sum), fold_dense(second_sum))
+    share_up = finish_expert(arrived, grad_up, up_inner, up_outer)
+    return grad_in, grad_rows, dense, (share_gate, share_up, share_down), hop_down, waited
+
+
+def reduce_dense(blocks):
+    return lax.psum_scatter(blocks, (EXPERT, OUTER), scatter_dimension=0, tiled=False)
+
+
+def fold_dense(blocks):
+    count = lax.axis_size(EXPERT)
+    expert_index, outer_index = lax.axis_index(EXPERT), lax.axis_index(OUTER)
+    blocks = blocks.reshape(count, 2, -1, blocks.shape[-1])
+    part = plus(take(blocks, outer_index, 1), outer_swap(take(blocks, 1 - outer_index, 1)))
+    total = take(part, expert_index, 0).astype(F32)
+    for ahead in range(1, count):
+        given = take(part, jnp.remainder(expert_index + ahead, count), 0)
+        total = total + shift_to(given, EXPERT, ahead).astype(F32)
+    total = total.astype(BF16)
+    total = plus(total, lax.ppermute(total, SECTION, [(1, 0)]))
+    partner = outer_swap(total)
+    lower, even = outer_index == 0, lax.axis_index(INNER) == 0
+    own = jnp.where(lower, jnp.stack([total, partner]), jnp.stack([partner, total]))
+    other = inner_swap(own)
+    return jnp.where(even, jnp.stack([own, other]), jnp.stack([other, own]))
+
+
+def finish_expert(left, right, taken, last):
     return plus(dot_tn(replica_columns(left, 0), right) + take(taken, lax.axis_index(OUTER), 0).astype(F32), last)
 
 
@@ -477,48 +494,6 @@
     width = values.shape[1] // 4
     place = 2 * jnp.bitwise_xor(lax.axis_index(OUTER), other) + lax.axis_index(INNER)
     return lax.dynamic_slice_in_dim(values, place * width, width, 1)
-
-
-def fold_experts(blocks):
-    count, index = lax.axis_size(EXPERT), lax.axis_index(EXPERT)
-    total = take(blocks, index, 0).astype(F32)
-    for ahead in range(1, count):
-        given = take(blocks, jnp.remainder(index + ahead, count), 0)
-        total = total + shift_to(given, EXPERT, ahead).astype(F32)
-    return total
-
-
-def fold_dense(own_pair, given_pair):
-    given = dot_tn(*given_pair).astype(BF16)
-    return [inner_swap(given), own_pair]
-
-
-def finish_dense(fold):
-    taken, (left, right) = fold
-    outer_index, even = lax.axis_index(OUTER), lax.axis_index(INNER) == 0
-    count = lax.axis_size(EXPERT)
-    size = left.shape[1] // (2 * count)
-    rows = taken.reshape(count, 2, -1, taken.shape[1])
-
-    def part(index):
-        term = dot_tn(pick_columns(left, index, size, 2), right)
-        return term.reshape(count, -1, taken.shape[1]) + take(rows, index, 1).astype(F32)
-
-    outer_taken = outer_swap(part(1 - outer_index).astype(BF16))
-    total = fold_experts(plus(part(outer_index), outer_taken)).astype(BF16)
-    total = plus(total, lax.ppermute(total, SECTION, [(1, 0)]))
-    partner = outer_swap(total)
-    lower = outer_index == 0
-    own = jnp.concatenate([jnp.where(lower, total, partner), jnp.where(lower, partner, total)], axis=0)
-    other = inner_swap(own)
-    return jnp.where(even, own, other), jnp.where(even, other, own)
-
-
-def fold_small(flat, source):
-    flat = flat + inner_swap(flat)
-    flat = flat + outer_swap(flat)
-    flat = fold_experts(flat)
-    return flat + lax.ppermute(flat, SECTION, [(source, 1 - source)])
 
 
 def pack_small(router, first, second, position, count):
@@ -591,7 +566,7 @@
     def half_of(part, index):
         return lax.dynamic_slice_in_dim(part, index * (part.shape[0] // 2), part.shape[0] // 2, 0)
 
-    def ring_gather(piece):
+    def ring_gather(piece, joined=(), at=None):
         whole = jnp.zeros((model_width, piece.shape[1]), BF16)
         for step in range(expert_count):
             start = jnp.remainder(expert_index - step + expert_count, expert_count) * dense_rows
@@ -599,7 +574,9 @@
             whole = lax.dynamic_update_slice(whole, inner_swap(piece), (start + (1 - inner_index) * half_rows, 0))
             if step + 1 < expert_count:
                 piece = shift_to(piece, EXPERT, 1)
-        return whole
+            if step == at:
+                piece, joined = lax.optimization_barrier((piece, joined))
+        return whole, joined
 
     def half_of(part, index):
         return lax.dynamic_slice_in_dim(part, index * (part.shape[0] // 2), part.shape[0] // 2, 0)
@@ -620,23 +597,23 @@
     second_own, pair_piece = lax.optimization_barrier(
         (half_piece(query_weight[0], output_weight[0]), pair_piece)
     )
-    second_half = from_first(second_own)
     wide_own = (expert_gate[0, 0], expert_up[0, 0], expert_down[0, 0].T)
     wide_kept = jnp.concatenate([half_of(part, section_index) for part in wide_own], axis=1)
     wide_sent = jnp.concatenate([half_of(part, 1 - section_index) for part in wide_own], axis=1)
-    wide_sent, second_half = lax.optimization_barrier((wide_sent, second_half))
+    wide_sent, pair_piece = lax.optimization_barrier((wide_sent, pair_piece))
     wide_taken = section_swap(wide_sent)
-    first_pair = ring_gather(pair_piece)
-    first_pair, small_all = lax.optimization_barrier((first_pair, small_all))
+    second_half = from_first(second_own)
+    first_pair, wide_taken = ring_gather(pair_piece, wide_taken, expert_count - 2 if expert_count > 1 else 0)
+    first_pair, small_all, second_half = lax.optimization_barrier((first_pair, small_all, second_half))
     small_parts = [
         unpack_small(small_all[layer], dense_rows, expert_count, position_bias.shape[1], position_bias.shape[2])
         for layer in range(2)
     ]
     normed = rms_scale(own_rows.astype(F32), small_parts[0][1].astype(F32)).astype(BF16)
     first_own = matmul(normed, first_pair).astype(BF16)
-    second_half, first_own, wide_taken = lax.optimization_barrier((second_half, first_own, wide_taken))
+    second_half, first_own = lax.optimization_barrier((second_half, first_own))
     first_outer = outer_swap(first_own)
-    second_whole = ring_gather(second_half)
+    second_whole, unused = ring_gather(second_half)
     second_whole, first_outer = lax.optimization_barrier((second_whole, first_outer))
     first_query, first_output = second_whole[:, :model_width], second_whole[:, model_width:]
 
@@ -714,45 +691,48 @@
         kept.append(stored)
 
     weights, windows, tables = layers[1]
-    grad_in_one, dense_terms, small_one, pending, waited = backward(
-        own_cotangent, kept[1], tables, weights, windows, bucket_rows, True, [()] * 6
-    )
-    grads = grad_in_one.astype(BF16)
-    small_one = pack_small(*small_one, expert_count).astype(BF16).reshape(1, expert_count, -1, model_width)
-    small_one = jnp.pad(small_one, ((0, 3), (0, 0), (0, -small_one.shape[2] % 16), (0, 0)))
-    dense = jnp.stack(dense_terms).reshape(4, expert_count, dense_rows, model_width)
-    dense = jnp.concatenate([dense, small_one], axis=2).reshape(4 * expert_count, -1, model_width)
-    grads, dense = lax.optimization_barrier((grads, dense))
-    dense_share = lax.psum_scatter(dense, REPLICA + (EXPERT,), scatter_dimension=0, tiled=False)
-    shares_one = [finish_expert(part) for part in pending]
-    hops_one = [lax.ppermute(share, SECTION, [(0, 1)]) for share in shares_one]
+    grad_in_one, grads, dense_one, shares_one, hop_down_one, waited = backward(
+        own_cotangent, kept[1], tables, weights, windows, bucket_rows, 0, [()] * 6
+    )
+    hop_gate_one, hop_up_one = (lax.ppermute(share, SECTION, [(0, 1)]) for share in shares_one[:2])
     grad_from_one = lax.ppermute(grads, SECTION, [(0, 1)])
 
     weights, windows, tables = layers[0]
-    waited = [tuple(shares_one), hops_one[2], grad_from_one, hops_one[0], (), hops_one[1]]
-    grad_in_zero, folds_zero, small_zero, pending, waited = backward(
-        grads, kept[0], tables, weights, windows, bucket_rows, False, waited
-    )
-    shares_one, hop_two, grad_from_one, hop_zero, unused, hop_one = waited
-    hops_one = (hop_zero, hop_one, hop_two)
-    shares_zero = [finish_expert(part) for part in pending]
-    hops_zero = [lax.ppermute(share, SECTION, [(1, 0)]) for share in shares_zero]
-
+    output_taken = section_swap(jnp.where(first_section, outputs[1], outputs[0]))
+    waited = [(hop_down_one, output_taken), shares_one, (), hop_gate_one, (), dense_one]
+    grad_in_zero, grads, dense_zero, shares_zero, hop_down_zero, waited = backward(
+        grads, kept[0], tables, weights, windows, bucket_rows, 1, waited
+    )
+    (hop_down_one, output_taken), shares_one, unused, hop_gate_one, unused, dense_one = waited
+    hops_one = (hop_gate_one, hop_up_one, hop_down_one)
+    hop_gate_zero, hop_up_zero = (lax.ppermute(share, SECTION, [(1, 0)]) for share in shares_zero[:2])
+    early_zero, late_zero = dense_zero
+    half_count = dense_rows // 2
+    early_taken = lax.ppermute(early_zero, SECTION, [(1, 0)])
+    one_taken = lax.ppermute(dense_one, SECTION, [(0, 1)])
+    early_own = jnp.where(
+        first_section, plus(early_zero, early_taken), plus(dense_one[:half_count], one_taken[:half_count])
+    )
+    dense_own = jnp.concatenate([early_own, plus(dense_one[half_count:], one_taken[half_count:])], axis=0)
+    hops_zero = (hop_gate_zero, hop_up_zero, hop_down_zero)
     final_gate, final_up, final_down = (
         jnp.where(first_section, zero, one).astype(F32) + jnp.where(first_section, zero_hop, one_hop).astype(F32)
         for zero, zero_hop, one, one_hop in zip(shares_zero, hops_zero, shares_one, hops_one)
     )
-    dense_share, grad_in_zero = lax.optimization_barrier((dense_share, grad_in_zero))
-    dense_share = plus(dense_share, lax.ppermute(dense_share, SECTION, [(0, 1)]))
-    dense_one = lax.all_gather(dense_share, REPLICA, axis=0, tiled=False)
-    dense_zero = finish_dense(folds_zero[0]) + finish_dense(folds_zero[1])
-    final_output, final_query, final_key, final_value = (
-        jnp.where(first_section, dense_zero[k], dense_one[k, :dense_rows]).astype(F32) for k in range(4)
-    )
-    small_zero = fold_small(pack_small(*small_zero, expert_count), 1)
-    small_one = dense_one[0, dense_rows:].reshape(-1)[: small_zero.shape[0]].astype(F32)
+    final_dense = lax.all_gather(dense_own, REPLICA, axis=0, tiled=False).reshape(2, 2, -1, model_width)
+    late_own = jnp.where(first_section, late_zero, final_dense[:, :, half_count:].transpose(1, 0, 2, 3))
+    final_output, final_query = (
+        final_dense[:, inner, :half_count].reshape(dense_rows, model_width).astype(F32) for inner in range(2)
+    )
+    final_key, final_value = (
+        late_own[inner, :, :half_count].reshape(dense_rows, model_width).astype(F32) for inner in range(2)
+    )
+    small_rows = late_own[:, :, half_count:].astype(F32)
+    small_rows = (small_rows[0] + small_rows[1]).reshape(2, -1)
+    small_length = small_own.shape[0]
+    small_rows = small_rows[:, : small_length // 2].reshape(1, -1)
     final_router, final_first, final_second, final_position = unpack_small(
-        jnp.where(first_section, small_zero, small_one).reshape(1, -1), dense_rows, expert_count, heads_own, buckets
+        small_rows, dense_rows, expert_count, heads_own, buckets
     )
 
     def both_micros(kept_one, taken_one):
@@ -760,9 +740,8 @@
             first_section, jnp.stack([kept_one, taken_one]), jnp.stack([taken_one, kept_one])
         )[None, :, None]
 
-    output_taken = section_swap(jnp.where(first_section, outputs[1], outputs[0]))
     section_output = both_micros(jnp.where(first_section, outputs[0], outputs[1]), output_taken)
-    grad_from_zero = lax.ppermute(grad_in_zero.astype(BF16), SECTION, [(1, 0)])
+    grad_from_zero = lax.ppermute(grads, SECTION, [(1, 0)])
     grad_taken = jnp.where(first_section, grad_from_zero, grad_from_one).astype(F32)
     grad_kept = jnp.where(first_section, grad_in_zero, grad_in_one)
     input_gradient = both_micros(grad_kept, grad_taken)

time: 1130 us -> 1060 us (0.938)
  starting transfers between devices: 177 us -> 119 us
  waiting for transfers between devices: 474 us -> 461 us
    ppermute x84 -> x75, starting transfers between devices: 131 us -> 70 us  [shift_to(): lax.ppermute(value, axis, [(source, (source + steps) % count) for source...]
    ppermute x8, waiting for transfers between devices: 10.5 us -> 53.6 us  [the longest x1 32.4 us: shards(): early_taken = lax.ppermute(early_zero, SECTION, [(1, 0)])]
    ppermute x84 -> x75, waiting for transfers between devices: 375 us -> 341 us  [shift_to(): lax.ppermute(value, axis, [(source, (source + steps) % count) for source...]
    reduce_scatter x1 -> x2, waiting for transfers between devices: 0.01 us -> 30.8 us  [reduce_dense(): lax.psum_scatter(blocks, (EXPERT, OUTER), scatter_dimension=0, tiled=False)]
    ppermute x3 -> x2, waiting for transfers between devices: 28 us -> 0.01 us  [shards(): lax.ppermute(share, SECTION, [(1, 0)])]
    ppermute x5, waiting for transfers between devices: 32.8 us -> 8.73 us  [section_swap(): return lax.ppermute(value, SECTION, [(0, 1), (1, 0)])]
    all_gather x1, waiting for transfers between devices: 26.7 us -> 13.2 us  [shards(): second_all = lax.all_gather(second_piece, dense_axes, axis=0, tiled=True)]
    dot_general x36 -> x34, matrix products: 89.9 us -> 91.5 us  [dot_tn(): lax.dot_general(left, right, (((0,), (0,)), ((), ())), preferred_element_...]
  transfers between devices with their start and end apart: 108 -> 99, of which waited for: 43 -> 52; matrix products, arithmetic and copies ran while one was open for 25% -> 29% of each run, Pallas kernels for 8% -> 9%
where the time goes in v3:
time: 1060 us; the launch traced here: 1050 us
  waiting for transfers between devices  461 us (43%)
  matrix products  240 us (23%)
  starting transfers between devices  119 us (11%)
  Pallas kernels  94 us (9%)
  local copies, waits for them, and re-layouts  61 us (6%)
  other arithmetic  59.4 us (6%)
  between operations  17.2 us (2%)
    ppermute x75, waiting for transfers between devices, shift_to(): lax.ppermute(value, axis, [(source, (source + steps) % count) for source...  341 us
    dot_general x34, matrix products, dot_tn(): lax.dot_general(left, right, (((0,), (0,)), ((), ())), preferred_element_...  91.5 us
    dot_general x24, matrix products, matmul(): return jnp.dot(left, right, preferred_element_type=F32)  85.3 us
    ppermute x75, starting transfers between devices, shift_to(): lax.ppermute(value, axis, [(source, (source + steps) % count) for source...  70 us
    pallas_call x4, Pallas kernels, attention_backward(): pl.pallas_call(functools.partial(attention_backward_kernel, given=given i...  63.2 us
    dot_general x18, matrix products, dot_nt(): lax.dot_general(left, right, (((1,), (1,)), ((), ())), preferred_element_...  60.6 us
    ppermute x1, waiting for transfers between devices, shards(): early_taken = lax.ppermute(early_zero, SECTION, [(1, 0)])  32.4 us
    reduce_scatter x2, waiting for transfers between devices, reduce_dense(): lax.psum_scatter(blocks, (EXPERT, OUTER), scatter_dimension=0, tiled=False)  30.8 us
  transfers between devices with their start and end apart: 99, of which 52 were waited for; matrix products, arithmetic and copies ran while one was open for 29% of the time, Pallas kernels for 9%

profile of v3, /device:TPU:0, one launch (start us, length us, event | category | flops | bytes accessed | tf_op | source)
XLA Modules:
  0.0 1050.5 jit_solution(886023228395500857)
XLA Ops:
  30.8 12.8 %collective-permute-done.2 = bf16[128,2048]{1,0:T(8,128)(2,1)S(1)} collective-permute-done((bf16[128,2048]{1,0:T(8,128)(2,1)S(1)}, bf16[128,2048]{1,0:T(8,128)(2,1)S(1)}, u32[]{:S(2)}, u32[]{:S(2)}) %collective-permute-start.2) | collective-permute-done | bytes 524320 | tf_op jit(solution)/shard_map/ppermute | solution.py:56
  43.6 13.6 %collective-permute-done.4 = bf16[128,2048]{1,0:T(8,128)(2,1)} collective-permute-done((bf16[128,2048]{1,0:T(8,128)(2,1)S(1)}, bf16[128,2048]{1,0:T(8,128)(2,1)}, u32[]{:S(2)}, u32[]{:S(2)}) %collective-permute-start.4) | collective-permute-done | bytes 524320 | tf_op jit(solution)/shard_map/ppermute | solution.py:56
  57.4 12.4 %collective-permute-done.6 = bf16[128,2048]{1,0:T(8,128)(2,1)S(1)} collective-permute-done((bf16[128,2048]{1,0:T(8,128)(2,1)}, bf16[128,2048]{1,0:T(8,128)(2,1)S(1)}, u32[]{:S(2)}, u32[]{:S(2)}) %collective-permute-start.6) | collective-permute-done | bytes 524320 | tf_op jit(solution)/shard_map/ppermute | solution.py:56
  130.0 15.5 %collective-permute-done.18 = bf16[128,2048]{1,0:T(8,128)(2,1)} collective-permute-done((bf16[128,2048]{1,0:T(8,128)(2,1)S(1)}, bf16[128,2048]{1,0:T(8,128)(2,1)}, u32[]{:S(2)}, u32[]{:S(2)}) %collective-permute-start.18) | collective-permute-done | bytes 524320 | tf_op jit(solution)/shard_map/ppermute | solution.py:56
  180.4 15.4 %attention_forward.2 = (bf16[256,1024]{1,0:T(8,128)(2,1)}, f32[256,1024]{1,0:T(8,128)}, f32[8,2,256]{2,1,0:T(2,128)}) custom-call(bf16[256,1024]{1,0:T(8,128)(2,1)} %convolution_convert_fusion.13.q_ref, bf16[256,2048]{1,0:T(8,128)(2,1)} %copy-done.13, bf16[256,2048]{1,0:T(8,128)(2,1)} %copy-done.15, bf16[256,2048]{1,0:T(8,128)(2,1)} %copy-done.14, ...), custom_call_target="tpu_custom_call" | custom-call | flops 1073741824 | bytes 5242880 | tf_op jit(solution)/shard_map/attention_forward/pallas_call | solution.py:108
  212.5 19.4 %collective-permute-done.27 = bf16[144,1024]{1,0:T(8,128)(2,1)S(1)} collective-permute-done((bf16[144,1024]{1,0:T(8,128)(2,1)}, bf16[144,1024]{1,0:T(8,128)(2,1)S(1)}, u32[]{:S(2)}, u32[]{:S(2)}) %collective-permute-start.27) | collective-permute-done | bytes 294944 | tf_op jit(solution)/shard_map/ppermute | solution.py:56
  272.0 19.8 %collective-permute-done.30 = bf16[144,1024]{1,0:T(8,128)(2,1)S(1)} collective-permute-done((bf16[144,1024]{1,0:T(8,128)(2,1)S(1)}, bf16[144,1024]{1,0:T(8,128)(2,1)S(1)}, u32[]{:S(2)}, u32[]{:S(2)}) %collective-permute-start.30) | collective-permute-done | bytes 294944 | tf_op jit(solution)/shard_map/ppermute | solution.py:56
  293.2 13.2 %all-gather.8.cloned.1.call-done = bf16[1024,4096]{1,0:T(8,128)(2,1)} async-done(((bf16[32,4096]{1,0:T(8,128)(2,1)}), bf16[1024,4096]{1,0:T(8,128)(2,1)}) %all-gather.8.cloned.1.call-update) | async-done | bytes 8388624 | tf_op jit(solution)/shard_map/all_gather | solution.py:647
  311.5 41.1 %collective-permute-done.33.k2.v2.k0.v0 = bf16[256,2048]{1,0:T(8,128)(2,1)} collective-permute-done((bf16[256,2048]{1,0:T(8,128)(2,1)S(1)}, bf16[256,2048]{1,0:T(8,128)(2,1)}, u32[]{:S(2)}, u32[]{:S(2)}) %collective-permute-start.33) | collective-permute-done | bytes 1048608 | tf_op jit(solution)/shard_map/ppermute | solution.py:56
  359.0 15.4 %attention_forward.3 = (bf16[256,1024]{1,0:T(8,128)(2,1)}, f32[256,1024]{1,0:T(8,128)}, f32[8,2,256]{2,1,0:T(2,128)}) custom-call(bf16[256,1024]{1,0:T(8,128)(2,1)} %fusion.109.q_ref, bf16[256,2048]{1,0:T(8,128)(2,1)} %copy-done.16, bf16[256,2048]{1,0:T(8,128)(2,1)} %copy-done.17, bf16[256,2048]{1,0:T(8,128)(2,1)} %collective-permute-done.33.k2.v2.k0.v0, ...), custom_call_target="tpu_custom_call" | custom-call | flops 1073741824 | bytes 5242880 | tf_op jit(solution)/shard_map/attention_forward/pallas_call | solution.py:108
  387.3 19.3 %collective-permute-done.36 = bf16[144,1024]{1,0:T(8,128)(2,1)S(1)} collective-permute-done((bf16[144,1024]{1,0:T(8,128)(2,1)S(1)}, bf16[144,1024]{1,0:T(8,128)(2,1)S(1)}, u32[]{:S(2)}, u32[]{:S(2)}) %collective-permute-start.36) | collective-permute-done | bytes 294944 | tf_op jit(solution)/shard_map/ppermute | solution.py:56
  459.0 11.7 %collective-permute-done.39 = bf16[144,1024]{1,0:T(8,128)(2,1)} collective-permute-done((bf16[144,1024]{1,0:T(8,128)(2,1)}, bf16[144,1024]{1,0:T(8,128)(2,1)}, u32[]{:S(2)}, u32[]{:S(2)}) %collective-permute-start.39) | collective-permute-done | bytes 294944 | tf_op jit(solution)/shard_map/ppermute | solution.py:56
  472.0 13.3 %multiply_convert_fusion.1 = (bf16[576,2816]{1,0:T(8,128)(2,1)S(1)}, bf16[576,2816]{1,0:T(8,128)(2,1)S(1)}) fusion(f32[576,2816]{1,0:T(8,128)} %fusion.25, f32[576,2816]{1,0:T(8,128)} %get-tuple-element.442, bf16[576,1024]{1,0:T(8,128)(2,1)} %copy-done.45, bf16[1024,8448]{1,0:T(8,128)(2,1)} %all-gather.10.cloned.1.call-done), kind=kOutput, calls=%fused_computation.21 | convolution fusion | flops 3360817152 | bytes 26411008 | tf_op jit(solution)/shard_map/dot_general | solution.py:29
  532.8 11.7 %collective-permute-done.48 = bf16[144,1024]{1,0:T(8,128)(2,1)S(1)} collective-permute-done((bf16[144,1024]{1,0:T(8,128)(2,1)S(1)}, bf16[144,1024]{1,0:T(8,128)(2,1)S(1)}, u32[]{:S(2)}, u32[]{:S(2)}) %collective-permute-start.48) | collective-permute-done | bytes 294944 | tf_op jit(solution)/shard_map/ppermute | solution.py:56
  553.2 15.8 %attention_backward.4 = (f32[256,1024]{1,0:T(8,128)}, f32[2,256,1024]{2,1,0:T(8,128)}, bf16[2,256,1024]{2,1,0:T(8,128)(2,1)}, f32[16,2,512]{2,1,0:T(2,128)}) custom-call(bf16[256,1024]{1,0:T(8,128)(2,1)} %fusion.109.q_ref, bf16[256,1024]{1,0:T(8,128)(2,1)} %fusion.112.g_ref, f32[256,1024]{1,0:T(8,128)} %get-tuple-element.192.o_ref, ...), custom_call_target="tpu_custom_call" | custom-call | flops 1342177280 | bytes 9437184 | tf_op jit(solution)/shard_map/attention_backward/pallas_call | solution.py:203
  582.5 15.8 %attention_backward.5 = (bf16[256,1024]{1,0:T(8,128)(2,1)}, f32[2,256,1024]{2,1,0:T(8,128)}, bf16[2,256,1024]{2,1,0:T(8,128)(2,1)}, f32[16,2,512]{2,1,0:T(2,128)}) custom-call(bf16[256,1024]{1,0:T(8,128)(2,1)} %fusion.109.q_ref, bf16[256,1024]{1,0:T(8,128)(2,1)} %fusion.112.g_ref, f32[256,1024]{1,0:T(8,128)} %get-tuple-element.192.o_ref, ...), custom_call_target="tpu_custom_call" | custom-call | flops 1342177280 | bytes 9437184 | tf_op jit(solution)/shard_map/attention_backward/pallas_call | solution.py:203
  656.2 19.8 %collective-permute-done.58 = bf16[144,1024]{1,0:T(8,128)(2,1)S(1)} collective-permute-done((bf16[144,1024]{1,0:T(8,128)(2,1)S(1)}, bf16[144,1024]{1,0:T(8,128)(2,1)S(1)}, u32[]{:S(2)}, u32[]{:S(2)}) %collective-permute-start.58) | collective-permute-done | bytes 294944 | tf_op jit(solution)/shard_map/ppermute | solution.py:56
  683.2 12.1 %multiply_convert_fusion = (bf16[576,2816]{1,0:T(8,128)(2,1)S(1)}, bf16[576,2816]{1,0:T(8,128)(2,1)S(1)}) fusion(f32[576,2816]{1,0:T(8,128)} %fusion.37, f32[576,2816]{1,0:T(8,128)} %get-tuple-element.432, bf16[576,1024]{1,0:T(8,128)(2,1)S(1)} %pad_maximum_fusion.8, bf16[1024,8448]{1,0:T(8,128)(2,1)} %all-gather.6.cloned.1.call-done), kind=kOutput, calls=%fused_computation.20 | convolution fusion | flops 3360817152 | bytes 26411008 | tf_op jit(solution)/shard_map/dot_general | solution.py:29
  772.7 15.9 %attention_backward.6 = (f32[256,1024]{1,0:T(8,128)}, f32[2,256,1024]{2,1,0:T(8,128)}, bf16[2,256,1024]{2,1,0:T(8,128)(2,1)}, f32[16,2,512]{2,1,0:T(2,128)}) custom-call(bf16[256,1024]{1,0:T(8,128)(2,1)} %convolution_convert_fusion.13.q_ref, bf16[256,1024]{1,0:T(8,128)(2,1)} %fusion.106.g_ref, f32[256,1024]{1,0:T(8,128)} %get-tuple-element.248.o_ref, ...), custom_call_target="tpu_custom_call" | custom-call | flops 1342177280 | bytes 9437184 | tf_op jit(solution)/shard_map/attention_backward/pallas_call | solution.py:203
  791.5 13.8 %collective-permute-done.71 = bf16[256,2816]{1,0:T(8,128)(2,1)} collective-permute-done((bf16[256,2816]{1,0:T(8,128)(2,1)}, bf16[256,2816]{1,0:T(8,128)(2,1)}, u32[]{:S(2)}, u32[]{:S(2)}) %collective-permute-start.71) | collective-permute-done | bytes 1441824 | tf_op jit(solution)/shard_map/ppermute | solution.py:56
  808.6 15.8 %attention_backward.7 = (bf16[256,1024]{1,0:T(8,128)(2,1)}, f32[2,256,1024]{2,1,0:T(8,128)}, bf16[2,256,1024]{2,1,0:T(8,128)(2,1)}, f32[16,2,512]{2,1,0:T(2,128)}) custom-call(bf16[256,1024]{1,0:T(8,128)(2,1)} %convolution_convert_fusion.13.q_ref, bf16[256,1024]{1,0:T(8,128)(2,1)} %fusion.106.g_ref, f32[256,1024]{1,0:T(8,128)} %get-tuple-element.248.o_ref, ...), custom_call_target="tpu_custom_call" | custom-call | flops 1342177280 | bytes 9437184 | tf_op jit(solution)/shard_map/attention_backward/pallas_call | solution.py:203
  849.3 15.8 %reduce-scatter.3.cloned.1.call-done = bf16[1,272,1024]{2,1,0:T(8,128)(2,1)} async-done(((bf16[8,272,1024]{2,1,0:T(8,128)(2,1)}), bf16[1,272,1024]{2,1,0:T(8,128)(2,1)}) %reduce-scatter.3.cloned.1.call-update) | async-done | bytes 557072 | tf_op jit(solution)/shard_map/reduce_scatter | solution.py:448
  929.6 15.0 %reduce-scatter.5.cloned.1.call-done = bf16[1,128,1024]{2,1,0:T(8,128)(2,1)} async-done(((bf16[8,128,1024]{2,1,0:T(8,128)(2,1)}), bf16[1,128,1024]{2,1,0:T(8,128)(2,1)}) %reduce-scatter.5.cloned.1.call-update) | async-done | bytes 262160 | tf_op jit(solution)/shard_map/reduce_scatter | solution.py:448
  955.9 32.4 %collective-permute-done.78 = bf16[128,1024]{1,0:T(8,128)(2,1)S(1)} collective-permute-done((bf16[128,1024]{1,0:T(8,128)(2,1)}, bf16[128,1024]{1,0:T(8,128)(2,1)S(1)}, u32[]{:S(2)}, u32[]{:S(2)}) %collective-permute-start.78) | collective-permute-done | bytes 262176 | tf_op jit(solution)/shard_map/ppermute | solution.py:711
  (729 shorter events, 626.8 us)
Async XLA Ops:
  7.2 224.8 %all-gather.6.cloned.1.call-start = ((), (), s32[]{:S(2)}) async-start(), calls=%async_computation.2 | async-start | bytes 19464192 | tf_op jit(solution)/shard_map/all_gather | solution.py:646
  25.6 50.1 %collective-permute-start.7 = (bf16[128,8448]{1,0:T(8,128)(2,1)}, bf16[128,8448]{1,0:T(8,128)(2,1)}, u32[]{:S(2)}, u32[]{:S(2)}) collective-permute-start(bf16[128,8448]{1,0:T(8,128)(2,1)} %pad_maximum_fusion), channel_id=1, source_target_pairs={{0,16},{16,0},{1,17},{17,1},{2,18},{18,2},{3,19},{19,3},{4,20},{20... | collective-permute-start | bytes 6488072 | tf_op jit(solution)/shard_map/ppermute | solution.py:234
  79.4 227.0 %all-gather.8.cloned.1.call-start = ((), (), s32[]{:S(2)}) async-start(), calls=%async_computation.3 | async-start | bytes 8650752 | tf_op jit(solution)/shard_map/all_gather | solution.py:647
  117.5 48.0 %collective-permute-start.22 = (bf16[256,2048]{1,0:T(8,128)(2,1)S(1)}, bf16[256,2048]{1,0:T(8,128)(2,1)S(1)}, u32[]{:S(2)}, u32[]{:S(2)}) collective-permute-start(bf16[256,2048]{1,0:T(8,128)(2,1)S(1)} %convolution_convert_fusion.6.k0.v0), channel_id=1, source_target_pairs={{0,2},{2,0},{1,3},{3,1},{4,6},{6,4},{5,7},{7,5},{8,10},{10,8},{9,1... | collective-permute-start | bytes 3145736 | tf_op jit(solution)/shard_map/ppermute | solution.py:56
  169.0 245.4 %all-gather.10.cloned.1.call-start = ((), (), s32[]{:S(2)}) async-start(), calls=%async_computation.4 | async-start | bytes 19464192 | tf_op jit(solution)/shard_map/all_gather | solution.py:648
  169.8 695.3 %reduce-scatter.3.cloned.1.call-start = ((), (), s32[]{:S(2)}) async-start(), calls=%async_computation.5 | async-start | bytes 5013504 | tf_op jit(solution)/shard_map/reduce_scatter | solution.py:448
  255.6 36.1 %collective-permute-start.30 = (bf16[144,1024]{1,0:T(8,128)(2,1)S(1)}, bf16[144,1024]{1,0:T(8,128)(2,1)S(1)}, u32[]{:S(2)}, u32[]{:S(2)}) collective-permute-start(bf16[144,1024]{1,0:T(8,128)(2,1)S(1)} %get-tuple-element.391), channel_id=1, source_target_pairs={{0,8},{4,12},{8,0},{12,4},{1,9},{5,13},{9,1},{13,5},{2,10},{6,14},... | collective-permute-start | bytes 884744 | tf_op jit(solution)/shard_map/ppermute | solution.py:56
  309.9 42.7 %collective-permute-start.33 = (bf16[256,2048]{1,0:T(8,128)(2,1)S(1)}, bf16[256,2048]{1,0:T(8,128)(2,1)}, u32[]{:S(2)}, u32[]{:S(2)}) collective-permute-start(bf16[256,2048]{1,0:T(8,128)(2,1)S(1)} %fusion.52.k0.v0), channel_id=1, source_target_pairs={{0,2},{2,0},{1,3},{3,1},{4,6},{6,4},{5,7},{7,5},{8,10},{10,8},{9,1... | collective-permute-start | bytes 3145736 | tf_op jit(solution)/shard_map/ppermute | solution.py:56
  311.5 46.5 %collective-permute-start.32 = (bf16[256,2048]{1,0:T(8,128)(2,1)S(1)}, bf16[256,2048]{1,0:T(8,128)(2,1)S(1)}, u32[]{:S(2)}, u32[]{:S(2)}) collective-permute-start(bf16[256,2048]{1,0:T(8,128)(2,1)S(1)} %fusion.52.k0.v0), channel_id=1, source_target_pairs={{0,1},{1,0},{2,3},{3,2},{4,5},{5,4},{6,7},{7,6},{8,9},{9,8},{10,11... | collective-permute-start | bytes 3145736 | tf_op jit(solution)/shard_map/ppermute | solution.py:56
  442.6 42.6 %collective-permute-start.44 = (bf16[512,2816]{1,0:T(8,128)(2,1)}, bf16[512,2816]{1,0:T(8,128)(2,1)}, u32[]{:S(2)}, u32[]{:S(2)}) collective-permute-start(bf16[512,2816]{1,0:T(8,128)(2,1)} %convolution_convert_fusion.5), channel_id=1, source_target_pairs={{0,1},{1,0},{2,3},{3,2},{4,5},{5,4},{6,7},{7,6},{8,9},{9,8},{10,11... | collective-permute-start | bytes 8650760 | tf_op jit(solution)/shard_map/ppermute | solution.py:56
  498.4 46.2 %collective-permute-start.50 = (bf16[256,2816]{1,0:T(8,128)(2,1)S(1)}, bf16[256,2816]{1,0:T(8,128)(2,1)S(1)}, u32[]{:S(2)}, u32[]{:S(2)}) collective-permute-start(bf16[256,2816]{1,0:T(8,128)(2,1)S(1)} %fusion.44), channel_id=1, source_target_pairs={{0,2},{2,0},{1,3},{3,1},{4,6},{6,4},{5,7},{7,5},{8,10},{10,8},{9,1... | collective-permute-start | bytes 4325384 | tf_op jit(solution)/shard_map/ppermute | solution.py:56
  619.3 56.8 %collective-permute-start.61 = (bf16[256,1024]{1,0:T(8,128)(2,1)}, bf16[256,1024]{1,0:T(8,128)(2,1)}, u32[]{:S(2)}, u32[]{:S(2)}) collective-permute-start(bf16[256,1024]{1,0:T(8,128)(2,1)} %get-tuple-element.398), channel_id=1, source_target_pairs={{0,16},{16,0},{1,17},{17,1},{2,18},{18,2},{3,19},{19,3},{4,20},{20... | collective-permute-start | bytes 1572872 | tf_op jit(solution)/shard_map/ppermute | solution.py:234
  620.6 55.4 %collective-permute-start.60 = (bf16[256,2816]{1,0:T(8,128)(2,1)}, bf16[256,2816]{1,0:T(8,128)(2,1)}, u32[]{:S(2)}, u32[]{:S(2)}) collective-permute-start(bf16[256,2816]{1,0:T(8,128)(2,1)} %add_convert_fusion.7), channel_id=1, source_target_pairs={{0,16},{1,17},{2,18},{3,19},{4,20},{5,21},{6,22},{7,23},{8,24},{9,... | collective-permute-start | bytes 4325384 | tf_op jit(solution)/shard_map/ppermute | solution.py:386
  754.1 190.5 %reduce-scatter.5.cloned.1.call-start = ((), (), s32[]{:S(2)}) async-start(), calls=%async_computation.6 | async-start | bytes 2359296 | tf_op jit(solution)/shard_map/reduce_scatter | solution.py:448
  760.7 44.6 %collective-permute-start.71 = (bf16[256,2816]{1,0:T(8,128)(2,1)}, bf16[256,2816]{1,0:T(8,128)(2,1)}, u32[]{:S(2)}, u32[]{:S(2)}) collective-permute-start(bf16[256,2816]{1,0:T(8,128)(2,1)} %fusion.48), channel_id=1, source_target_pairs={{0,2},{2,0},{1,3},{3,1},{4,6},{6,4},{5,7},{7,5},{8,10},{10,8},{9,1... | collective-permute-start | bytes 4325384 | tf_op jit(solution)/shard_map/ppermute | solution.py:56
  869.2 164.1 %all-gather.12.cloned.1.call-start = ((), (), s32[]{:S(2)}) async-start(), calls=%async_computation.7 | async-start | bytes 2785280 | tf_op jit(solution)/shard_map/all_gather | solution.py:722
  869.4 155.0 %collective-permute-start.91 = (bf16[256,2816]{1,0:T(8,128)(2,1)}, bf16[256,2816]{1,0:T(8,128)(2,1)}, u32[]{:S(2)}, u32[]{:S(2)}) collective-permute-start(bf16[256,2816]{1,0:T(8,128)(2,1)} %add_convert_fusion.5), channel_id=1, source_target_pairs={{0,16},{1,17},{2,18},{3,19},{4,20},{5,21},{6,22},{7,23},{8,24},{9,... | collective-permute-start | bytes 4325384 | tf_op jit(solution)/shard_map/ppermute | solution.py:697
  877.9 43.2 %collective-permute-start.89 = (bf16[256,2816]{1,0:T(8,128)(2,1)}, bf16[256,2816]{1,0:T(8,128)(2,1)}, u32[]{:S(2)}, u32[]{:S(2)}) collective-permute-start(bf16[256,2816]{1,0:T(8,128)(2,1)} %fusion.49), channel_id=1, source_target_pairs={{0,2},{2,0},{1,3},{3,1},{4,6},{6,4},{5,7},{7,5},{8,10},{10,8},{9,1... | collective-permute-start | bytes 4325384 | tf_op jit(solution)/shard_map/ppermute | solution.py:56
  879.3 48.6 %collective-permute-start.79 = (bf16[272,1024]{1,0:T(8,128)(2,1)}, bf16[272,1024]{1,0:T(8,128)(2,1)}, u32[]{:S(2)}, u32[]{:S(2)}) collective-permute-start(bf16[272,1024]{1,0:T(8,128)(2,1)} %bitcast.383), channel_id=1, source_target_pairs={{0,16},{1,17},{2,18},{3,19},{4,20},{5,21},{6,22},{7,23},{8,24},{9,... | collective-permute-start | bytes 1671176 | tf_op jit(solution)/shard_map/ppermute | solution.py:712
  898.5 50.1 %collective-permute-start.81 = (bf16[4,144,1024]{2,1,0:T(8,128)(2,1)}, bf16[4,144,1024]{2,1,0:T(8,128)(2,1)}, u32[]{:S(2)}, u32[]{:S(2)}) collective-permute-start(bf16[4,144,1024]{2,1,0:T(8,128)(2,1)} %fusion.116), channel_id=1, source_target_pairs={{0,2},{2,0},{1,3},{3,1},{4,6},{6,4},{5,7},{7,5},{8,10},{10,8},{9,1... | collective-permute-start | bytes 3538952 | tf_op jit(solution)/shard_map/ppermute | solution.py:56
  916.7 75.8 %collective-permute-start.88 = (bf16[256,2816]{1,0:T(8,128)(2,1)}, bf16[256,2816]{1,0:T(8,128)(2,1)}, u32[]{:S(2)}, u32[]{:S(2)}) collective-permute-start(bf16[256,2816]{1,0:T(8,128)(2,1)} %fusion.51), channel_id=1, source_target_pairs={{16,0},{17,1},{18,2},{19,3},{20,4},{21,5},{22,6},{23,7},{24,8},{25... | collective-permute-start | bytes 4325384 | tf_op jit(solution)/shard_map/ppermute | solution.py:708
  926.6 97.8 %collective-permute-start.90 = (bf16[256,2816]{1,0:T(8,128)(2,1)}, bf16[256,2816]{1,0:T(8,128)(2,1)}, u32[]{:S(2)}, u32[]{:S(2)}) collective-permute-start(bf16[256,2816]{1,0:T(8,128)(2,1)} %fusion.50), channel_id=1, source_target_pairs={{16,0},{17,1},{18,2},{19,3},{20,4},{21,5},{22,6},{23,7},{24,8},{25... | collective-permute-start | bytes 4325384 | tf_op jit(solution)/shard_map/ppermute | solution.py:708
  944.6 43.7 %collective-permute-start.78 = (bf16[128,1024]{1,0:T(8,128)(2,1)}, bf16[128,1024]{1,0:T(8,128)(2,1)S(1)}, u32[]{:S(2)}, u32[]{:S(2)}) collective-permute-start(bf16[128,1024]{1,0:T(8,128)(2,1)} %bitcast.390), channel_id=1, source_target_pairs={{16,0},{17,1},{18,2},{19,3},{20,4},{21,5},{22,6},{23,7},{24,8},{25... | collective-permute-start | bytes 786440 | tf_op jit(solution)/shard_map/ppermute | solution.py:711
  952.6 44.9 %collective-permute-start.84 = (bf16[144,1024]{1,0:T(8,128)(2,1)}, bf16[144,1024]{1,0:T(8,128)(2,1)}, u32[]{:S(2)}, u32[]{:S(2)}) collective-permute-start(bf16[144,1024]{1,0:T(8,128)(2,1)} %get-tuple-element.355), channel_id=1, source_target_pairs={{0,12},{4,0},{8,4},{12,8},{1,13},{5,1},{9,5},{13,9},{2,14},{6,2},{... | collective-permute-start | bytes 884744 | tf_op jit(solution)/shard_map/ppermute | solution.py:56
  (217 other events, 3329.6 us)
Sparse Core Ops, SparseCore 0:
  79.5 112.4 all-gather.5
  194.9 111.4 all-gather.7
  308.8 105.5 all-gather.9
  754.1 110.8 reduce-scatter.2
  869.4 75.1 reduce-scatter.4
  992.7 21.8 all-gather.11

commit v4 on v3

--- a/solution.py
+++ b/solution.py
@@ -419,8 +419,8 @@
     grad_pair = (near_sum + outer_sum.astype(F32)).astype(BF16)
     index = lax.axis_index(INNER)
     given = dot_tn(normed, take(grad_pair, 1 - index, 0)).astype(BF16)
-    grad_pair, grad_normed, first_taken, given, small_early, waited[5] = lax.optimization_barrier(
-        (grad_pair, grad_normed, first_taken, given, small_early, waited[5])
+    grad_pair, grad_normed, first_taken, given, small_early = lax.optimization_barrier(
+        (grad_pair, grad_normed, first_taken, given, small_early)
     )
     second_taken = inner_swap(given)
     count = lax.axis_size(EXPERT)
@@ -439,8 +439,13 @@
         dense = jnp.concatenate([first_sum, second_sum], axis=1)
         grad_rows, dense = lax.optimization_barrier((grad_rows, dense))
     else:
-        dense = (reduce_dense(first_sum), fold_dense(second_sum))
+        second_sum, waited[5] = lax.optimization_barrier((second_sum, waited[5]))
+        dense = reduce_dense(first_sum)
     share_up = finish_expert(arrived, grad_up, up_inner, up_outer)
+    if source == 1:
+        hops = [lax.ppermute(value, SECTION, [(1, 0)]) for value in (share_gate, share_up, grad_rows)]
+        late, hops = fold_dense(second_sum, hops)
+        dense = (dense, late, hops)
     return grad_in, grad_rows, dense, (share_gate, share_up, share_down), hop_down, waited
 
 
@@ -448,7 +453,7 @@
     return lax.psum_scatter(blocks, (EXPERT, OUTER), scatter_dimension=0, tiled=False)
 
 
-def fold_dense(blocks):
+def fold_dense(blocks, joined):
     count = lax.axis_size(EXPERT)
     expert_index, outer_index = lax.axis_index(EXPERT), lax.axis_index(OUTER)
     blocks = blocks.reshape(count, 2, -1, blocks.shape[-1])
@@ -457,13 +462,13 @@
     for ahead in range(1, count):
         given = take(part, jnp.remainder(expert_index + ahead, count), 0)
         total = total + shift_to(given, EXPERT, ahead).astype(F32)
-    total = total.astype(BF16)
+    total, joined = lax.optimization_barrier((total.astype(BF16), joined))
     total = plus(total, lax.ppermute(total, SECTION, [(1, 0)]))
     partner = outer_swap(total)
     lower, even = outer_index == 0, lax.axis_index(INNER) == 0
     own = jnp.where(lower, jnp.stack([total, partner]), jnp.stack([partner, total]))
     other = inner_swap(own)
-    return jnp.where(even, jnp.stack([own, other]), jnp.stack([other, own]))
+    return jnp.where(even, jnp.stack([own, other]), jnp.stack([other, own])), joined
 
 
 def finish_expert(left, right, taken, last):
@@ -705,8 +710,7 @@
     )
     (hop_down_one, output_taken), shares_one, unused, hop_gate_one, unused, dense_one = waited
     hops_one = (hop_gate_one, hop_up_one, hop_down_one)
-    hop_gate_zero, hop_up_zero = (lax.ppermute(share, SECTION, [(1, 0)]) for share in shares_zero[:2])
-    early_zero, late_zero = dense_zero
+    early_zero, late_zero, (hop_gate_zero, hop_up_zero, grad_from_zero) = dense_zero
     half_count = dense_rows // 2
     early_taken = lax.ppermute(early_zero, SECTION, [(1, 0)])
     one_taken = lax.ppermute(dense_one, SECTION, [(0, 1)])
@@ -741,7 +745,6 @@
         )[None, :, None]
 
     section_output = both_micros(jnp.where(first_section, outputs[0], outputs[1]), output_taken)
-    grad_from_zero = lax.ppermute(grads, SECTION, [(1, 0)])
     grad_taken = jnp.where(first_section, grad_from_zero, grad_from_one).astype(F32)
     grad_kept = jnp.where(first_section, grad_in_zero, grad_in_one)
     input_gradient = both_micros(grad_kept, grad_taken)

time: 1060 us -> 1040 us (0.981)
  waiting for transfers between devices: 461 us -> 442 us
    ppermute x1, waiting for transfers between devices: 32.4 us -> 5.5 us  [shards(): early_taken = lax.ppermute(early_zero, SECTION, [(1, 0)])]
    ppermute x75, waiting for transfers between devices: 341 us -> 364 us  [shift_to(): lax.ppermute(value, axis, [(source, (source + steps) % count) for source...]
  transfers between devices with their start and end apart: 99 -> 99, of which waited for: 52 -> 50; matrix products, arithmetic and copies ran while one was open for 29% -> 30% of each run, Pallas kernels for 9% -> 9%
where the time goes in v4:
time: 1040 us
  waiting for transfers between devices  442 us (42%)
  matrix products  238 us (23%)
  starting transfers between devices  122 us (12%)
  Pallas kernels  94.2 us (9%)
  local copies, waits for them, and re-layouts  62.1 us (6%)
  other arithmetic  61 us (6%)
  between operations  17.2 us (2%)
    ppermute x75, waiting for transfers between devices, shift_to(): lax.ppermute(value, axis, [(source, (source + steps) % count) for source...  364 us
    dot_general x34, matrix products, dot_tn(): lax.dot_general(left, right, (((0,), (0,)), ((), ())), preferred_element_...  89.6 us
    dot_general x24, matrix products, matmul(): return jnp.dot(left, right, preferred_element_type=F32)  85.2 us
    ppermute x75, starting transfers between devices, shift_to(): lax.ppermute(value, axis, [(source, (source + steps) % count) for source...  66 us
    pallas_call x4, Pallas kernels, attention_backward(): pl.pallas_call(functools.partial(attention_backward_kernel, given=given i...  63.4 us
    dot_general x18, matrix products, dot_nt(): lax.dot_general(left, right, (((1,), (1,)), ((), ())), preferred_element_...  60.5 us
    reduce_scatter x2, waiting for transfers between devices, reduce_dense(): lax.psum_scatter(blocks, (EXPERT, OUTER), scatter_dimension=0, tiled=False)  32.5 us
    pallas_call x2, Pallas kernels, attention_forward(): pl.pallas_call(attention_forward_kernel, grid=(pairs,), in_specs=[chunk_s...  30.7 us
  transfers between devices with their start and end apart: 99, of which 50 were waited for; matrix products, arithmetic and copies ran while one was open for 30% of the time, Pallas kernels for 9%

profile of v4, /device:TPU:0, one launch (start us, length us, event | category | flops | bytes accessed | tf_op | source)
XLA Modules:
  0.0 1036.3 jit_solution(14462318248315650897)
XLA Ops:
  30.8 12.8 %collective-permute-done.2 = bf16[128,2048]{1,0:T(8,128)(2,1)S(1)} collective-permute-done((bf16[128,2048]{1,0:T(8,128)(2,1)S(1)}, bf16[128,2048]{1,0:T(8,128)(2,1)S(1)}, u32[]{:S(2)}, u32[]{:S(2)}) %collective-permute-start.2) | collective-permute-done | bytes 524320 | tf_op jit(solution)/shard_map/ppermute | solution.py:56
  43.6 13.6 %collective-permute-done.4 = bf16[128,2048]{1,0:T(8,128)(2,1)} collective-permute-done((bf16[128,2048]{1,0:T(8,128)(2,1)S(1)}, bf16[128,2048]{1,0:T(8,128)(2,1)}, u32[]{:S(2)}, u32[]{:S(2)}) %collective-permute-start.4) | collective-permute-done | bytes 524320 | tf_op jit(solution)/shard_map/ppermute | solution.py:56
  57.4 12.4 %collective-permute-done.6 = bf16[128,2048]{1,0:T(8,128)(2,1)S(1)} collective-permute-done((bf16[128,2048]{1,0:T(8,128)(2,1)}, bf16[128,2048]{1,0:T(8,128)(2,1)S(1)}, u32[]{:S(2)}, u32[]{:S(2)}) %collective-permute-start.6) | collective-permute-done | bytes 524320 | tf_op jit(solution)/shard_map/ppermute | solution.py:56
  130.0 15.5 %collective-permute-done.18 = bf16[128,2048]{1,0:T(8,128)(2,1)} collective-permute-done((bf16[128,2048]{1,0:T(8,128)(2,1)S(1)}, bf16[128,2048]{1,0:T(8,128)(2,1)}, u32[]{:S(2)}, u32[]{:S(2)}) %collective-permute-start.18) | collective-permute-done | bytes 524320 | tf_op jit(solution)/shard_map/ppermute | solution.py:56
  150.2 10.8 %collective-permute-done.20 = bf16[128,2048]{1,0:T(8,128)(2,1)S(1)} collective-permute-done((bf16[128,2048]{1,0:T(8,128)(2,1)}, bf16[128,2048]{1,0:T(8,128)(2,1)S(1)}, u32[]{:S(2)}, u32[]{:S(2)}) %collective-permute-start.20) | collective-permute-done | bytes 524320 | tf_op jit(solution)/shard_map/ppermute | solution.py:56
  180.4 15.4 %attention_forward.2 = (bf16[256,1024]{1,0:T(8,128)(2,1)}, f32[256,1024]{1,0:T(8,128)}, f32[8,2,256]{2,1,0:T(2,128)}) custom-call(bf16[256,1024]{1,0:T(8,128)(2,1)} %convolution_convert_fusion.13.q_ref, bf16[256,2048]{1,0:T(8,128)(2,1)} %copy-done.12, bf16[256,2048]{1,0:T(8,128)(2,1)} %copy-done.14, bf16[256,2048]{1,0:T(8,128)(2,1)} %copy-done.13, ...), custom_call_target="tpu_custom_call" | custom-call | flops 1073741824 | bytes 5242880 | tf_op jit(solution)/shard_map/attention_forward/pallas_call | solution.py:108
  212.5 19.4 %collective-permute-done.27 = bf16[144,1024]{1,0:T(8,128)(2,1)S(1)} collective-permute-done((bf16[144,1024]{1,0:T(8,128)(2,1)}, bf16[144,1024]{1,0:T(8,128)(2,1)S(1)}, u32[]{:S(2)}, u32[]{:S(2)}) %collective-permute-start.27) | collective-permute-done | bytes 294944 | tf_op jit(solution)/shard_map/ppermute | solution.py:56
  271.9 19.8 %collective-permute-done.30 = bf16[144,1024]{1,0:T(8,128)(2,1)S(1)} collective-permute-done((bf16[144,1024]{1,0:T(8,128)(2,1)S(1)}, bf16[144,1024]{1,0:T(8,128)(2,1)S(1)}, u32[]{:S(2)}, u32[]{:S(2)}) %collective-permute-start.30) | collective-permute-done | bytes 294944 | tf_op jit(solution)/shard_map/ppermute | solution.py:56
  293.2 13.2 %all-gather.8.cloned.1.call-done = bf16[1024,4096]{1,0:T(8,128)(2,1)} async-done(((bf16[32,4096]{1,0:T(8,128)(2,1)}), bf16[1024,4096]{1,0:T(8,128)(2,1)}) %all-gather.8.cloned.1.call-update) | async-done | bytes 8388624 | tf_op jit(solution)/shard_map/all_gather | solution.py:652
  311.4 41.1 %collective-permute-done.33.k2.v2.k0.v0 = bf16[256,2048]{1,0:T(8,128)(2,1)} collective-permute-done((bf16[256,2048]{1,0:T(8,128)(2,1)S(1)}, bf16[256,2048]{1,0:T(8,128)(2,1)}, u32[]{:S(2)}, u32[]{:S(2)}) %collective-permute-start.33) | collective-permute-done | bytes 1048608 | tf_op jit(solution)/shard_map/ppermute | solution.py:56
  359.0 15.4 %attention_forward.3 = (bf16[256,1024]{1,0:T(8,128)(2,1)}, f32[256,1024]{1,0:T(8,128)}, f32[8,2,256]{2,1,0:T(2,128)}) custom-call(bf16[256,1024]{1,0:T(8,128)(2,1)} %fusion.111.q_ref, bf16[256,2048]{1,0:T(8,128)(2,1)} %copy-done.15, bf16[256,2048]{1,0:T(8,128)(2,1)} %copy-done.16, bf16[256,2048]{1,0:T(8,128)(2,1)} %collective-permute-done.33.k2.v2.k0.v0, ...), custom_call_target="tpu_custom_call" | custom-call | flops 1073741824 | bytes 5242880 | tf_op jit(solution)/shard_map/attention_forward/pallas_call | solution.py:108
  387.2 19.3 %collective-permute-done.36 = bf16[144,1024]{1,0:T(8,128)(2,1)S(1)} collective-permute-done((bf16[144,1024]{1,0:T(8,128)(2,1)S(1)}, bf16[144,1024]{1,0:T(8,128)(2,1)S(1)}, u32[]{:S(2)}, u32[]{:S(2)}) %collective-permute-start.36) | collective-permute-done | bytes 294944 | tf_op jit(solution)/shard_map/ppermute | solution.py:56
  459.0 11.7 %collective-permute-done.39 = bf16[144,1024]{1,0:T(8,128)(2,1)} collective-permute-done((bf16[144,1024]{1,0:T(8,128)(2,1)}, bf16[144,1024]{1,0:T(8,128)(2,1)}, u32[]{:S(2)}, u32[]{:S(2)}) %collective-permute-start.39) | collective-permute-done | bytes 294944 | tf_op jit(solution)/shard_map/ppermute | solution.py:56
  472.0 13.3 %multiply_convert_fusion.1 = (bf16[576,2816]{1,0:T(8,128)(2,1)S(1)}, bf16[576,2816]{1,0:T(8,128)(2,1)S(1)}) fusion(f32[576,2816]{1,0:T(8,128)} %fusion.25, f32[576,2816]{1,0:T(8,128)} %get-tuple-element.452, bf16[576,1024]{1,0:T(8,128)(2,1)} %copy-done.44, bf16[1024,8448]{1,0:T(8,128)(2,1)} %all-gather.10.cloned.1.call-done), kind=kOutput, calls=%fused_computation.21 | convolution fusion | flops 3360817152 | bytes 26411008 | tf_op jit(solution)/shard_map/dot_general | solution.py:29
  532.7 11.7 %collective-permute-done.48 = bf16[144,1024]{1,0:T(8,128)(2,1)S(1)} collective-permute-done((bf16[144,1024]{1,0:T(8,128)(2,1)S(1)}, bf16[144,1024]{1,0:T(8,128)(2,1)S(1)}, u32[]{:S(2)}, u32[]{:S(2)}) %collective-permute-start.48) | collective-permute-done | bytes 294944 | tf_op jit(solution)/shard_map/ppermute | solution.py:56
  553.2 15.8 %attention_backward.4 = (f32[256,1024]{1,0:T(8,128)}, f32[2,256,1024]{2,1,0:T(8,128)}, bf16[2,256,1024]{2,1,0:T(8,128)(2,1)}, f32[16,2,512]{2,1,0:T(2,128)}) custom-call(bf16[256,1024]{1,0:T(8,128)(2,1)} %fusion.111.q_ref, bf16[256,1024]{1,0:T(8,128)(2,1)} %fusion.114.g_ref, f32[256,1024]{1,0:T(8,128)} %get-tuple-element.197.o_ref, ...), custom_call_target="tpu_custom_call" | custom-call | flops 1342177280 | bytes 9437184 | tf_op jit(solution)/shard_map/attention_backward/pallas_call | solution.py:203
  582.4 15.8 %attention_backward.5 = (bf16[256,1024]{1,0:T(8,128)(2,1)}, f32[2,256,1024]{2,1,0:T(8,128)}, bf16[2,256,1024]{2,1,0:T(8,128)(2,1)}, f32[16,2,512]{2,1,0:T(2,128)}) custom-call(bf16[256,1024]{1,0:T(8,128)(2,1)} %fusion.111.q_ref, bf16[256,1024]{1,0:T(8,128)(2,1)} %fusion.114.g_ref, f32[256,1024]{1,0:T(8,128)} %get-tuple-element.197.o_ref, ...), custom_call_target="tpu_custom_call" | custom-call | flops 1342177280 | bytes 9437184 | tf_op jit(solution)/shard_map/attention_backward/pallas_call | solution.py:203
  656.1 19.8 %collective-permute-done.58 = bf16[144,1024]{1,0:T(8,128)(2,1)S(1)} collective-permute-done((bf16[144,1024]{1,0:T(8,128)(2,1)S(1)}, bf16[144,1024]{1,0:T(8,128)(2,1)S(1)}, u32[]{:S(2)}, u32[]{:S(2)}) %collective-permute-start.58) | collective-permute-done | bytes 294944 | tf_op jit(solution)/shard_map/ppermute | solution.py:56
  683.2 12.1 %multiply_convert_fusion = (bf16[576,2816]{1,0:T(8,128)(2,1)S(1)}, bf16[576,2816]{1,0:T(8,128)(2,1)S(1)}) fusion(f32[576,2816]{1,0:T(8,128)} %fusion.37, f32[576,2816]{1,0:T(8,128)} %get-tuple-element.442, bf16[576,1024]{1,0:T(8,128)(2,1)S(1)} %pad_maximum_fusion.8, bf16[1024,8448]{1,0:T(8,128)(2,1)} %all-gather.6.cloned.1.call-done), kind=kOutput, calls=%fused_computation.20 | convolution fusion | flops 3360817152 | bytes 26411008 | tf_op jit(solution)/shard_map/dot_general | solution.py:29
  772.6 15.9 %attention_backward.6 = (f32[256,1024]{1,0:T(8,128)}, f32[2,256,1024]{2,1,0:T(8,128)}, bf16[2,256,1024]{2,1,0:T(8,128)(2,1)}, f32[16,2,512]{2,1,0:T(2,128)}) custom-call(bf16[256,1024]{1,0:T(8,128)(2,1)} %convolution_convert_fusion.13.q_ref, bf16[256,1024]{1,0:T(8,128)(2,1)} %fusion.108.g_ref, f32[256,1024]{1,0:T(8,128)} %get-tuple-element.253.o_ref, ...), custom_call_target="tpu_custom_call" | custom-call | flops 1342177280 | bytes 9437184 | tf_op jit(solution)/shard_map/attention_backward/pallas_call | solution.py:203
  791.5 13.8 %collective-permute-done.71 = bf16[256,2816]{1,0:T(8,128)(2,1)} collective-permute-done((bf16[256,2816]{1,0:T(8,128)(2,1)}, bf16[256,2816]{1,0:T(8,128)(2,1)}, u32[]{:S(2)}, u32[]{:S(2)}) %collective-permute-start.71) | collective-permute-done | bytes 1441824 | tf_op jit(solution)/shard_map/ppermute | solution.py:56
  808.5 15.9 %attention_backward.7 = (bf16[256,1024]{1,0:T(8,128)(2,1)}, f32[2,256,1024]{2,1,0:T(8,128)}, bf16[2,256,1024]{2,1,0:T(8,128)(2,1)}, f32[16,2,512]{2,1,0:T(2,128)}) custom-call(bf16[256,1024]{1,0:T(8,128)(2,1)} %convolution_convert_fusion.13.q_ref, bf16[256,1024]{1,0:T(8,128)(2,1)} %fusion.108.g_ref, f32[256,1024]{1,0:T(8,128)} %get-tuple-element.253.o_ref, ...), custom_call_target="tpu_custom_call" | custom-call | flops 1342177280 | bytes 9437184 | tf_op jit(solution)/shard_map/attention_backward/pallas_call | solution.py:203
  874.2 24.3 %collective-permute-done.82 = bf16[256,2816]{1,0:T(8,128)(2,1)} collective-permute-done((bf16[256,2816]{1,0:T(8,128)(2,1)}, bf16[256,2816]{1,0:T(8,128)(2,1)}, u32[]{:S(2)}, u32[]{:S(2)}) %collective-permute-start.82) | collective-permute-done | bytes 1441824 | tf_op jit(solution)/shard_map/ppermute | solution.py:56
  911.7 32.5 %reduce-scatter.5.cloned.1.call-done = bf16[1,128,1024]{2,1,0:T(8,128)(2,1)} async-done(((bf16[8,128,1024]{2,1,0:T(8,128)(2,1)}), bf16[1,128,1024]{2,1,0:T(8,128)(2,1)}) %reduce-scatter.5.cloned.1.call-update) | async-done | bytes 262160 | tf_op jit(solution)/shard_map/reduce_scatter | solution.py:453
  (735 shorter events, 607.7 us)
Async XLA Ops:
  7.2 224.7 %all-gather.6.cloned.1.call-start = ((), (), s32[]{:S(2)}) async-start(), calls=%async_computation.2 | async-start | bytes 19464192 | tf_op jit(solution)/shard_map/all_gather | solution.py:651
  25.6 50.1 %collective-permute-start.7 = (bf16[128,8448]{1,0:T(8,128)(2,1)}, bf16[128,8448]{1,0:T(8,128)(2,1)}, u32[]{:S(2)}, u32[]{:S(2)}) collective-permute-start(bf16[128,8448]{1,0:T(8,128)(2,1)} %pad_maximum_fusion), channel_id=1, source_target_pairs={{0,16},{16,0},{1,17},{17,1},{2,18},{18,2},{3,19},{19,3},{4,20},{20... | collective-permute-start | bytes 6488072 | tf_op jit(solution)/shard_map/ppermute | solution.py:234
  79.4 226.9 %all-gather.8.cloned.1.call-start = ((), (), s32[]{:S(2)}) async-start(), calls=%async_computation.3 | async-start | bytes 8650752 | tf_op jit(solution)/shard_map/all_gather | solution.py:652
  117.5 48.0 %collective-permute-start.22 = (bf16[256,2048]{1,0:T(8,128)(2,1)S(1)}, bf16[256,2048]{1,0:T(8,128)(2,1)S(1)}, u32[]{:S(2)}, u32[]{:S(2)}) collective-permute-start(bf16[256,2048]{1,0:T(8,128)(2,1)S(1)} %convolution_convert_fusion.6.k0.v0), channel_id=1, source_target_pairs={{0,2},{2,0},{1,3},{3,1},{4,6},{6,4},{5,7},{7,5},{8,10},{10,8},{9,1... | collective-permute-start | bytes 3145736 | tf_op jit(solution)/shard_map/ppermute | solution.py:56
  169.0 245.5 %all-gather.10.cloned.1.call-start = ((), (), s32[]{:S(2)}) async-start(), calls=%async_computation.4 | async-start | bytes 19464192 | tf_op jit(solution)/shard_map/all_gather | solution.py:653
  169.7 701.5 %reduce-scatter.3.cloned.1.call-start = ((), (), s32[]{:S(2)}) async-start(), calls=%async_computation.5 | async-start | bytes 5013504 | tf_op jit(solution)/shard_map/reduce_scatter | solution.py:453
  255.6 36.1 %collective-permute-start.30 = (bf16[144,1024]{1,0:T(8,128)(2,1)S(1)}, bf16[144,1024]{1,0:T(8,128)(2,1)S(1)}, u32[]{:S(2)}, u32[]{:S(2)}) collective-permute-start(bf16[144,1024]{1,0:T(8,128)(2,1)S(1)} %get-tuple-element.401), channel_id=1, source_target_pairs={{0,8},{4,12},{8,0},{12,4},{1,9},{5,13},{9,1},{13,5},{2,10},{6,14},... | collective-permute-start | bytes 884744 | tf_op jit(solution)/shard_map/ppermute | solution.py:56
  309.9 42.7 %collective-permute-start.33 = (bf16[256,2048]{1,0:T(8,128)(2,1)S(1)}, bf16[256,2048]{1,0:T(8,128)(2,1)}, u32[]{:S(2)}, u32[]{:S(2)}) collective-permute-start(bf16[256,2048]{1,0:T(8,128)(2,1)S(1)} %fusion.53.k0.v0), channel_id=1, source_target_pairs={{0,2},{2,0},{1,3},{3,1},{4,6},{6,4},{5,7},{7,5},{8,10},{10,8},{9,1... | collective-permute-start | bytes 3145736 | tf_op jit(solution)/shard_map/ppermute | solution.py:56
  311.4 46.5 %collective-permute-start.32 = (bf16[256,2048]{1,0:T(8,128)(2,1)S(1)}, bf16[256,2048]{1,0:T(8,128)(2,1)S(1)}, u32[]{:S(2)}, u32[]{:S(2)}) collective-permute-start(bf16[256,2048]{1,0:T(8,128)(2,1)S(1)} %fusion.53.k0.v0), channel_id=1, source_target_pairs={{0,1},{1,0},{2,3},{3,2},{4,5},{5,4},{6,7},{7,6},{8,9},{9,8},{10,11... | collective-permute-start | bytes 3145736 | tf_op jit(solution)/shard_map/ppermute | solution.py:56
  442.6 42.7 %collective-permute-start.44 = (bf16[512,2816]{1,0:T(8,128)(2,1)}, bf16[512,2816]{1,0:T(8,128)(2,1)}, u32[]{:S(2)}, u32[]{:S(2)}) collective-permute-start(bf16[512,2816]{1,0:T(8,128)(2,1)} %convolution_convert_fusion.5), channel_id=1, source_target_pairs={{0,1},{1,0},{2,3},{3,2},{4,5},{5,4},{6,7},{7,6},{8,9},{9,8},{10,11... | collective-permute-start | bytes 8650760 | tf_op jit(solution)/shard_map/ppermute | solution.py:56
  498.4 46.1 %collective-permute-start.50 = (bf16[256,2816]{1,0:T(8,128)(2,1)S(1)}, bf16[256,2816]{1,0:T(8,128)(2,1)S(1)}, u32[]{:S(2)}, u32[]{:S(2)}) collective-permute-start(bf16[256,2816]{1,0:T(8,128)(2,1)S(1)} %fusion.45), channel_id=1, source_target_pairs={{0,2},{2,0},{1,3},{3,1},{4,6},{6,4},{5,7},{7,5},{8,10},{10,8},{9,1... | collective-permute-start | bytes 4325384 | tf_op jit(solution)/shard_map/ppermute | solution.py:56
  619.2 56.7 %collective-permute-start.61 = (bf16[256,1024]{1,0:T(8,128)(2,1)}, bf16[256,1024]{1,0:T(8,128)(2,1)}, u32[]{:S(2)}, u32[]{:S(2)}) collective-permute-start(bf16[256,1024]{1,0:T(8,128)(2,1)} %get-tuple-element.408), channel_id=1, source_target_pairs={{0,16},{16,0},{1,17},{17,1},{2,18},{18,2},{3,19},{19,3},{4,20},{20... | collective-permute-start | bytes 1572872 | tf_op jit(solution)/shard_map/ppermute | solution.py:234
  620.6 55.4 %collective-permute-start.60 = (bf16[256,2816]{1,0:T(8,128)(2,1)}, bf16[256,2816]{1,0:T(8,128)(2,1)}, u32[]{:S(2)}, u32[]{:S(2)}) collective-permute-start(bf16[256,2816]{1,0:T(8,128)(2,1)} %add_convert_fusion.7), channel_id=1, source_target_pairs={{0,16},{1,17},{2,18},{3,19},{4,20},{5,21},{6,22},{7,23},{8,24},{9,... | collective-permute-start | bytes 4325384 | tf_op jit(solution)/shard_map/ppermute | solution.py:386
  718.1 35.8 %collective-permute-start.68 = (bf16[256,2816]{1,0:T(8,128)(2,1)S(1)}, bf16[256,2816]{1,0:T(8,128)(2,1)}, u32[]{:S(2)}, u32[]{:S(2)}) collective-permute-start(bf16[256,2816]{1,0:T(8,128)(2,1)S(1)} %fusion.48), channel_id=1, source_target_pairs={{0,2},{2,0},{1,3},{3,1},{4,6},{6,4},{5,7},{7,5},{8,10},{10,8},{9,1... | collective-permute-start | bytes 4325384 | tf_op jit(solution)/shard_map/ppermute | solution.py:56
  754.1 190.2 %reduce-scatter.5.cloned.1.call-start = ((), (), s32[]{:S(2)}) async-start(), calls=%async_computation.6 | async-start | bytes 2359296 | tf_op jit(solution)/shard_map/reduce_scatter | solution.py:453
  760.7 44.5 %collective-permute-start.71 = (bf16[256,2816]{1,0:T(8,128)(2,1)}, bf16[256,2816]{1,0:T(8,128)(2,1)}, u32[]{:S(2)}, u32[]{:S(2)}) collective-permute-start(bf16[256,2816]{1,0:T(8,128)(2,1)} %fusion.49), channel_id=1, source_target_pairs={{0,2},{2,0},{1,3},{3,1},{4,6},{6,4},{5,7},{7,5},{8,10},{10,8},{9,1... | collective-permute-start | bytes 4325384 | tf_op jit(solution)/shard_map/ppermute | solution.py:56
  851.9 167.2 %all-gather.12.cloned.1.call-start = ((), (), s32[]{:S(2)}) async-start(), calls=%async_computation.7 | async-start | bytes 2785280 | tf_op jit(solution)/shard_map/all_gather | solution.py:726
  855.3 109.7 %collective-permute-start.92 = (bf16[256,2816]{1,0:T(8,128)(2,1)}, bf16[256,2816]{1,0:T(8,128)(2,1)}, u32[]{:S(2)}, u32[]{:S(2)}) collective-permute-start(bf16[256,2816]{1,0:T(8,128)(2,1)} %add_convert_fusion.4), channel_id=1, source_target_pairs={{16,0},{17,1},{18,2},{19,3},{20,4},{21,5},{22,6},{23,7},{24,8},{25... | collective-permute-start | bytes 4325384 | tf_op jit(solution)/shard_map/ppermute | solution.py:386
  856.6 141.9 %collective-permute-start.81 = (bf16[256,2816]{1,0:T(8,128)(2,1)}, bf16[256,2816]{1,0:T(8,128)(2,1)}, u32[]{:S(2)}, u32[]{:S(2)}) collective-permute-start(bf16[256,2816]{1,0:T(8,128)(2,1)} %fusion.52), channel_id=1, source_target_pairs={{16,0},{17,1},{18,2},{19,3},{20,4},{21,5},{22,6},{23,7},{24,8},{25... | collective-permute-start | bytes 4325384 | tf_op jit(solution)/shard_map/ppermute | solution.py:446
  858.1 40.4 %collective-permute-start.82 = (bf16[256,2816]{1,0:T(8,128)(2,1)}, bf16[256,2816]{1,0:T(8,128)(2,1)}, u32[]{:S(2)}, u32[]{:S(2)}) collective-permute-start(bf16[256,2816]{1,0:T(8,128)(2,1)} %fusion.50), channel_id=1, source_target_pairs={{0,2},{2,0},{1,3},{3,1},{4,6},{6,4},{5,7},{7,5},{8,10},{10,8},{9,1... | collective-permute-start | bytes 4325384 | tf_op jit(solution)/shard_map/ppermute | solution.py:56
  873.6 83.4 %collective-permute-start.77 = (bf16[4,144,1024]{2,1,0:T(8,128)(2,1)}, bf16[4,144,1024]{2,1,0:T(8,128)(2,1)}, u32[]{:S(2)}, u32[]{:S(2)}) collective-permute-start(bf16[4,144,1024]{2,1,0:T(8,128)(2,1)} %dynamic-slice_bitcast_fusion), channel_id=1, source_target_pairs={{0,2},{2,0},{1,3},{3,1},{4,6},{6,4},{5,7},{7,5},{8,10},{10,8},{9,1... | collective-permute-start | bytes 3538952 | tf_op jit(solution)/shard_map/ppermute | solution.py:56
  904.0 51.8 %collective-permute-start.87 = (bf16[272,1024]{1,0:T(8,128)(2,1)S(1)}, bf16[272,1024]{1,0:T(8,128)(2,1)}, u32[]{:S(2)}, u32[]{:S(2)}) collective-permute-start(bf16[272,1024]{1,0:T(8,128)(2,1)S(1)} %bitcast.382), channel_id=1, source_target_pairs={{0,16},{1,17},{2,18},{3,19},{4,20},{5,21},{6,22},{7,23},{8,24},{9,... | collective-permute-start | bytes 1671176 | tf_op jit(solution)/shard_map/ppermute | solution.py:716
  954.5 45.9 %collective-permute-start.83 = (bf16[256,2816]{1,0:T(8,128)(2,1)}, bf16[256,2816]{1,0:T(8,128)(2,1)}, u32[]{:S(2)}, u32[]{:S(2)}) collective-permute-start(bf16[256,2816]{1,0:T(8,128)(2,1)} %fusion.51), channel_id=1, source_target_pairs={{16,0},{17,1},{18,2},{19,3},{20,4},{21,5},{22,6},{23,7},{24,8},{25... | collective-permute-start | bytes 4325384 | tf_op jit(solution)/shard_map/ppermute | solution.py:446
  965.0 44.5 %collective-permute-start.91 = (bf16[256,2816]{1,0:T(8,128)(2,1)}, bf16[256,2816]{1,0:T(8,128)(2,1)}, u32[]{:S(2)}, u32[]{:S(2)}) collective-permute-start(bf16[256,2816]{1,0:T(8,128)(2,1)} %add_convert_fusion.5), channel_id=1, source_target_pairs={{0,16},{1,17},{2,18},{3,19},{4,20},{5,21},{6,22},{7,23},{8,24},{9,... | collective-permute-start | bytes 4325384 | tf_op jit(solution)/shard_map/ppermute | solution.py:702
  (220 other events, 3236.1 us)
Sparse Core Ops, SparseCore 0:
  79.5 112.4 all-gather.5
  194.9 111.4 all-gather.7
  308.8 105.6 all-gather.9
  754.1 110.5 reduce-scatter.2
  869.1 75.1 reduce-scatter.4
  965.1 25.0 all-gather.11

commit v5 on v4

--- a/solution.py
+++ b/solution.py
@@ -346,8 +346,20 @@
     grad_hidden = matmul(received, weights["down"])
     unused_value, pull_gelu = jax.vjp(gated_gelu, gate_part, up_part)
     grad_gate, grad_up = pull_gelu(grad_hidden)
-    grad_gate, grad_up, down_inner, returned = lax.optimization_barrier(
-        (grad_gate.astype(BF16), grad_up.astype(BF16), down_inner, returned)
+    grad_gate, grad_up, down_inner = lax.optimization_barrier(
+        (grad_gate.astype(BF16), grad_up.astype(BF16), down_inner)
+    )
+    grad_gate, grad_up, down_given = lax.optimization_barrier(
+        (grad_gate, grad_up, for_outer(received, hidden, down_inner))
+    )
+    down_outer = outer_swap(down_given)
+    gate_given, up_given, grad_gate, grad_up = lax.optimization_barrier(
+        (for_inner(arrived, grad_gate), for_inner(arrived, grad_up), grad_gate, grad_up)
+    )
+    gate_inner, up_inner = from_inner(gate_given), from_inner(up_given)
+    grad_arrived = (dot_nt(grad_gate, weights["gate"]) + dot_nt(grad_up, weights["up"])).astype(BF16)
+    grad_arrived, gate_inner, up_inner, returned = lax.optimization_barrier(
+        (grad_arrived, gate_inner, up_inner, returned)
     )
     products = jnp.where(spots, dot_nt(grad_rows, returned), 0.0)
     grad_gates = jnp.dot(products, members, precision=lax.Precision.HIGHEST, preferred_element_type=F32)
@@ -355,16 +367,6 @@
     grad_logits = grad_logits.astype(BF16)
     term_router = dot_tn(mixed_in, grad_logits)
 
-    grad_gate, grad_up, down_given = lax.optimization_barrier(
-        (grad_gate, grad_up, for_outer(received, hidden, down_inner))
-    )
-    down_outer = outer_swap(down_given)
-    gate_given, up_given, grad_gate, grad_up = lax.optimization_barrier(
-        (for_inner(arrived, grad_gate), for_inner(arrived, grad_up), grad_gate, grad_up)
-    )
-    gate_inner, up_inner = from_inner(gate_given), from_inner(up_given)
-    grad_arrived = (dot_nt(grad_gate, weights["gate"]) + dot_nt(grad_up, weights["up"])).astype(BF16)
-    grad_arrived, gate_inner, up_inner = lax.optimization_barrier((grad_arrived, gate_inner, up_inner))
     back_rows = send_slots(grad_arrived.reshape(expert_count, -1, width), -1)
     gate_given = for_outer(arrived, grad_gate, gate_inner)
     up_given = for_outer(arrived, grad_up, up_inner)

time: 1040 us -> 1050 us (level)
  transfers between devices with their start and end apart: 99 -> 99, of which waited for: 50 -> 48; matrix products, arithmetic and copies ran while one was open for 30% -> 30% of each run, Pallas kernels for 9% -> 9%
where the time goes in v5:
time: 1050 us; the launch traced here: 1040 us
  waiting for transfers between devices  437 us (42%)
  matrix products  240 us (23%)
  starting transfers between devices  124 us (12%)
  Pallas kernels  93.9 us (9%)
  other arithmetic  62.4 us (6%)
  local copies, waits for them, and re-layouts  61.9 us (6%)
  between operations  17.4 us (2%)
    ppermute x75, waiting for transfers between devices, shift_to(): lax.ppermute(value, axis, [(source, (source + steps) % count) for source...  359 us
    dot_general x34, matrix products, dot_tn(): lax.dot_general(left, right, (((0,), (0,)), ((), ())), preferred_element_...  91.6 us
    dot_general x24, matrix products, matmul(): return jnp.dot(left, right, preferred_element_type=F32)  85.3 us
    ppermute x75, starting transfers between devices, shift_to(): lax.ppermute(value, axis, [(source, (source + steps) % count) for source...  68.4 us
    pallas_call x4, Pallas kernels, attention_backward(): pl.pallas_call(functools.partial(attention_backward_kernel, given=given i...  63.2 us
    dot_general x18, matrix products, dot_nt(): lax.dot_general(left, right, (((1,), (1,)), ((), ())), preferred_element_...  61.2 us
    reduce_scatter x2, waiting for transfers between devices, reduce_dense(): lax.psum_scatter(blocks, (EXPERT, OUTER), scatter_dimension=0, tiled=False)  33.4 us
    pallas_call x2, Pallas kernels, attention_forward(): pl.pallas_call(attention_forward_kernel, grid=(pairs,), in_specs=[chunk_s...  30.7 us
  transfers between devices with their start and end apart: 99, of which 48 were waited for; matrix products, arithmetic and copies ran while one was open for 30% of the time, Pallas kernels for 9%

profile of v5, /device:TPU:0, one launch (start us, length us, event | category | flops | bytes accessed | tf_op | source)
XLA Modules:
  0.0 1037.8 jit_solution(3296536972856011834)
XLA Ops:
  30.8 12.8 %collective-permute-done.2 = bf16[128,2048]{1,0:T(8,128)(2,1)S(1)} collective-permute-done((bf16[128,2048]{1,0:T(8,128)(2,1)S(1)}, bf16[128,2048]{1,0:T(8,128)(2,1)S(1)}, u32[]{:S(2)}, u32[]{:S(2)}) %collective-permute-start.2) | collective-permute-done | bytes 524320 | tf_op jit(solution)/shard_map/ppermute | solution.py:56
  43.6 13.6 %collective-permute-done.4 = bf16[128,2048]{1,0:T(8,128)(2,1)} collective-permute-done((bf16[128,2048]{1,0:T(8,128)(2,1)S(1)}, bf16[128,2048]{1,0:T(8,128)(2,1)}, u32[]{:S(2)}, u32[]{:S(2)}) %collective-permute-start.4) | collective-permute-done | bytes 524320 | tf_op jit(solution)/shard_map/ppermute | solution.py:56
  57.4 12.4 %collective-permute-done.6 = bf16[128,2048]{1,0:T(8,128)(2,1)S(1)} collective-permute-done((bf16[128,2048]{1,0:T(8,128)(2,1)}, bf16[128,2048]{1,0:T(8,128)(2,1)S(1)}, u32[]{:S(2)}, u32[]{:S(2)}) %collective-permute-start.6) | collective-permute-done | bytes 524320 | tf_op jit(solution)/shard_map/ppermute | solution.py:56
  130.1 15.5 %collective-permute-done.18 = bf16[128,2048]{1,0:T(8,128)(2,1)} collective-permute-done((bf16[128,2048]{1,0:T(8,128)(2,1)S(1)}, bf16[128,2048]{1,0:T(8,128)(2,1)}, u32[]{:S(2)}, u32[]{:S(2)}) %collective-permute-start.18) | collective-permute-done | bytes 524320 | tf_op jit(solution)/shard_map/ppermute | solution.py:56
  150.2 10.9 %collective-permute-done.20 = bf16[128,2048]{1,0:T(8,128)(2,1)S(1)} collective-permute-done((bf16[128,2048]{1,0:T(8,128)(2,1)}, bf16[128,2048]{1,0:T(8,128)(2,1)S(1)}, u32[]{:S(2)}, u32[]{:S(2)}) %collective-permute-start.20) | collective-permute-done | bytes 524320 | tf_op jit(solution)/shard_map/ppermute | solution.py:56
  180.5 15.4 %attention_forward.2 = (bf16[256,1024]{1,0:T(8,128)(2,1)}, f32[256,1024]{1,0:T(8,128)}, f32[8,2,256]{2,1,0:T(2,128)}) custom-call(bf16[256,1024]{1,0:T(8,128)(2,1)} %convolution_convert_fusion.13.q_ref, bf16[256,2048]{1,0:T(8,128)(2,1)} %copy-done.15, bf16[256,2048]{1,0:T(8,128)(2,1)} %copy-done.17, bf16[256,2048]{1,0:T(8,128)(2,1)} %copy-done.16, ...), custom_call_target="tpu_custom_call" | custom-call | flops 1073741824 | bytes 5242880 | tf_op jit(solution)/shard_map/attention_forward/pallas_call | solution.py:108
  212.7 19.4 %collective-permute-done.27 = bf16[144,1024]{1,0:T(8,128)(2,1)S(1)} collective-permute-done((bf16[144,1024]{1,0:T(8,128)(2,1)}, bf16[144,1024]{1,0:T(8,128)(2,1)S(1)}, u32[]{:S(2)}, u32[]{:S(2)}) %collective-permute-start.27) | collective-permute-done | bytes 294944 | tf_op jit(solution)/shard_map/ppermute | solution.py:56
  272.1 19.7 %collective-permute-done.30 = bf16[144,1024]{1,0:T(8,128)(2,1)S(1)} collective-permute-done((bf16[144,1024]{1,0:T(8,128)(2,1)S(1)}, bf16[144,1024]{1,0:T(8,128)(2,1)S(1)}, u32[]{:S(2)}, u32[]{:S(2)}) %collective-permute-start.30) | collective-permute-done | bytes 294944 | tf_op jit(solution)/shard_map/ppermute | solution.py:56
  293.3 13.2 %all-gather.8.cloned.1.call-done = bf16[1024,4096]{1,0:T(8,128)(2,1)} async-done(((bf16[32,4096]{1,0:T(8,128)(2,1)}), bf16[1024,4096]{1,0:T(8,128)(2,1)}) %all-gather.8.cloned.1.call-update) | async-done | bytes 8388624 | tf_op jit(solution)/shard_map/all_gather | solution.py:654
  311.5 41.2 %collective-permute-done.33.k2.v2.k0.v0 = bf16[256,2048]{1,0:T(8,128)(2,1)} collective-permute-done((bf16[256,2048]{1,0:T(8,128)(2,1)S(1)}, bf16[256,2048]{1,0:T(8,128)(2,1)}, u32[]{:S(2)}, u32[]{:S(2)}) %collective-permute-start.33) | collective-permute-done | bytes 1048608 | tf_op jit(solution)/shard_map/ppermute | solution.py:56
  359.1 15.4 %attention_forward.3 = (bf16[256,1024]{1,0:T(8,128)(2,1)}, f32[256,1024]{1,0:T(8,128)}, f32[8,2,256]{2,1,0:T(2,128)}) custom-call(bf16[256,1024]{1,0:T(8,128)(2,1)} %fusion.111.q_ref, bf16[256,2048]{1,0:T(8,128)(2,1)} %copy-done.18, bf16[256,2048]{1,0:T(8,128)(2,1)} %copy-done.19, bf16[256,2048]{1,0:T(8,128)(2,1)} %collective-permute-done.33.k2.v2.k0.v0, ...), custom_call_target="tpu_custom_call" | custom-call | flops 1073741824 | bytes 5242880 | tf_op jit(solution)/shard_map/attention_forward/pallas_call | solution.py:108
  387.3 19.3 %collective-permute-done.36 = bf16[144,1024]{1,0:T(8,128)(2,1)S(1)} collective-permute-done((bf16[144,1024]{1,0:T(8,128)(2,1)S(1)}, bf16[144,1024]{1,0:T(8,128)(2,1)S(1)}, u32[]{:S(2)}, u32[]{:S(2)}) %collective-permute-start.36) | collective-permute-done | bytes 294944 | tf_op jit(solution)/shard_map/ppermute | solution.py:56
  443.7 13.4 %multiply_convert_fusion.1 = (bf16[576,2816]{1,0:T(8,128)(2,1)S(1)}, bf16[576,2816]{1,0:T(8,128)(2,1)S(1)}) fusion(f32[576,2816]{1,0:T(8,128)} %copy-done.149, f32[576,2816]{1,0:T(8,128)} %get-tuple-element.452, bf16[576,1024]{1,0:T(8,128)(2,1)} %copy-done.45, bf16[1024,8448]{1,0:T(8,128)(2,1)} %all-gather.10.cloned.1.call-done), kind=kOutput, calls=%fused_computation.21 | convolution fusion | flops 3360817152 | bytes 26411008 | tf_op jit(solution)/shard_map/dot_general | solution.py:29
  490.0 11.7 %collective-permute-done.39 = bf16[144,1024]{1,0:T(8,128)(2,1)} collective-permute-done((bf16[144,1024]{1,0:T(8,128)(2,1)}, bf16[144,1024]{1,0:T(8,128)(2,1)}, u32[]{:S(2)}, u32[]{:S(2)}) %collective-permute-start.39) | collective-permute-done | bytes 294944 | tf_op jit(solution)/shard_map/ppermute | solution.py:56
  556.3 15.7 %attention_backward.4 = (f32[256,1024]{1,0:T(8,128)}, f32[2,256,1024]{2,1,0:T(8,128)}, bf16[2,256,1024]{2,1,0:T(8,128)(2,1)}, f32[16,2,512]{2,1,0:T(2,128)}) custom-call(bf16[256,1024]{1,0:T(8,128)(2,1)} %fusion.111.q_ref, bf16[256,1024]{1,0:T(8,128)(2,1)} %fusion.114.g_ref, f32[256,1024]{1,0:T(8,128)} %get-tuple-element.197.o_ref, ...), custom_call_target="tpu_custom_call" | custom-call | flops 1342177280 | bytes 9437184 | tf_op jit(solution)/shard_map/attention_backward/pallas_call | solution.py:203
  584.6 15.8 %attention_backward.5 = (bf16[256,1024]{1,0:T(8,128)(2,1)}, f32[2,256,1024]{2,1,0:T(8,128)}, bf16[2,256,1024]{2,1,0:T(8,128)(2,1)}, f32[16,2,512]{2,1,0:T(2,128)}) custom-call(bf16[256,1024]{1,0:T(8,128)(2,1)} %fusion.111.q_ref, bf16[256,1024]{1,0:T(8,128)(2,1)} %fusion.114.g_ref, f32[256,1024]{1,0:T(8,128)} %get-tuple-element.197.o_ref, ...), custom_call_target="tpu_custom_call" | custom-call | flops 1342177280 | bytes 9437184 | tf_op jit(solution)/shard_map/attention_backward/pallas_call | solution.py:203
  658.8 19.6 %collective-permute-done.58 = bf16[144,1024]{1,0:T(8,128)(2,1)S(1)} collective-permute-done((bf16[144,1024]{1,0:T(8,128)(2,1)S(1)}, bf16[144,1024]{1,0:T(8,128)(2,1)S(1)}, u32[]{:S(2)}, u32[]{:S(2)}) %collective-permute-start.58) | collective-permute-done | bytes 294944 | tf_op jit(solution)/shard_map/ppermute | solution.py:56
  684.1 12.1 %multiply_convert_fusion = (bf16[576,2816]{1,0:T(8,128)(2,1)S(1)}, bf16[576,2816]{1,0:T(8,128)(2,1)S(1)}) fusion(f32[576,2816]{1,0:T(8,128)} %fusion.37, f32[576,2816]{1,0:T(8,128)} %get-tuple-element.442, bf16[576,1024]{1,0:T(8,128)(2,1)S(1)} %pad_maximum_fusion.8, bf16[1024,8448]{1,0:T(8,128)(2,1)} %all-gather.6.cloned.1.call-done), kind=kOutput, calls=%fused_computation.20 | convolution fusion | flops 3360817152 | bytes 26411008 | tf_op jit(solution)/shard_map/dot_general | solution.py:29
  704.7 10.8 %collective-permute-done.69 = bf16[256,2816]{1,0:T(8,128)(2,1)S(1)} collective-permute-done((bf16[256,2816]{1,0:T(8,128)(2,1)S(1)}, bf16[256,2816]{1,0:T(8,128)(2,1)S(1)}, u32[]{:S(2)}, u32[]{:S(2)}) %collective-permute-start.69) | collective-permute-done | bytes 1441824 | tf_op jit(solution)/shard_map/ppermute | solution.py:56
  774.9 15.9 %attention_backward.6 = (f32[256,1024]{1,0:T(8,128)}, f32[2,256,1024]{2,1,0:T(8,128)}, bf16[2,256,1024]{2,1,0:T(8,128)(2,1)}, f32[16,2,512]{2,1,0:T(2,128)}) custom-call(bf16[256,1024]{1,0:T(8,128)(2,1)} %convolution_convert_fusion.13.q_ref, bf16[256,1024]{1,0:T(8,128)(2,1)} %fusion.108.g_ref, f32[256,1024]{1,0:T(8,128)} %get-tuple-element.253.o_ref, ...), custom_call_target="tpu_custom_call" | custom-call | flops 1342177280 | bytes 9437184 | tf_op jit(solution)/shard_map/attention_backward/pallas_call | solution.py:203
  793.7 13.9 %collective-permute-done.71 = bf16[256,2816]{1,0:T(8,128)(2,1)} collective-permute-done((bf16[256,2816]{1,0:T(8,128)(2,1)}, bf16[256,2816]{1,0:T(8,128)(2,1)}, u32[]{:S(2)}, u32[]{:S(2)}) %collective-permute-start.71) | collective-permute-done | bytes 1441824 | tf_op jit(solution)/shard_map/ppermute | solution.py:56
  812.1 15.9 %attention_backward.7 = (bf16[256,1024]{1,0:T(8,128)(2,1)}, f32[2,256,1024]{2,1,0:T(8,128)}, bf16[2,256,1024]{2,1,0:T(8,128)(2,1)}, f32[16,2,512]{2,1,0:T(2,128)}) custom-call(bf16[256,1024]{1,0:T(8,128)(2,1)} %convolution_convert_fusion.13.q_ref, bf16[256,1024]{1,0:T(8,128)(2,1)} %fusion.108.g_ref, f32[256,1024]{1,0:T(8,128)} %get-tuple-element.253.o_ref, ...), custom_call_target="tpu_custom_call" | custom-call | flops 1342177280 | bytes 9437184 | tf_op jit(solution)/shard_map/attention_backward/pallas_call | solution.py:203
  875.8 24.3 %collective-permute-done.82 = bf16[256,2816]{1,0:T(8,128)(2,1)} collective-permute-done((bf16[256,2816]{1,0:T(8,128)(2,1)}, bf16[256,2816]{1,0:T(8,128)(2,1)}, u32[]{:S(2)}, u32[]{:S(2)}) %collective-permute-start.82) | collective-permute-done | bytes 1441824 | tf_op jit(solution)/shard_map/ppermute | solution.py:56
  913.4 33.4 %reduce-scatter.5.cloned.1.call-done = bf16[1,128,1024]{2,1,0:T(8,128)(2,1)} async-done(((bf16[8,128,1024]{2,1,0:T(8,128)(2,1)}), bf16[1,128,1024]{2,1,0:T(8,128)(2,1)}) %reduce-scatter.5.cloned.1.call-update) | async-done | bytes 262160 | tf_op jit(solution)/shard_map/reduce_scatter | solution.py:455
  (745 shorter events, 609.4 us)
Async XLA Ops:
  7.2 224.9 %all-gather.6.cloned.1.call-start = ((), (), s32[]{:S(2)}) async-start(), calls=%async_computation.2 | async-start | bytes 19464192 | tf_op jit(solution)/shard_map/all_gather | solution.py:653
  25.6 50.1 %collective-permute-start.7 = (bf16[128,8448]{1,0:T(8,128)(2,1)}, bf16[128,8448]{1,0:T(8,128)(2,1)}, u32[]{:S(2)}, u32[]{:S(2)}) collective-permute-start(bf16[128,8448]{1,0:T(8,128)(2,1)} %pad_maximum_fusion), channel_id=1, source_target_pairs={{0,16},{16,0},{1,17},{17,1},{2,18},{18,2},{3,19},{19,3},{4,20},{20... | collective-permute-start | bytes 6488072 | tf_op jit(solution)/shard_map/ppermute | solution.py:234
  79.4 227.0 %all-gather.8.cloned.1.call-start = ((), (), s32[]{:S(2)}) async-start(), calls=%async_computation.3 | async-start | bytes 8650752 | tf_op jit(solution)/shard_map/all_gather | solution.py:654
  117.6 48.0 %collective-permute-start.22 = (bf16[256,2048]{1,0:T(8,128)(2,1)S(1)}, bf16[256,2048]{1,0:T(8,128)(2,1)S(1)}, u32[]{:S(2)}, u32[]{:S(2)}) collective-permute-start(bf16[256,2048]{1,0:T(8,128)(2,1)S(1)} %convolution_convert_fusion.6.k0.v0), channel_id=1, source_target_pairs={{0,2},{2,0},{1,3},{3,1},{4,6},{6,4},{5,7},{7,5},{8,10},{10,8},{9,1... | collective-permute-start | bytes 3145736 | tf_op jit(solution)/shard_map/ppermute | solution.py:56
  169.1 245.4 %all-gather.10.cloned.1.call-start = ((), (), s32[]{:S(2)}) async-start(), calls=%async_computation.4 | async-start | bytes 19464192 | tf_op jit(solution)/shard_map/all_gather | solution.py:655
  169.9 702.2 %reduce-scatter.3.cloned.1.call-start = ((), (), s32[]{:S(2)}) async-start(), calls=%async_computation.5 | async-start | bytes 5013504 | tf_op jit(solution)/shard_map/reduce_scatter | solution.py:455
  255.7 36.2 %collective-permute-start.30 = (bf16[144,1024]{1,0:T(8,128)(2,1)S(1)}, bf16[144,1024]{1,0:T(8,128)(2,1)S(1)}, u32[]{:S(2)}, u32[]{:S(2)}) collective-permute-start(bf16[144,1024]{1,0:T(8,128)(2,1)S(1)} %get-tuple-element.401), channel_id=1, source_target_pairs={{0,8},{4,12},{8,0},{12,4},{1,9},{5,13},{9,1},{13,5},{2,10},{6,14},... | collective-permute-start | bytes 884744 | tf_op jit(solution)/shard_map/ppermute | solution.py:56
  310.0 42.7 %collective-permute-start.33 = (bf16[256,2048]{1,0:T(8,128)(2,1)S(1)}, bf16[256,2048]{1,0:T(8,128)(2,1)}, u32[]{:S(2)}, u32[]{:S(2)}) collective-permute-start(bf16[256,2048]{1,0:T(8,128)(2,1)S(1)} %fusion.53.k0.v0), channel_id=1, source_target_pairs={{0,2},{2,0},{1,3},{3,1},{4,6},{6,4},{5,7},{7,5},{8,10},{10,8},{9,1... | collective-permute-start | bytes 3145736 | tf_op jit(solution)/shard_map/ppermute | solution.py:56
  311.5 46.6 %collective-permute-start.32 = (bf16[256,2048]{1,0:T(8,128)(2,1)S(1)}, bf16[256,2048]{1,0:T(8,128)(2,1)S(1)}, u32[]{:S(2)}, u32[]{:S(2)}) collective-permute-start(bf16[256,2048]{1,0:T(8,128)(2,1)S(1)} %fusion.53.k0.v0), channel_id=1, source_target_pairs={{0,1},{1,0},{2,3},{3,2},{4,5},{5,4},{6,7},{7,6},{8,9},{9,8},{10,11... | collective-permute-start | bytes 3145736 | tf_op jit(solution)/shard_map/ppermute | solution.py:56
  470.5 48.2 %collective-permute-start.45 = (bf16[512,2816]{1,0:T(8,128)(2,1)}, bf16[512,2816]{1,0:T(8,128)(2,1)}, u32[]{:S(2)}, u32[]{:S(2)}) collective-permute-start(bf16[512,2816]{1,0:T(8,128)(2,1)} %convolution_convert_fusion.4), channel_id=1, source_target_pairs={{0,1},{1,0},{2,3},{3,2},{4,5},{5,4},{6,7},{7,6},{8,9},{9,8},{10,11... | collective-permute-start | bytes 8650760 | tf_op jit(solution)/shard_map/ppermute | solution.py:56
  471.0 47.7 %collective-permute-start.46 = (bf16[512,2816]{1,0:T(8,128)(2,1)}, bf16[512,2816]{1,0:T(8,128)(2,1)}, u32[]{:S(2)}, u32[]{:S(2)}) collective-permute-start(bf16[512,2816]{1,0:T(8,128)(2,1)} %convolution_convert_fusion.3), channel_id=1, source_target_pairs={{0,1},{1,0},{2,3},{3,2},{4,5},{5,4},{6,7},{7,6},{8,9},{9,8},{10,11... | collective-permute-start | bytes 8650760 | tf_op jit(solution)/shard_map/ppermute | solution.py:56
  503.0 43.3 %collective-permute-start.50 = (bf16[256,2816]{1,0:T(8,128)(2,1)S(1)}, bf16[256,2816]{1,0:T(8,128)(2,1)S(1)}, u32[]{:S(2)}, u32[]{:S(2)}) collective-permute-start(bf16[256,2816]{1,0:T(8,128)(2,1)S(1)} %copy-done.73), channel_id=1, source_target_pairs={{0,2},{2,0},{1,3},{3,1},{4,6},{6,4},{5,7},{7,5},{8,10},{10,8},{9,1... | collective-permute-start | bytes 4325384 | tf_op jit(solution)/shard_map/ppermute | solution.py:56
  621.9 56.6 %collective-permute-start.61 = (bf16[256,1024]{1,0:T(8,128)(2,1)}, bf16[256,1024]{1,0:T(8,128)(2,1)}, u32[]{:S(2)}, u32[]{:S(2)}) collective-permute-start(bf16[256,1024]{1,0:T(8,128)(2,1)} %get-tuple-element.408), channel_id=1, source_target_pairs={{0,16},{16,0},{1,17},{17,1},{2,18},{18,2},{3,19},{19,3},{4,20},{20... | collective-permute-start | bytes 1572872 | tf_op jit(solution)/shard_map/ppermute | solution.py:234
  623.2 55.3 %collective-permute-start.60 = (bf16[256,2816]{1,0:T(8,128)(2,1)}, bf16[256,2816]{1,0:T(8,128)(2,1)}, u32[]{:S(2)}, u32[]{:S(2)}) collective-permute-start(bf16[256,2816]{1,0:T(8,128)(2,1)} %add_convert_fusion.7), channel_id=1, source_target_pairs={{0,16},{1,17},{2,18},{3,19},{4,20},{5,21},{6,22},{7,23},{8,24},{9,... | collective-permute-start | bytes 4325384 | tf_op jit(solution)/shard_map/ppermute | solution.py:388
  755.5 191.3 %reduce-scatter.5.cloned.1.call-start = ((), (), s32[]{:S(2)}) async-start(), calls=%async_computation.6 | async-start | bytes 2359296 | tf_op jit(solution)/shard_map/reduce_scatter | solution.py:455
  762.9 44.7 %collective-permute-start.71 = (bf16[256,2816]{1,0:T(8,128)(2,1)}, bf16[256,2816]{1,0:T(8,128)(2,1)}, u32[]{:S(2)}, u32[]{:S(2)}) collective-permute-start(bf16[256,2816]{1,0:T(8,128)(2,1)} %fusion.49), channel_id=1, source_target_pairs={{0,2},{2,0},{1,3},{3,1},{4,6},{6,4},{5,7},{7,5},{8,10},{10,8},{9,1... | collective-permute-start | bytes 4325384 | tf_op jit(solution)/shard_map/ppermute | solution.py:56
  854.0 166.6 %all-gather.12.cloned.1.call-start = ((), (), s32[]{:S(2)}) async-start(), calls=%async_computation.7 | async-start | bytes 2785280 | tf_op jit(solution)/shard_map/all_gather | solution.py:728
  856.9 110.3 %collective-permute-start.92 = (bf16[256,2816]{1,0:T(8,128)(2,1)}, bf16[256,2816]{1,0:T(8,128)(2,1)}, u32[]{:S(2)}, u32[]{:S(2)}) collective-permute-start(bf16[256,2816]{1,0:T(8,128)(2,1)} %add_convert_fusion.4), channel_id=1, source_target_pairs={{16,0},{17,1},{18,2},{19,3},{20,4},{21,5},{22,6},{23,7},{24,8},{25... | collective-permute-start | bytes 4325384 | tf_op jit(solution)/shard_map/ppermute | solution.py:388
  858.2 142.0 %collective-permute-start.81 = (bf16[256,2816]{1,0:T(8,128)(2,1)}, bf16[256,2816]{1,0:T(8,128)(2,1)}, u32[]{:S(2)}, u32[]{:S(2)}) collective-permute-start(bf16[256,2816]{1,0:T(8,128)(2,1)} %fusion.52), channel_id=1, source_target_pairs={{16,0},{17,1},{18,2},{19,3},{20,4},{21,5},{22,6},{23,7},{24,8},{25... | collective-permute-start | bytes 4325384 | tf_op jit(solution)/shard_map/ppermute | solution.py:448
  859.7 40.4 %collective-permute-start.82 = (bf16[256,2816]{1,0:T(8,128)(2,1)}, bf16[256,2816]{1,0:T(8,128)(2,1)}, u32[]{:S(2)}, u32[]{:S(2)}) collective-permute-start(bf16[256,2816]{1,0:T(8,128)(2,1)} %fusion.50), channel_id=1, source_target_pairs={{0,2},{2,0},{1,3},{3,1},{4,6},{6,4},{5,7},{7,5},{8,10},{10,8},{9,1... | collective-permute-start | bytes 4325384 | tf_op jit(solution)/shard_map/ppermute | solution.py:56
  874.4 84.8 %collective-permute-start.77 = (bf16[4,144,1024]{2,1,0:T(8,128)(2,1)}, bf16[4,144,1024]{2,1,0:T(8,128)(2,1)}, u32[]{:S(2)}, u32[]{:S(2)}) collective-permute-start(bf16[4,144,1024]{2,1,0:T(8,128)(2,1)} %dynamic-slice_bitcast_fusion), channel_id=1, source_target_pairs={{0,2},{2,0},{1,3},{3,1},{4,6},{6,4},{5,7},{7,5},{8,10},{10,8},{9,1... | collective-permute-start | bytes 3538952 | tf_op jit(solution)/shard_map/ppermute | solution.py:56
  905.6 52.3 %collective-permute-start.87 = (bf16[272,1024]{1,0:T(8,128)(2,1)}, bf16[272,1024]{1,0:T(8,128)(2,1)}, u32[]{:S(2)}, u32[]{:S(2)}) collective-permute-start(bf16[272,1024]{1,0:T(8,128)(2,1)} %bitcast.64), channel_id=1, source_target_pairs={{0,16},{1,17},{2,18},{3,19},{4,20},{5,21},{6,22},{7,23},{8,24},{9,... | collective-permute-start | bytes 1671176 | tf_op jit(solution)/shard_map/ppermute | solution.py:718
  956.6 45.6 %collective-permute-start.83 = (bf16[256,2816]{1,0:T(8,128)(2,1)}, bf16[256,2816]{1,0:T(8,128)(2,1)}, u32[]{:S(2)}, u32[]{:S(2)}) collective-permute-start(bf16[256,2816]{1,0:T(8,128)(2,1)} %fusion.51), channel_id=1, source_target_pairs={{16,0},{17,1},{18,2},{19,3},{20,4},{21,5},{22,6},{23,7},{24,8},{25... | collective-permute-start | bytes 4325384 | tf_op jit(solution)/shard_map/ppermute | solution.py:448
  967.2 44.1 %collective-permute-start.91 = (bf16[256,2816]{1,0:T(8,128)(2,1)}, bf16[256,2816]{1,0:T(8,128)(2,1)}, u32[]{:S(2)}, u32[]{:S(2)}) collective-permute-start(bf16[256,2816]{1,0:T(8,128)(2,1)} %add_convert_fusion.5), channel_id=1, source_target_pairs={{0,16},{1,17},{2,18},{3,19},{4,20},{5,21},{6,22},{7,23},{8,24},{9,... | collective-permute-start | bytes 4325384 | tf_op jit(solution)/shard_map/ppermute | solution.py:704
  (225 other events, 3586.0 us)
Sparse Core Ops, SparseCore 0:
  79.5 112.5 all-gather.5
  195.0 111.4 all-gather.7
  308.9 105.5 all-gather.9
  755.6 110.1 reduce-scatter.2
  870.2 76.5 reduce-scatter.4
  967.3 25.0 all-gather.11
